TPU v7x, 32 devices: a whole 2x2x4 slice. The times are simulated.
32 devices in a mesh: seq: 8 (over z, y), mp: 4 (over x, core).
Axes of the slice: x: 2, y: 2, z: 4, core: 2. Of those that a mesh axis runs over, the one named last changes fastest.
Arguments:
- inputs: bfloat16 [16384, 768], P(('seq', 'mp')), may hold values from -6 to 6
- doc_bounds: int32 [2, 16384], P(None, 'seq'), may hold values from 0 to 16384, as said below
- qkv_weight: bfloat16 [2, 3, 768, 768], P(None, None, None, 'mp'), may hold values from -0.21875 to 0.21875
- qv_bias: float32 [2, 2, 768], P(None, None, 'mp'), may hold values from -1.8 to 1.8
- conv_weight: float32 [2, 2, 5, 768], P(None, None, None, 'mp'), may hold values from -2.7 to 2.7
- conv_bias: float32 [2, 2, 768], P(None, None, 'mp'), may hold values from -1.8 to 1.8
- out_weight: bfloat16 [2, 768, 768], P(None, 'mp'), may hold values from -1.75 to 1.75
- up_weight: bfloat16 [2, 768, 3072], P(None, None, 'mp'), may hold values from -0.21875 to 0.21875
- up_bias: float32 [2, 3072], P(None, 'mp'), may hold values from -1.8 to 1.8
- down_weight: bfloat16 [2, 3072, 768], P(None, 'mp'), may hold values from -0.109375 to 0.109375
- norm_gains: float32 [2, 2, 768], replicated, may hold values from 0.5 to 1.5
- shared_biases: float32 [2, 4, 768], replicated, may hold values from -1.8 to 1.8
- cotangent: bfloat16 [16384, 768], P(('seq', 'mp')), may hold values from -6 to 6
Outputs:
- outputs: float32 [16384, 768], P(('seq', 'mp'))
- grad_input: float32 [16384, 768], P(('seq', 'mp'))
- grad_qkv: float32 [2, 3, 768, 768], P(None, None, None, 'mp')
- grad_qv_bias: float32 [2, 2, 768], P(None, None, 'mp')
- grad_conv_weight: float32 [2, 2, 5, 768], P(None, None, None, 'mp')
- grad_conv_bias: float32 [2, 2, 768], P(None, None, 'mp')
- grad_out_weight: float32 [2, 768, 768], P(None, 'mp')
- grad_up_weight: float32 [2, 768, 3072], P(None, None, 'mp')
- grad_up_bias: float32 [2, 3072], P(None, 'mp')
- grad_down_weight: float32 [2, 3072, 768], P(None, 'mp')
- grad_gains: float32 [2, 2, 768], replicated
- grad_biases: float32 [2, 4, 768], replicated
Inputs may be any that keep to these rules, and one draw needn't show every extreme that they name: Documents are contiguous runs that cover all 16384 tokens in order; for every token i, doc_bounds[0, i] is the first token of its document and doc_bounds[1, i] one past its last. One document holds 8192 tokens and starts at token 4096; the document right after it holds exactly 2048; every other holds at most 2048.
All inputs are finite; a program needn't handle non-finite values.
Results may differ from a plain program's by a relative error of at most 0.023.
Values may be sent and summed in bfloat16 or wider, within the bound.
A program may use at most 192 MiB of HBM per device.

v0:
```python
import jax
import jax.numpy as jnp
from jax import lax
from jax.sharding import PartitionSpec as P

HEAD_DIM = 64
LAYERS = 2
SCORE_ROWS = 512
WINDOW = 64
POOL_REACH = 64


NORM_EPSILON = 1e-05


def with_halo(cells, sides, width):
    for axis, dim in sides:
        count = lax.axis_size(axis)
        ends = count - 1
        head = lax.slice_in_dim(cells, 0, width, axis=dim)
        tail = lax.slice_in_dim(cells, cells.shape[dim] - width, cells.shape[dim], axis=dim)
        cells = jnp.concatenate(
            [
                lax.ppermute(tail, axis, [(i, (i + 1) % count) for i in range(ends)]),
                cells,
                lax.ppermute(head, axis, [((i + 1) % count, i) for i in range(ends)]),
            ],
            axis=dim,
        )
    return cells


def layer_norm(values, scale_gain, offset):
    average = jnp.mean(values, axis=-1, keepdims=True)
    centered = values - average
    spread = jnp.mean(centered * centered, axis=-1, keepdims=True)
    return centered * lax.rsqrt(spread + NORM_EPSILON) * scale_gain + offset


def exact_gelu(values):
    return jax.nn.gelu(values, approximate=False)


def product(left, right):
    return jnp.dot(left, right, preferred_element_type=jnp.float32)


def product_left_t(left, right):
    return lax.dot_general(
        left, right, (((0,), (0,)), ((), ())), preferred_element_type=jnp.float32
    )


def product_right_t(left, right):
    return lax.dot_general(
        left, right, (((1,), (1,)), ((), ())), preferred_element_type=jnp.float32
    )


def head_view(rows):
    return rows.reshape(rows.shape[0], -1, HEAD_DIM)


def allowed_keys(first_row, starts, finish):
    row_ids = first_row + jnp.arange(SCORE_ROWS, dtype=jnp.int32)
    window_ids = first_row - WINDOW + jnp.arange(SCORE_ROWS + 2 * WINDOW, dtype=jnp.int32)
    pooled_ids = 4 * (
        first_row // 4 - POOL_REACH + jnp.arange(SCORE_ROWS // 4 + 2 * POOL_REACH, dtype=jnp.int32)
    )
    near_rows = jnp.abs(row_ids[:, None] - window_ids[None]) <= WINDOW
    same_doc = (window_ids[None] >= starts[:, None]) & (window_ids[None] < finish[:, None])
    near_pooled = jnp.abs(row_ids[:, None] - pooled_ids[None]) <= 4 * POOL_REACH
    same_pooled = (pooled_ids[None] >= starts[:, None]) & (pooled_ids[None] < finish[:, None])
    return jnp.concatenate([near_rows & same_doc, near_pooled & same_pooled], axis=1)


def tap_keep(bounds, base_row, total):
    places = (
        base_row
        + 4 * jnp.arange(total // 4, dtype=jnp.int32)[:, None]
        + jnp.arange(5, dtype=jnp.int32)[None]
        - 2
    )
    first_token = bounds[0].reshape(-1, 4)[:, 0]
    past_end = bounds[1].reshape(-1, 4)[:, 0]
    return (places >= first_token[:, None]) & (places < past_end[:, None])


def tap_rows(kv_wide, total):
    leading = kv_wide[WINDOW - 2 : WINDOW - 2 + total].reshape(total // 4, 4, -1)
    trailing = kv_wide[WINDOW + 2 : WINDOW + 2 + total].reshape(total // 4, 4, -1)[:, :1]
    return jnp.concatenate([leading, trailing], axis=1)


def block_inputs(queries, kv_wide, pooled_wide, bounds, base_row, row_zero):
    width = queries.shape[1]
    query_rows = head_view(lax.dynamic_slice_in_dim(queries, row_zero, SCORE_ROWS, 0))
    window = lax.dynamic_slice_in_dim(kv_wide, row_zero, SCORE_ROWS + 2 * WINDOW, 0)
    pooled = lax.dynamic_slice_in_dim(
        pooled_wide, row_zero // 4, SCORE_ROWS // 4 + 2 * POOL_REACH, 0
    )
    key_rows = jnp.concatenate([window, pooled], axis=0)
    allowed = allowed_keys(
        base_row + row_zero,
        lax.dynamic_slice_in_dim(bounds[0], row_zero, SCORE_ROWS, 0),
        lax.dynamic_slice_in_dim(bounds[1], row_zero, SCORE_ROWS, 0),
    )
    return (query_rows, head_view(key_rows[:, :width]), head_view(key_rows[:, width:]), allowed)


def attend_forward(queries, kv_wide, pooled_wide, bounds, base_row):
    total, width = queries.shape
    score_scale = HEAD_DIM ** (-0.5)

    def one_block(carry, block_index):
        row_zero = block_index * SCORE_ROWS
        query_rows, key_heads, value_heads, allowed = block_inputs(
            queries, kv_wide, pooled_wide, bounds, base_row, row_zero
        )
        scores = (
            jnp.einsum("qhe,khe->hqk", query_rows, key_heads, preferred_element_type=jnp.float32)
            * score_scale
        )
        masked = jnp.where(allowed[None], scores, -1e30)
        log_total = jax.nn.logsumexp(masked, axis=-1, keepdims=True)
        weights = jnp.exp(masked - log_total).astype(jnp.bfloat16)
        mixed = jnp.einsum("hqk,khe->qhe", weights, value_heads, preferred_element_type=jnp.float32)
        return (carry, (mixed.astype(jnp.bfloat16).reshape(SCORE_ROWS, width), log_total[:, :, 0]))

    unused, (mixed, log_totals) = lax.scan(
        one_block, 0, jnp.arange(total // SCORE_ROWS, dtype=jnp.int32)
    )
    return (mixed.reshape(total, width), log_totals)


def attend_backward(queries, kv_wide, pooled_wide, bounds, base_row, log_totals, grad_mixed):
    total, width = queries.shape
    score_scale = HEAD_DIM ** (-0.5)
    span = SCORE_ROWS + 2 * WINDOW

    def one_block(block_index, state):
        grad_query, grad_kv, grad_pooled = state
        row_zero = block_index * SCORE_ROWS
        query_rows, key_heads, value_heads, allowed = block_inputs(
            queries, kv_wide, pooled_wide, bounds, base_row, row_zero
        )
        scores = (
            jnp.einsum("qhe,khe->hqk", query_rows, key_heads, preferred_element_type=jnp.float32)
            * score_scale
        )
        masked = jnp.where(allowed[None], scores, -1e30)
        log_total = lax.dynamic_index_in_dim(log_totals, block_index, 0, keepdims=False)
        probs = jnp.exp(masked - log_total[:, :, None])
        grad_rows = head_view(lax.dynamic_slice_in_dim(grad_mixed, row_zero, SCORE_ROWS, 0))
        grad_probs = jnp.einsum(
            "qhe,khe->hqk", grad_rows, value_heads, preferred_element_type=jnp.float32
        )
        grad_values = jnp.einsum(
            "hqk,qhe->khe",
            probs.astype(jnp.bfloat16),
            grad_rows,
            preferred_element_type=jnp.float32,
        )
        delta = jnp.sum(probs * grad_probs, axis=-1, keepdims=True)
        grad_scores = (probs * (grad_probs - delta)).astype(jnp.bfloat16)
        grad_q = (
            jnp.einsum("hqk,khe->qhe", grad_scores, key_heads, preferred_element_type=jnp.float32)
            * score_scale
        )
        grad_k = (
            jnp.einsum("hqk,qhe->khe", grad_scores, query_rows, preferred_element_type=jnp.float32)
            * score_scale
        )
        key_count = grad_k.shape[0]
        grad_keys = jnp.concatenate(
            [grad_k.reshape(key_count, width), grad_values.reshape(key_count, width)], axis=1
        )
        grad_query = lax.dynamic_update_slice_in_dim(
            grad_query, grad_q.reshape(SCORE_ROWS, width), row_zero, 0
        )
        window_old = lax.dynamic_slice_in_dim(grad_kv, row_zero, span, 0)
        grad_kv = lax.dynamic_update_slice_in_dim(
            grad_kv, window_old + grad_keys[:span], row_zero, 0
        )
        pooled_old = lax.dynamic_slice_in_dim(grad_pooled, row_zero // 4, key_count - span, 0)
        grad_pooled = lax.dynamic_update_slice_in_dim(
            grad_pooled, pooled_old + grad_keys[span:], row_zero // 4, 0
        )
        return (grad_query, grad_kv, grad_pooled)

    initial = (
        jnp.zeros((total, width), jnp.float32),
        jnp.zeros((total + 2 * WINDOW, 2 * width), jnp.float32),
        jnp.zeros((total // 4 + 2 * POOL_REACH, 2 * width), jnp.float32),
    )
    return lax.fori_loop(0, total // SCORE_ROWS, one_block, initial)


def layer_forward(hidden, bounds, weights, base_row):
    (
        qkv_layer,
        qv_layer,
        conv_layer,
        conv_bias_layer,
        out_layer,
        up_layer,
        up_bias_layer,
        down_layer,
        gains,
        biases,
    ) = weights
    wide_in = lax.all_gather(hidden.astype(jnp.bfloat16), "mp", axis=0, tiled=True)
    total = wide_in.shape[0]
    projected = jnp.einsum("td,sdw->tsw", wide_in, qkv_layer, preferred_element_type=jnp.float32)
    queries = (projected[:, 0] + qv_layer[0]).astype(jnp.bfloat16)
    key_rows = projected[:, 1].astype(jnp.bfloat16)
    value_rows = (projected[:, 2] + qv_layer[1]).astype(jnp.bfloat16)
    kv_rows = jnp.concatenate([key_rows, value_rows], axis=1)
    kv_wide = with_halo(kv_rows, (("seq", 0),), WINDOW)
    tap_values = jnp.where(
        tap_keep(bounds, base_row, total)[:, :, None],
        tap_rows(kv_wide, total).astype(jnp.float32),
        0.0,
    )
    tap_weights = jnp.concatenate([conv_layer[0], conv_layer[1]], axis=1)
    pooled = (
        jnp.sum(tap_values * tap_weights[None], axis=1)
        + jnp.concatenate([conv_bias_layer[0], conv_bias_layer[1]])
    ).astype(jnp.bfloat16)
    pooled_wide = with_halo(pooled, (("seq", 0),), POOL_REACH)
    mixed, log_totals = attend_forward(queries, kv_wide, pooled_wide, bounds, base_row)
    branch = lax.psum_scatter(product(mixed, out_layer), "mp", scatter_dimension=0, tiled=True)
    resid = hidden + (branch + biases[0])
    normed = layer_norm(resid, gains[0], biases[1])
    wide_normed = lax.all_gather(normed.astype(jnp.bfloat16), "mp", axis=0, tiled=True)
    pre = product(wide_normed, up_layer) + up_bias_layer
    act = exact_gelu(pre).astype(jnp.bfloat16)
    middle = normed + (
        lax.psum_scatter(product(act, down_layer), "mp", scatter_dimension=0, tiled=True)
        + biases[2]
    )
    result = layer_norm(middle, gains[1], biases[3])
    saved = (
        wide_in,
        queries,
        kv_wide,
        pooled_wide,
        tap_values,
        mixed,
        log_totals,
        resid,
        normed,
        wide_normed,
        pre,
        act,
        middle,
    )
    return (result, saved)


def layer_backward(grad_out, bounds, weights, saved, base_row):
    (
        qkv_layer,
        qv_layer,
        conv_layer,
        conv_bias_layer,
        out_layer,
        up_layer,
        up_bias_layer,
        down_layer,
        gains,
        biases,
    ) = weights
    (
        wide_in,
        queries,
        kv_wide,
        pooled_wide,
        tap_values,
        mixed,
        log_totals,
        resid,
        normed,
        wide_normed,
        pre,
        act,
        middle,
    ) = saved
    total, width = queries.shape
    pooled_count = total // 4
    second_back = jax.vjp(layer_norm, middle, gains[1], biases[3])[1]
    grad_middle, gain_two, shift_two = second_back(grad_out)
    bias_down = jnp.sum(grad_middle, axis=0)
    wide_grad = lax.all_gather(grad_middle.astype(jnp.bfloat16), "mp", axis=0, tiled=True)
    grad_w_down = product_left_t(act, wide_grad)
    grad_act = product_right_t(wide_grad, down_layer)
    gelu_back = jax.vjp(exact_gelu, pre)[1]
    grad_pre = gelu_back(grad_act)[0]
    grad_b_up = jnp.sum(grad_pre, axis=0)
    grad_pre_low = grad_pre.astype(jnp.bfloat16)
    grad_w_up = product_left_t(wide_normed, grad_pre_low)
    grad_normed = (
        lax.psum_scatter(
            product_right_t(grad_pre_low, up_layer), "mp", scatter_dimension=0, tiled=True
        )
        + grad_middle
    )
    first_back = jax.vjp(layer_norm, resid, gains[0], biases[1])[1]
    grad_resid, gain_one, shift_one = first_back(grad_normed)
    bias_out = jnp.sum(grad_resid, axis=0)
    wide_resid = lax.all_gather(grad_resid.astype(jnp.bfloat16), "mp", axis=0, tiled=True)
    grad_w_out = product_left_t(mixed, wide_resid)
    grad_mixed = product_right_t(wide_resid, out_layer).astype(jnp.bfloat16)
    grad_query, grad_kv, grad_pooled = attend_backward(
        queries, kv_wide, pooled_wide, bounds, base_row, log_totals, grad_mixed
    )
    pooled_sent = jnp.concatenate([grad_pooled[:POOL_REACH], grad_pooled[-POOL_REACH:]], axis=0)
    pooled_back = with_halo(pooled_sent, (("seq", 0),), POOL_REACH)
    pooled_own = grad_pooled[POOL_REACH : POOL_REACH + pooled_count]
    pooled_own = pooled_own.at[:POOL_REACH].add(pooled_back[:POOL_REACH])
    pooled_own = pooled_own.at[-POOL_REACH:].add(pooled_back[-POOL_REACH:])
    grad_conv_b = jnp.sum(pooled_own, axis=0).reshape(2, width)
    grad_conv_w = (
        jnp.sum(pooled_own[:, None, :] * tap_values, axis=0).reshape(5, 2, width).transpose(1, 0, 2)
    )
    tap_weights = jnp.concatenate([conv_layer[0], conv_layer[1]], axis=1)
    grad_taps = jnp.where(
        tap_keep(bounds, base_row, total)[:, :, None],
        pooled_own[:, None, :] * tap_weights[None],
        0.0,
    )
    grad_kv = grad_kv.at[WINDOW - 2 : WINDOW - 2 + total].add(
        grad_taps[:, :4].reshape(total, 2 * width)
    )
    trailing = jnp.concatenate(
        [grad_taps[:, 4:], jnp.zeros((pooled_count, 3, 2 * width), jnp.float32)], axis=1
    )
    grad_kv = grad_kv.at[WINDOW + 2 : WINDOW + 2 + total].add(trailing.reshape(total, 2 * width))
    kv_sent = jnp.concatenate([grad_kv[:WINDOW], grad_kv[-WINDOW:]], axis=0)
    kv_back = with_halo(kv_sent, (("seq", 0),), WINDOW)
    kv_own = grad_kv[WINDOW : WINDOW + total]
    kv_own = kv_own.at[:WINDOW].add(kv_back[:WINDOW])
    kv_own = kv_own.at[-WINDOW:].add(kv_back[-WINDOW:])
    grad_values = kv_own[:, width:]
    grad_b_qv = jnp.stack([jnp.sum(grad_query, axis=0), jnp.sum(grad_values, axis=0)])
    grad_proj = jnp.stack([grad_query, kv_own[:, :width], grad_values], axis=1).astype(jnp.bfloat16)
    grad_w_qkv = jnp.einsum("td,tsw->sdw", wide_in, grad_proj, preferred_element_type=jnp.float32)
    grad_hidden = (
        lax.psum_scatter(
            jnp.einsum("tsw,sdw->td", grad_proj, qkv_layer, preferred_element_type=jnp.float32),
            "mp",
            scatter_dimension=0,
            tiled=True,
        )
        + grad_resid
    )
    parts = (
        grad_w_qkv,
        grad_b_qv,
        grad_conv_w,
        grad_conv_b,
        grad_w_out,
        grad_w_up,
        grad_b_up,
        grad_w_down,
        jnp.stack([gain_one, gain_two]),
        jnp.stack([bias_out, shift_one, bias_down, shift_two]),
    )
    return (grad_hidden, parts)


def seq_totals(parts):
    return lax.psum(
        (
            parts[0],
            parts[1],
            parts[2],
            parts[3],
            parts[4],
            parts[5],
            parts[6],
            parts[7],
            parts[8],
            parts[9],
        ),
        "seq",
    )


def shards(
    inputs,
    doc_bounds,
    qkv_weight,
    qv_bias,
    conv_weight,
    conv_bias,
    out_weight,
    up_weight,
    up_bias,
    down_weight,
    norm_gains,
    shared_biases,
    cotangent,
):
    base_row = lax.axis_index("seq") * doc_bounds.shape[1]
    hidden = inputs.astype(jnp.float32)
    saved_layers = []
    for layer_index in range(LAYERS):
        weights = (
            qkv_weight[layer_index],
            qv_bias[layer_index],
            conv_weight[layer_index],
            conv_bias[layer_index],
            out_weight[layer_index],
            up_weight[layer_index],
            up_bias[layer_index],
            down_weight[layer_index],
            norm_gains[layer_index],
            shared_biases[layer_index],
        )
        hidden, saved = layer_forward(hidden, doc_bounds, weights, base_row)
        saved_layers.append((weights, saved))
    gradient = cotangent.astype(jnp.float32)
    collected = [None] * LAYERS
    for layer_index in reversed(range(LAYERS)):
        weights, saved = saved_layers[layer_index]
        gradient, parts = layer_backward(gradient, doc_bounds, weights, saved, base_row)
        collected[layer_index] = parts
    stacked = tuple(
        (
            jnp.stack([collected[layer_index][member] for layer_index in range(LAYERS)])
            for member in range(10)
        )
    )
    stacked = seq_totals(stacked)
    gains_total, biases_total = lax.psum((stacked[8], stacked[9]), "mp")
    return (
        hidden,
        gradient,
        stacked[0],
        stacked[1],
        stacked[2],
        stacked[3],
        stacked[4],
        stacked[5],
        stacked[6],
        stacked[7],
        gains_total,
        biases_total,
    )


def solution(mesh):
    return jax.shard_map(
        shards,
        mesh=mesh,
        in_specs=(
            P(("seq", "mp"), None),
            P(None, "seq"),
            P(None, None, None, "mp"),
            P(None, None, "mp"),
            P(None, None, None, "mp"),
            P(None, None, "mp"),
            P(None, "mp", None),
            P(None, None, "mp"),
            P(None, "mp"),
            P(None, "mp", None),
            P(),
            P(),
            P(("seq", "mp"), None),
        ),
        out_specs=(
            P(("seq", "mp"), None),
            P(("seq", "mp"), None),
            P(None, None, None, "mp"),
            P(None, None, "mp"),
            P(None, None, None, "mp"),
            P(None, None, "mp"),
            P(None, "mp", None),
            P(None, None, "mp"),
            P(None, "mp"),
            P(None, "mp", None),
            P(),
            P(),
        ),
        check_vma=False,
    )
```

profile of v0, /device:TPU:15, one launch (start us, length us, event | category | flops | bytes accessed | tf_op | source)
XLA Modules:
  0.0 1942.5 jit_solution(15384740190170718457)
XLA Ops:
  13.1 25.7 %all-gather.9.cloned.1.call-done = bf16[2048,768]{1,0:T(8,128)(2,1)} async-done(((bf16[512,768]{1,0:T(8,128)(2,1)}), bf16[2048,768]{1,0:T(8,128)(2,1)}) %all-gather.9.cloned.1.call-update) | async-done | bytes 3145744 | tf_op jit(solution)/shard_map/all_gather | solution.py:212
  82.8 41.1 %while.82 = (s32[]{:T(128)}, bf16[4,512,192]{1,2,0:T(8,128)(2,1)S(1)}, f32[4,3,512]{2,1,0:T(4,128)S(1)}, s32[4]{0:T(128)S(1)}, bf16[2176,384]{0,1:T(8,128)(2,1)}...) while((s32[]{:T(128)}, ...), condition=%wide.region_4.5_spmd, body=%wide.region_1.4_spmd.sunk | while | flops 372618944 | bytes 24030860 | solution.py:130
  130.7 57.0 %reduce-scatter.9.cloned.1.call-done = f32[512,768]{1,0:T(8,128)} async-done(((f32[2048,768]{1,0:T(8,128)}), f32[512,768]{1,0:T(8,128)}) %reduce-scatter.9.cloned.1.call-update) | async-done | bytes 1572880 | tf_op jit(solution)/shard_map/reduce_scatter | solution.py:232
  191.8 28.2 %all-gather.11.cloned.1.call-done = bf16[2048,768]{1,0:T(8,128)(2,1)} async-done(((bf16[512,768]{1,0:T(8,128)(2,1)}), bf16[2048,768]{1,0:T(8,128)(2,1)}) %all-gather.11.cloned.1.call-update) | async-done | bytes 3145744 | tf_op jit(solution)/shard_map/all_gather | solution.py:235
  220.0 18.8 multiply_convert_fusion.3
  240.6 4.5 fusion.104
  245.1 58.1 %reduce-scatter.11.cloned.1.call-done = f32[512,768]{1,0:T(8,128)} async-done(((f32[2048,768]{1,0:T(8,128)}), f32[512,768]{1,0:T(8,128)}) %reduce-scatter.11.cloned.1.call-update) | async-done | bytes 1572880 | tf_op jit(solution)/shard_map/reduce_scatter | solution.py:239
  306.9 29.0 %all-gather.13.cloned.1.call-done = bf16[2048,768]{1,0:T(8,128)(2,1)} async-done(((bf16[512,768]{1,0:T(8,128)(2,1)}), bf16[2048,768]{1,0:T(8,128)(2,1)}) %all-gather.13.cloned.1.call-update) | async-done | bytes 3145744 | tf_op jit(solution)/shard_map/all_gather | solution.py:212
  350.8 4.6 pad_maximum_fusion.17
  367.0 9.5 multiply_reduce_fusion.4
  390.2 43.7 %while.83 = (s32[]{:T(128)}, bf16[4,512,192]{1,2,0:T(8,128)(2,1)}, f32[4,3,512]{2,1,0:T(4,128)S(1)}, s32[4]{0:T(128)S(1)}, bf16[2176,384]{0,1:T(8,128)(2,1)}, /*...) while((s32[]{:T(128)}, bf16[4,512,192]{1,2,0:T(8,128)(2,1)}, ...), condition=%wide.region_15.16_spmd, body=%wide.region_12.15_spmd.sunk | while | flops 372618944 | bytes 24031368 | solution.py:130
  435.9 4.6 fusion.128
  440.6 58.9 %reduce-scatter.13.cloned.1.call-done = f32[512,768]{1,0:T(8,128)} async-done(((f32[2048,768]{1,0:T(8,128)}), f32[512,768]{1,0:T(8,128)}) %reduce-scatter.13.cloned.1.call-update) | async-done | bytes 1572880 | tf_op jit(solution)/shard_map/reduce_scatter | solution.py:232
  503.3 28.9 %all-gather.15.cloned.1.call-done = bf16[2048,768]{1,0:T(8,128)(2,1)} async-done(((bf16[512,768]{1,0:T(8,128)(2,1)}), bf16[2048,768]{1,0:T(8,128)(2,1)}) %all-gather.15.cloned.1.call-update) | async-done | bytes 3145744 | tf_op jit(solution)/shard_map/all_gather | solution.py:235
  532.1 18.8 multiply_convert_fusion.2
  552.7 4.4 fusion.95
  557.2 58.1 %reduce-scatter.15.cloned.1.call-done = f32[512,768]{1,0:T(8,128)} async-done(((f32[2048,768]{1,0:T(8,128)}), f32[512,768]{1,0:T(8,128)}) %reduce-scatter.15.cloned.1.call-update) | async-done | bytes 1572880 | tf_op jit(solution)/shard_map/reduce_scatter | solution.py:239
  622.7 28.8 %all-gather.17.cloned.1.call-done = bf16[2048,768]{1,0:T(8,128)(2,1)} async-done(((bf16[512,768]{1,0:T(8,128)(2,1)}), bf16[2048,768]{1,0:T(8,128)(2,1)}) %all-gather.17.cloned.1.call-update) | async-done | bytes 3145744 | tf_op jit(solution)/shard_map/all_gather | solution.py:294
  651.5 11.2 fusion.180
  664.4 4.5 fusion.82
  669.0 58.0 %reduce-scatter.17.cloned.1.call-done = f32[512,768]{1,0:T(8,128)} async-done(((f32[2048,768]{1,0:T(8,128)}), f32[512,768]{1,0:T(8,128)}) %reduce-scatter.17.cloned.1.call-update) | async-done | bytes 1572880 | tf_op jit(solution)/shard_map/reduce_scatter | solution.py:303
  733.9 28.6 %all-gather.19.cloned.1.call-done = bf16[2048,768]{1,0:T(8,128)(2,1)} async-done(((bf16[512,768]{1,0:T(8,128)(2,1)}), bf16[2048,768]{1,0:T(8,128)(2,1)}) %all-gather.19.cloned.1.call-update) | async-done | bytes 3145744 | tf_op jit(solution)/shard_map/all_gather | solution.py:311
  770.8 105.8 %while.84 = (s32[]{:T(128)}, f32[2048,192]{0,1:T(8,128)}, f32[2176,384]{0,1:T(8,128)}, f32[640,384]{0,1:T(8,128)}, bf16[2176,384]{0,1:T(8,128)(2,1)}, /*index=5*...) while((s32[]{:T(128)}, f32[2048,192]{0,1:T(8,128)}, ...), condition=%wide.region_29.30_spmd, body=%wide.region_27.29_spmd.sunk | while | flops 907452544 | bytes 83517328 | solution.py:196
  910.5 4.4 slice_add_fusion.3
  915.0 15.1 scatter-add.44
  930.1 4.4 slice_add_fusion.1
  934.6 15.1 scatter-add.45
  974.4 6.7 convolution_bitcast_fusion.1
  981.2 58.9 %reduce-scatter.19.cloned.1.call-done = f32[512,768]{1,0:T(8,128)} async-done(((f32[2048,768]{1,0:T(8,128)}), f32[512,768]{1,0:T(8,128)}) %reduce-scatter.19.cloned.1.call-update) | async-done | bytes 1572880 | tf_op jit(solution)/shard_map/reduce_scatter | solution.py:349
  1045.4 29.1 %all-gather.21.cloned.1.call-done = bf16[2048,768]{1,0:T(8,128)(2,1)} async-done(((bf16[512,768]{1,0:T(8,128)(2,1)}), bf16[2048,768]{1,0:T(8,128)(2,1)}) %all-gather.21.cloned.1.call-update) | async-done | bytes 3145744 | tf_op jit(solution)/shard_map/all_gather | solution.py:294
  1074.5 11.2 fusion.181
  1087.4 4.5 fusion.79
  1092.3 57.7 %reduce-scatter.21.cloned.1.call-done = f32[512,768]{1,0:T(8,128)} async-done(((f32[2048,768]{1,0:T(8,128)}), f32[512,768]{1,0:T(8,128)}) %reduce-scatter.21.cloned.1.call-update) | async-done | bytes 1572880 | tf_op jit(solution)/shard_map/reduce_scatter | solution.py:303
  1156.4 29.0 %all-gather.23.cloned.1.call-done = bf16[2048,768]{1,0:T(8,128)(2,1)} async-done(((bf16[512,768]{1,0:T(8,128)(2,1)}), bf16[2048,768]{1,0:T(8,128)(2,1)}) %all-gather.23.cloned.1.call-update) | async-done | bytes 3145744 | tf_op jit(solution)/shard_map/all_gather | solution.py:311
  1193.7 109.5 %while.85 = (s32[]{:T(128)}, f32[2048,192]{0,1:T(8,128)}, f32[2176,384]{0,1:T(8,128)}, f32[640,384]{0,1:T(8,128)}, bf16[2176,384]{0,1:T(8,128)(2,1)}, /*index=5*...) while((s32[]{:T(128)}, f32[2048,192]{0,1:T(8,128)}, ...), condition=%wide.region_38.39_spmd, body=%wide.region_36.38_spmd.sunk | while | flops 907452544 | bytes 83517328 | solution.py:196
  1229.9 4.3 multiply_reduce_fusion.19
  1324.8 8.1 multiply_reduce_fusion.3
  1341.1 4.4 slice_add_fusion.2
  1345.5 15.1 scatter-add.54
  1364.0 4.9 reshape.999
  1372.4 4.4 slice_add_fusion
  1376.9 15.1 scatter-add.55
  1413.1 6.7 convolution_bitcast_fusion
  1420.1 5.7 convolution_bitcast_fusion.2
  1460.9 23.8 %all-reduce.2 = (f32[2,2,192]{2,1,0:T(2,128)}, f32[2,2,5,192]{3,1,2,0:T(2,128)}, f32[2,2,192]{2,1,0:T(2,128)}, f32[2,768]{1,0:T(2,128)}, f32[2,2,768]{2,1,0:T(2,128)S(1)}, /*index=5*/f32[2,4,768]{2,1,0:T(4,128)S(1)}) all-reduce(f32[2,2,192]{2,1,0:T(2,128)S(1)} %pad_maximum_fusion.36, ...), channel_id=1, replica_groups=mesh['seq'=8,'mp'=4] {'seq'}, use_global_device_ids=true, to_apply=%region_45.46 | all-reduce | flops 16128 | bytes 129024 | tf_op jit(solution)/shard_map/psum | solution.py:373
  1484.6 20.9 %all-reduce.4 = (f32[2,2,768]{2,1,0:T(2,128)}, f32[2,4,768]{2,1,0:T(4,128)}) all-reduce(f32[2,2,768]{2,1,0:T(2,128)S(1)} %get-tuple-element.1260, f32[2,4,768]{2,1,0:T(4,128)S(1)} %get-tuple-element.1261), channel_id=1, replica_groups=mesh['seq'=8,'mp'=4] {'mp'}, use_global_device_ids=true, to_apply=%region_63.64 | all-reduce | flops 9216 | bytes 73728 | tf_op jit(solution)/shard_map/psum | solution.py:436
  1508.3 416.1 %all-reduce.7.cloned.1.call-done = (f32[2,3,768,192]{2,3,1,0:T(8,128)}, f32[2,192,768]{2,1,0:T(8,128)}, f32[2,768,768]{2,1,0:T(8,128)}, f32[2,768,768]{2,1,0:T(8,128)}) async-done(((f32[2,3,768,192]{2,3,1,0:T(8,128)}, f32[2,192,768]{2,1,0:T(8,128)}, f32[2,768,768]{2,1,0:T(8,128)}, f32[2,768,768]{2,1,0:T(8,128)}), (f32[2,3,768,192]{2,3,1,0:T(8,128)}, f32[2,192,768]{2,1,0:T(8,128)}, f32[2,768,768]{2,1,0:T(8,128)}, ...) | async-done | bytes 14155792 | tf_op jit(solution)/shard_map/psum | solution.py:373
  1924.4 4.4 copy.168
  (991 shorter events, 607.6 us)
Async XLA Ops:
  7.2 31.5 %all-gather.9.cloned.1.call-start = ((), (), s32[]{:S(2)}) async-start(), calls=%async_computation.8 | async-start | bytes 3932160 | tf_op jit(solution)/shard_map/all_gather | solution.py:212
  7.9 179.7 %reduce-scatter.9.cloned.1.call-start = ((), (), s32[]{:S(2)}) async-start(), calls=%async_computation.9 | async-start | bytes 7864320 | tf_op jit(solution)/shard_map/reduce_scatter | solution.py:232
  43.9 6.0 collective-permute-start
  47.0 6.6 collective-permute-start.1
  49.5 317.4 %copy-start.44 = (pred[512,5]{1,0:T(8,128)(4,1)}, pred[512,5]{1,0:T(8,128)(4,1)S(1)}, u32[]{:S(2)}) copy-start(pred[512,5]{1,0:T(8,128)(4,1)S(1)} %copy.65) | copy-start | bytes 7684
  71.8 9.8 collective-permute-start.2
  74.1 7.6 collective-permute-start.3
  128.7 91.3 %all-gather.11.cloned.1.call-start = ((), (), s32[]{:S(2)}) async-start(), calls=%async_computation.10 | async-start | bytes 3932160 | tf_op jit(solution)/shard_map/all_gather | solution.py:235
  130.0 173.2 %copy-start.62 = (f32[768]{0:T(1024)}, f32[768]{0:T(1024)S(1)}, u32[]{:S(2)}) copy-start(f32[768]{0:T(1024)S(1)} %get-tuple-element.1172) | copy-start | bytes 9220
  130.0 369.5 %copy-start.64 = (f32[768]{0:T(1024)}, f32[768]{0:T(1024)S(1)}, u32[]{:S(2)}) copy-start(f32[768]{0:T(1024)S(1)} %get-tuple-element.1171) | copy-start | bytes 9220
  130.7 174.9 %copy-start.75 = (f32[768]{0:T(1024)}, f32[768]{0:T(1024)S(1)}, u32[]{:S(2)}) copy-start(f32[768]{0:T(1024)S(1)} %get-tuple-element.1163) | copy-start | bytes 9220
  189.3 113.9 %copy-start.8 = (f32[512,768]{1,0:T(8,128)}, f32[512,768]{1,0:T(8,128)S(1)}, u32[]{:S(2)}) copy-start(f32[512,768]{1,0:T(8,128)S(1)} %get-tuple-element.1290) | copy-start | bytes 4718596
  189.3 113.9 %copy-start.66 = (f32[512]{0:T(512)}, f32[512]{0:T(512)S(1)}, u32[]{:S(2)}) copy-start(f32[512]{0:T(512)S(1)} %broadcast_multiply_fusion.3) | copy-start | bytes 6148
  189.7 113.6 %copy-start.70 = (f32[512]{0:T(512)}, f32[512]{0:T(512)S(1)}, u32[]{:S(2)}) copy-start(f32[512]{0:T(512)S(1)} %fusion.144) | copy-start | bytes 6148
  190.9 112.3 %reduce-scatter.11.cloned.1.call-start = ((), (), s32[]{:S(2)}) async-start(), calls=%async_computation.11 | async-start | bytes 7864320 | tf_op jit(solution)/shard_map/reduce_scatter | solution.py:239
  245.1 90.8 %all-gather.13.cloned.1.call-start = ((), (), s32[]{:S(2)}) async-start(), calls=%async_computation.12 | async-start | bytes 3932160 | tf_op jit(solution)/shard_map/all_gather | solution.py:212
  305.2 194.3 %copy-start.10 = (f32[512,768]{1,0:T(8,128)}, f32[512,768]{1,0:T(8,128)S(1)}, u32[]{:S(2)}) copy-start(f32[512,768]{1,0:T(8,128)S(1)} %get-tuple-element.1286) | copy-start | bytes 4718596
  305.2 194.3 %copy-start.68 = (f32[512]{0:T(512)}, f32[512]{0:T(512)S(1)}, u32[]{:S(2)}) copy-start(f32[512]{0:T(512)S(1)} %broadcast_multiply_fusion.2) | copy-start | bytes 6148
  305.5 193.9 %copy-start.72 = (f32[512]{0:T(512)}, f32[512]{0:T(512)S(1)}, u32[]{:S(2)}) copy-start(f32[512]{0:T(512)S(1)} %fusion.145) | copy-start | bytes 6148
  306.8 192.7 %reduce-scatter.13.cloned.1.call-start = ((), (), s32[]{:S(2)}) async-start(), calls=%async_computation.13 | async-start | bytes 7864320 | tf_op jit(solution)/shard_map/reduce_scatter | solution.py:232
  306.9 60.0 %copy-start.60 = (f32[5,384]{1,0:T(8,128)}, f32[5,384]{1,0:T(8,128)S(1)}, u32[]{:S(2)}) copy-start(f32[5,384]{1,0:T(8,128)S(1)} %pad_maximum_fusion.33) | copy-start | bytes 23044
  341.1 6.0 collective-permute-start.4
  344.2 6.6 collective-permute-start.5
  377.3 9.7 collective-permute-start.6
  379.6 7.5 collective-permute-start.7
  440.6 91.6 %all-gather.15.cloned.1.call-start = ((), (), s32[]{:S(2)}) async-start(), calls=%async_computation.14 | async-start | bytes 3932160 | tf_op jit(solution)/shard_map/all_gather | solution.py:235
  503.0 112.3 %reduce-scatter.15.cloned.1.call-start = ((), (), s32[]{:S(2)}) async-start(), calls=%async_computation.15 | async-start | bytes 7864320 | tf_op jit(solution)/shard_map/reduce_scatter | solution.py:239
  557.1 94.4 %all-gather.17.cloned.1.call-start = ((), (), s32[]{:S(2)}) async-start(), calls=%async_computation.16 | async-start | bytes 3932160 | tf_op jit(solution)/shard_map/all_gather | solution.py:294
  622.4 104.6 %reduce-scatter.17.cloned.1.call-start = ((), (), s32[]{:S(2)}) async-start(), calls=%async_computation.17 | async-start | bytes 7864320 | tf_op jit(solution)/shard_map/reduce_scatter | solution.py:303
  669.0 93.5 %all-gather.19.cloned.1.call-start = ((), (), s32[]{:S(2)}) async-start(), calls=%async_computation.18 | async-start | bytes 3932160 | tf_op jit(solution)/shard_map/all_gather | solution.py:311
  733.4 306.8 %reduce-scatter.19.cloned.1.call-start = ((), (), s32[]{:S(2)}) async-start(), calls=%async_computation.19 | async-start | bytes 7864320 | tf_op jit(solution)/shard_map/reduce_scatter | solution.py:349
  877.7 8.1 collective-permute-start.8
  882.3 8.7 collective-permute-start.9
  950.4 11.6 collective-permute-start.10
  959.8 8.3 collective-permute-start.11
  981.1 59.1 %copy-start.69 = (f32[512]{0:T(512)S(1)}, f32[512]{0:T(512)}, u32[]{:S(2)}) copy-start(f32[512]{0:T(512)} %copy-done.68) | copy-start | bytes 6148
  981.1 59.1 %copy-start.73 = (f32[512]{0:T(512)S(1)}, f32[512]{0:T(512)}, u32[]{:S(2)}) copy-start(f32[512]{0:T(512)} %copy-done.72) | copy-start | bytes 6148
  981.1 61.8 %copy-start.82 = (f32[512]{0:T(512)S(1)}, f32[512]{0:T(512)}, u32[]{:S(2)}) copy-start(f32[512]{0:T(512)} %copy-done.81) | copy-start | bytes 6148
  981.1 93.3 %all-gather.21.cloned.1.call-start = ((), (), s32[]{:S(2)}) async-start(), calls=%async_computation.20 | async-start | bytes 3932160 | tf_op jit(solution)/shard_map/all_gather | solution.py:294
  1045.3 104.7 %reduce-scatter.21.cloned.1.call-start = ((), (), s32[]{:S(2)}) async-start(), calls=%async_computation.21 | async-start | bytes 7864320 | tf_op jit(solution)/shard_map/reduce_scatter | solution.py:303
  1091.9 61.0 %copy-start.80 = (f32[512]{0:T(512)S(1)}, f32[512]{0:T(512)}, u32[]{:S(2)}) copy-start(f32[512]{0:T(512)} %copy-done.79) | copy-start | bytes 6148
  1091.9 93.6 %all-gather.23.cloned.1.call-start = ((), (), s32[]{:S(2)}) async-start(), calls=%async_computation.22 | async-start | bytes 3932160 | tf_op jit(solution)/shard_map/all_gather | solution.py:311
  1156.4 349.1 %reduce-scatter.23.cloned.1.call-start = ((), (), s32[]{:S(2)}) async-start(), calls=%async_computation.23 | async-start | bytes 7864320 | tf_op jit(solution)/shard_map/reduce_scatter | solution.py:349
  1305.0 8.1 collective-permute-start.12
  1310.5 9.0 collective-permute-start.13
  1392.7 10.8 collective-permute-start.14
  1400.4 7.6 collective-permute-start.15
  1419.8 504.6 %all-reduce.7.cloned.1.call-start = ((), (), s32[]{:S(2)}) async-start(), calls=%async_computation.24 | async-start | bytes 28311552 | tf_op jit(solution)/shard_map/psum | solution.py:373
  (171 other events, 1726.0 us)
Sparse Core Ops, SparseCore 0:
  9.6 29.1 all-gather.8
  128.8 58.7 reduce-scatter.8
  191.0 28.9 all-gather.10
  245.2 57.9 reduce-scatter.10
  306.9 28.9 all-gather.12
  440.7 58.7 reduce-scatter.12
  503.1 28.9 all-gather.14
  557.3 57.9 reduce-scatter.14
  622.6 28.9 all-gather.16
  669.1 57.9 reduce-scatter.16
  733.5 28.9 all-gather.18
  981.3 58.8 reduce-scatter.18
  1045.5 28.9 all-gather.20
  1092.0 57.9 reduce-scatter.20
  1156.5 28.9 all-gather.22
  1419.9 59.5 reduce-scatter.22
  1485.2 439.1 all-reduce.6
where the time goes:
time: 1960 us; the launch traced here: 1940 us
  waiting for transfers between devices  1070 us (55%)
  local copies, waits for them, and re-layouts  320 us (16%)
  matrix products  245 us (12%)
  other arithmetic  190 us (10%)
  starting transfers between devices  46.1 us (2%)
  blocking collectives  44.6 us (2%)
    psum x1, waiting for transfers between devices, seq_totals(): lax.psum((parts[0], parts[1], parts[2], parts[3], parts[4], parts[5], par...  416 us
    reduce_scatter x2, waiting for transfers between devices, layer_forward(): lax.psum_scatter(product(act, down_layer), 'mp', scatter_dimension=0, til...  116 us
    reduce_scatter x2, waiting for transfers between devices, layer_forward(): lax.psum_scatter(product(mixed, out_layer), 'mp', scatter_dimension=0, ti...  116 us
    reduce_scatter x2, waiting for transfers between devices, layer_backward(): lax.psum_scatter(product_right_t(grad_pre_low, up_layer), 'mp', scatter_d...  116 us
    reduce_scatter x2, waiting for transfers between devices, layer_backward(): lax.psum_scatter(jnp.einsum('tsw,sdw->td', grad_proj, qkv_layer, preferre...  58.9 us
    all_gather x2, waiting for transfers between devices, layer_backward(): lax.all_gather(grad_middle.astype(jnp.bfloat16), 'mp', axis=0, tiled=True)  57.9 us
    all_gather x2, waiting for transfers between devices, layer_backward(): lax.all_gather(grad_resid.astype(jnp.bfloat16), 'mp', axis=0, tiled=True)  57.6 us
    all_gather x2, waiting for transfers between devices, layer_forward(): lax.all_gather(normed.astype(jnp.bfloat16), 'mp', axis=0, tiled=True)  57 us
  transfers between devices with their start and end apart: 33, of which 26 were waited for; matrix products, arithmetic and copies ran while one was open for 4% of the time, Pallas kernels for 0%

commit v1 on v0

v1 whole, which is shorter than its diff:
```python
import jax
import jax.numpy as jnp
from jax import lax
from jax.experimental import pallas as pl
from jax.experimental.pallas import tpu as pltpu
from jax.sharding import PartitionSpec as P

HEAD_DIM = 64
LAYERS = 2
WINDOW = 64
POOL_REACH = 64
NORM_EPSILON = 1e-05
LEFT = 320
LEFT_SENT = 272
RIGHT = 256
BOTH = ("seq", "mp")
BF16 = jnp.bfloat16
F32 = jnp.float32


def product(left, right):
    return jnp.dot(left, right, preferred_element_type=F32)


def product_left_t(left, right):
    return lax.dot_general(left, right, (((0,), (0,)), ((), ())), preferred_element_type=F32)


def product_right_t(left, right):
    return lax.dot_general(left, right, (((1,), (1,)), ((), ())), preferred_element_type=F32)


def swap(values, axis, bit):
    count = lax.axis_size(axis)
    return lax.ppermute(values, axis, [(i, i ^ bit) for i in range(count)])


def shift(values, step):
    count = lax.axis_size("seq") * lax.axis_size("mp")
    return lax.ppermute(
        values, BOTH, [(i, i + step) for i in range(count) if 0 <= i + step < count]
    )


def gather_parts(own):
    across = swap(own, "mp", 2)
    return [own, swap(own, "mp", 1), across, swap(across, "mp", 1)]


def gather_small(own):
    return gather_parts(own)


def norm_forward(values, gain, offset):
    average = jnp.mean(values, axis=-1, keepdims=True)
    centered = values - average
    spread = jnp.mean(centered * centered, axis=-1, keepdims=True)
    inverse = lax.rsqrt(spread + NORM_EPSILON)
    unit = centered * inverse
    return unit * gain + offset, unit, inverse


def norm_backward(grad, unit, inverse, gain):
    scaled = grad * gain
    result = (
        scaled
        - jnp.mean(scaled, axis=-1, keepdims=True)
        - unit * jnp.mean(scaled * unit, axis=-1, keepdims=True)
    ) * inverse
    return result, jnp.sum(grad * unit, axis=0), jnp.sum(grad, axis=0)


def with_halo(rows):
    left = shift(rows[rows.shape[0] - LEFT_SENT :], 1)
    right = shift(rows[:RIGHT], -1)
    empty = jnp.zeros((LEFT - LEFT_SENT, rows.shape[1]), rows.dtype)
    return jnp.concatenate([empty, left, rows, right], axis=0)


def tap_mask(starts, finish, base_row):
    count = starts.shape[0] // 4
    reach = (POOL_REACH,)
    first = jnp.concatenate(
        [
            jnp.broadcast_to(starts[:1], reach),
            starts.reshape(count, 4)[:, 0],
            jnp.broadcast_to(starts[-1:], reach),
        ]
    )
    past = jnp.concatenate(
        [
            jnp.broadcast_to(finish[:1], reach),
            finish.reshape(count, 4)[:, 0],
            jnp.broadcast_to(finish[-1:], reach),
        ]
    )
    places = (
        base_row
        + 4 * (jnp.arange(count + 2 * POOL_REACH, dtype=jnp.int32)[:, None] - POOL_REACH)
        + jnp.arange(5, dtype=jnp.int32)[None]
        - 2
    )
    return (places >= first[:, None]) & (places < past[:, None])


PAIR = 128
TILE = 128
SPAN = TILE + 2 * WINDOW
POOL_SPAN = TILE // 4 + 2 * POOL_REACH
FAR = -1e30


def tile_bias(tile, first, past):
    lane = lax.broadcasted_iota(jnp.int32, (1, TILE), 1) + tile * TILE
    near = lax.broadcasted_iota(jnp.int32, (SPAN, 1), 0) + (tile * TILE - WINDOW)
    far = 4 * (lax.broadcasted_iota(jnp.int32, (POOL_SPAN, 1), 0) + (tile * (TILE // 4) - POOL_REACH))

    def one(keys, reach):
        low = jnp.maximum(lane - reach, first)
        high = jnp.minimum(lane + reach + 1, past)
        return jnp.where((keys >= low) & (keys < high), 0.0, FAR)

    return jnp.concatenate([one(near, WINDOW), one(far, 4 * POOL_REACH)], axis=0)


def pair_mask():
    return lax.broadcasted_iota(jnp.int32, (1, PAIR), 1) < HEAD_DIM


def stacked(rows):
    left = pair_mask()
    zero = jnp.zeros_like(rows)
    return jnp.concatenate([jnp.where(left, rows, zero), jnp.where(left, zero, rows)], axis=0)


def keys_of(wide_ref, pooled_ref, tile, lanes):
    near = wide_ref[pl.ds(pl.multiple_of(LEFT - WINDOW + tile * TILE, TILE), SPAN), lanes]
    far = pooled_ref[pl.ds(pl.multiple_of(tile * (TILE // 4), TILE // 4), POOL_SPAN), lanes]
    return jnp.concatenate([near, far], axis=0)


def unstack(both):
    return jnp.concatenate([both[:HEAD_DIM, :TILE], both[HEAD_DIM:, TILE:]], axis=0)


def pool_into(wide_ref, wide_f32, keep_ref, conv_ref, conv_bias_ref, which, pooled_ref):
    count = pooled_ref.shape[0]
    begin = LEFT - 4 * POOL_REACH - 2
    for pair in range(pooled_ref.shape[1] // PAIR):
        lanes = slice(pair * PAIR, (pair + 1) * PAIR)
        wide_f32[...] = wide_ref[:, lanes].astype(F32)
        total = jnp.broadcast_to(conv_bias_ref[which : which + 1, lanes], (count, PAIR))
        for tap in range(5):
            rows = wide_f32[pl.ds(begin + tap, count, stride=4), :]
            kept = jnp.where(keep_ref[:, tap : tap + 1] > 0.0, rows, 0.0)
            total = total + kept * conv_ref[which, tap : tap + 1, lanes]
        pooled_ref[:, lanes] = total.astype(BF16)


def attend_forward_kernel(
    q_ref, k_ref, v_ref, first_ref, past_ref, keep_ref, conv_ref, conv_bias_ref,
    mixed_ref, lse_ref, pooled_k_ref, pooled_v_ref, wide_f32,
):
    pool_into(k_ref, wide_f32, keep_ref, conv_ref, conv_bias_ref, 0, pooled_k_ref)
    pool_into(v_ref, wide_f32, keep_ref, conv_ref, conv_bias_ref, 1, pooled_v_ref)
    pairs = q_ref.shape[1] // PAIR

    @pl.loop(0, q_ref.shape[0] // TILE)
    def _(tile):
        rows = pl.ds(pl.multiple_of(tile * TILE, TILE), TILE)
        bias = tile_bias(tile, first_ref[tile], past_ref[tile])
        bias = jnp.concatenate([bias, bias], axis=1)
        for pair in range(pairs):
            lanes = slice(pair * PAIR, (pair + 1) * PAIR)
            query = stacked(q_ref[rows, lanes] * BF16(HEAD_DIM**-0.5))
            key = keys_of(k_ref, pooled_k_ref, tile, lanes)
            value = keys_of(v_ref, pooled_v_ref, tile, lanes)
            scores = product_right_t(key, query) + bias
            most = jnp.max(scores, axis=0, keepdims=True)
            weight = jnp.exp(scores - most)
            total = jnp.sum(weight, axis=0, keepdims=True)
            both = product_left_t(value, weight.astype(BF16)) * (1.0 / total)
            mixed_ref[rows, lanes] = unstack(both).T.astype(BF16)
            lse_ref[tile, pair : pair + 1, :] = most + jnp.log(total)


def attend_backward_kernel(
    q_ref, k_ref, v_ref, pooled_k_ref, pooled_v_ref, grad_ref, lse_ref,
    first_ref, past_ref, keep_ref, conv_ref,
    grad_q_ref, grad_k_ref, grad_v_ref, small_ref,
    wide_k, wide_v, far_k, far_v, wide_f32,
):
    pairs = q_ref.shape[1] // PAIR
    wide_k[...] = jnp.zeros_like(wide_k)
    wide_v[...] = jnp.zeros_like(wide_v)
    far_k[...] = jnp.zeros_like(far_k)
    far_v[...] = jnp.zeros_like(far_v)
    small_ref[...] = jnp.zeros_like(small_ref)

    @pl.loop(0, q_ref.shape[0] // TILE)
    def _(tile):
        rows = pl.ds(pl.multiple_of(tile * TILE, TILE), TILE)
        near = pl.ds(pl.multiple_of(LEFT - WINDOW + tile * TILE, TILE), SPAN)
        far = pl.ds(pl.multiple_of(tile * (TILE // 4), TILE // 4), POOL_SPAN)
        bias = tile_bias(tile, first_ref[tile], past_ref[tile])
        bias = jnp.concatenate([bias, bias], axis=1)
        for pair in range(pairs):
            lanes = slice(pair * PAIR, (pair + 1) * PAIR)
            query = stacked(q_ref[rows, lanes] * BF16(HEAD_DIM**-0.5))
            grad = stacked(grad_ref[rows, lanes])
            key = keys_of(k_ref, pooled_k_ref, tile, lanes)
            value = keys_of(v_ref, pooled_v_ref, tile, lanes)
            scores = product_right_t(key, query) + bias
            probs = jnp.exp(scores - lse_ref[tile, pair : pair + 1, :])
            grad_probs = product_right_t(value, grad)
            delta = jnp.sum(probs * grad_probs, axis=0, keepdims=True)
            grad_scores = (probs * (grad_probs - delta)).astype(BF16)
            grad_value = product(probs.astype(BF16), grad)
            grad_key = product(grad_scores, query)
            wide_v[pair, near, :] += grad_value[:SPAN]
            far_v[far, lanes] += grad_value[SPAN:]
            wide_k[pair, near, :] += grad_key[:SPAN]
            far_k[far, lanes] += grad_key[SPAN:]
            grad_query = unstack(product_left_t(key, grad_scores)).T * (HEAD_DIM**-0.5)
            grad_q_ref[rows, lanes] = grad_query.astype(BF16)
            small_ref[0:1, lanes] += jnp.sum(grad_query, axis=0, keepdims=True)

    count = far_k.shape[0]
    begin = LEFT - 4 * POOL_REACH - 2
    for which, (source, wide, pooled, result) in enumerate(
        ((k_ref, wide_k, far_k, grad_k_ref), (v_ref, wide_v, far_v, grad_v_ref))
    ):
        for pair in range(pairs):
            lanes = slice(pair * PAIR, (pair + 1) * PAIR)
            wide_f32[...] = source[:, lanes].astype(F32)
            grad = pooled[:, lanes]
            at = 12 + which
            small_ref[at : at + 1, lanes] = jnp.sum(grad, axis=0, keepdims=True)
            for tap in range(5):
                places = pl.ds(begin + tap, count, stride=4)
                kept = jnp.where(keep_ref[:, tap : tap + 1] > 0.0, grad, 0.0)
                at = 2 + 5 * which + tap
                small_ref[at : at + 1, lanes] = jnp.sum(
                    kept * wide_f32[places, :], axis=0, keepdims=True
                )
                wide[pair, places, :] += kept * conv_ref[which, tap : tap + 1, lanes]
            if which == 1:
                small_ref[1:2, lanes] = jnp.sum(wide[pair], axis=0, keepdims=True)
            result[:, lanes] = wide[pair].astype(BF16)


def in_vmem(count):
    return [pl.BlockSpec(memory_space=pltpu.VMEM)] * count


VMEM_LIMIT = 56 * 1024 * 1024


def attend_forward(queries, keys, values, first, past, keep, conv, conv_bias):
    total, width = queries.shape
    count = total // 4 + 2 * POOL_REACH
    shape = jax.ShapeDtypeStruct
    return pl.pallas_call(
        attend_forward_kernel,
        out_shape=(
            shape((total, width), BF16),
            shape((total // TILE, width // PAIR, 2 * TILE), F32),
            shape((count, width), BF16),
            shape((count, width), BF16),
        ),
        in_specs=in_vmem(8),
        out_specs=tuple(in_vmem(4)),
        scratch_shapes=[pltpu.VMEM((keys.shape[0], PAIR), F32)],
        compiler_params=pltpu.CompilerParams(vmem_limit_bytes=VMEM_LIMIT),
        name="attend_forward",
    )(queries, keys, values, first, past, keep, conv, conv_bias)


def attend_backward(queries, keys, values, pooled_k, pooled_v, grad, lse, first, past, keep, conv):
    total, width = queries.shape
    shape = jax.ShapeDtypeStruct
    return pl.pallas_call(
        attend_backward_kernel,
        out_shape=(
            shape((total, width), BF16),
            shape(keys.shape, BF16),
            shape(keys.shape, BF16),
            shape((16, width), F32),
        ),
        in_specs=in_vmem(11),
        out_specs=tuple(in_vmem(4)),
        scratch_shapes=[
            pltpu.VMEM((width // PAIR, keys.shape[0], PAIR), F32),
            pltpu.VMEM((width // PAIR, keys.shape[0], PAIR), F32),
            pltpu.VMEM(pooled_k.shape, F32),
            pltpu.VMEM(pooled_k.shape, F32),
            pltpu.VMEM((keys.shape[0], PAIR), F32),
        ],
        compiler_params=pltpu.CompilerParams(vmem_limit_bytes=VMEM_LIMIT),
        name="attend_backward",
    )(queries, keys, values, pooled_k, pooled_v, grad, lse, first, past, keep, conv)


def gelu_parts(pre):
    size = jnp.abs(pre) * (0.5**0.5)
    t = 1.0 / (1.0 + 0.5 * size)
    series = 0.17087277
    for term in (-0.82215223, 1.48851587, -1.13520398, 0.27886807, -0.18628806, 0.09678418,
                 0.37409196, 1.00002368, -1.26551223):
        series = series * t + term
    tail = 0.5 * t * jnp.exp(series - size * size)
    cdf = jnp.where(pre < 0.0, tail, 1.0 - tail)
    density = jnp.exp(-0.5 * pre * pre) * (0.5 / jnp.pi) ** 0.5
    return pre * cdf, cdf + pre * density


def layer_forward(hidden, masks, weights):
    first, past, keep = masks
    qkv, qv, conv, conv_bias, out, up, up_bias, down, gains, biases = weights
    total = hidden.shape[0]
    entry_wide = with_halo(hidden.astype(BF16))
    entry = entry_wide[LEFT : LEFT + total]
    queries = (product(entry, qkv[0]) + qv[0]).astype(BF16)
    keys = product(entry_wide, qkv[1]).astype(BF16)
    values = (product(entry_wide, qkv[2]) + qv[1]).astype(BF16)

    mixed, lse, pooled_k, pooled_v = attend_forward(
        queries, keys, values, first, past, keep, conv, conv_bias
    )
    resid = hidden + (product(mixed, out) + biases[0])
    normed, unit_one, inverse_one = norm_forward(resid, gains[0], biases[1])
    normed_low = normed.astype(BF16)
    pre = product(normed_low, up) + up_bias
    act, slope = gelu_parts(pre)
    act, slope = act.astype(BF16), slope.astype(BF16)
    middle = normed + (product(act, down) + biases[2])
    result, unit_two, inverse_two = norm_forward(middle, gains[1], biases[3])
    saved = (
        entry_wide,
        queries,
        keys,
        values,
        pooled_k,
        pooled_v,
        mixed,
        lse,
        unit_one,
        inverse_one,
        normed_low,
        act,
        slope,
        unit_two,
        inverse_two,
    )
    return result, saved


def split_rows(values):
    return jnp.split(values, 4, axis=0)


def reduce_parts(parts):
    sent = jnp.stack([parts[1], parts[3]]).astype(BF16)
    received = swap(sent, "mp", 1).astype(F32)
    own = parts[0] + received[0]
    across = parts[2] + received[1]
    own = own + swap(across.astype(BF16), "mp", 2).astype(F32)
    place = lax.axis_index("seq")
    count = lax.axis_size("seq")
    bit = 1
    while bit < count:
        half = own.shape[0] // 2
        side = (place // bit) % 2
        kept = lax.dynamic_slice_in_dim(own, side * half, half, 0)
        given = lax.dynamic_slice_in_dim(own, (1 - side) * half, half, 0).astype(BF16)
        own = kept + swap(given, "seq", bit).astype(F32)
        bit *= 2
    whole = own.astype(BF16)
    while bit > 1:
        bit //= 2
        side = (place // bit) % 2
        other = swap(whole, "seq", bit)
        whole = jnp.where(
            side == 0,
            jnp.concatenate([whole, other], axis=0),
            jnp.concatenate([other, whole], axis=0),
        )
    return whole


def layer_backward(grad_out, masks, weights, saved):
    first, past, keep = masks
    qkv, qv, conv, conv_bias, out, up, up_bias, down, gains, biases = weights
    (
        entry_wide,
        queries,
        keys,
        values,
        pooled_k,
        pooled_v,
        mixed,
        lse,
        unit_one,
        inverse_one,
        normed_low,
        act,
        slope,
        unit_two,
        inverse_two,
    ) = saved
    total, width = queries.shape
    grad_middle, gain_two, shift_two = norm_backward(grad_out, unit_two, inverse_two, gains[1])
    bias_down = jnp.sum(grad_middle, axis=0)
    grad_middle_low = grad_middle.astype(BF16)
    grad_w_down = product_left_t(act, grad_middle_low)
    grad_pre = product_right_t(grad_middle_low, down) * slope.astype(F32)
    grad_b_up = jnp.sum(grad_pre, axis=0)
    grad_pre_low = grad_pre.astype(BF16)
    grad_w_up_t = product_left_t(grad_pre_low, normed_low)
    feed_parts = [
        jnp.concatenate(pair, axis=0)
        for pair in zip(split_rows(grad_w_down), split_rows(grad_w_up_t))
    ]
    feed = reduce_parts(feed_parts)
    grad_normed = product_right_t(grad_pre_low, up) + grad_middle
    grad_resid, gain_one, shift_one = norm_backward(grad_normed, unit_one, inverse_one, gains[0])
    bias_out = jnp.sum(grad_resid, axis=0)
    grad_resid_low = grad_resid.astype(BF16)
    grad_w_out = product_left_t(mixed, grad_resid_low)
    grad_mixed = product_right_t(grad_resid_low, out).astype(BF16)
    grad_q_low, grad_k_low, grad_v_low, small = attend_backward(
        queries, keys, values, pooled_k, pooled_v, grad_mixed, lse, first, past, keep, conv
    )
    entry = entry_wide[LEFT : LEFT + total]
    w_q = product_left_t(grad_q_low, entry)
    w_k = product_left_t(grad_k_low, entry_wide)
    w_v = product_left_t(grad_v_low, entry_wide)
    rest_parts = [
        jnp.concatenate(pieces, axis=0)
        for pieces in zip(*(split_rows(piece) for piece in (grad_w_out, w_q, w_k, w_v)))
    ]
    rest = reduce_parts(rest_parts)
    wide_grad = product_right_t(grad_k_low, qkv[1]) + product_right_t(grad_v_low, qkv[2])
    from_right = shift(wide_grad[LEFT - LEFT_SENT : LEFT].astype(BF16), -1).astype(F32)
    from_left = shift(wide_grad[LEFT + total :].astype(BF16), 1).astype(F32)
    grad_hidden = (
        product_right_t(grad_q_low, qkv[0])
        + wide_grad[LEFT : LEFT + total]
        + grad_resid
        + jnp.pad(from_right, ((total - LEFT_SENT, 0), (0, 0)))
        + jnp.pad(from_left, ((0, total - RIGHT), (0, 0)))
    )
    grad_b_up_rows = grad_b_up.reshape(4, -1, width // 4).transpose(1, 0, 2).reshape(-1, width)
    small_split = jnp.concatenate([small[:14], grad_b_up_rows], axis=0)
    small_whole = jnp.stack([gain_one, gain_two, bias_out, shift_one, bias_down, shift_two])
    return grad_hidden, feed, rest, small_split, small_whole


def to_absolute(rows):
    quarter = rows.shape[1] // 4
    parts = [rows[:, k * quarter : (k + 1) * quarter] for k in range(4)]
    place = lax.axis_index("mp")
    odd, high = place % 2 == 1, place // 2 == 1
    parts = [jnp.where(odd, parts[k ^ 1], parts[k]) for k in range(4)]
    parts = [jnp.where(high, parts[k ^ 2], parts[k]) for k in range(4)]
    return jnp.concatenate(parts, axis=1)


def shards(
    inputs,
    doc_bounds,
    qkv_weight,
    qv_bias,
    conv_weight,
    conv_bias,
    out_weight,
    up_weight,
    up_bias,
    down_weight,
    norm_gains,
    shared_biases,
    cotangent,
):
    total, width = inputs.shape
    place = lax.axis_index("mp")
    base_row = lax.axis_index("seq") * doc_bounds.shape[1] + place * total
    bounds = lax.dynamic_slice_in_dim(doc_bounds, place * total, total, 1)
    keep = jnp.pad(tap_mask(bounds[0], bounds[1], base_row).astype(F32), ((0, 0), (0, 3)))
    near_bounds = (bounds - base_row).reshape(2, total // TILE, 1, TILE)
    masks = (near_bounds[0], near_bounds[1], keep)
    quarter = width // 4
    small = jnp.concatenate(
        [
            qv_bias.reshape(-1, quarter),
            conv_weight.reshape(-1, quarter),
            conv_bias.reshape(-1, quarter),
            up_bias.reshape(-1, quarter),
        ],
        axis=0,
    )
    small = gather_small(small)
    layers = []
    for index in range(LAYERS):
        qkv = jnp.concatenate(gather_parts(qkv_weight[index]), axis=2)
        out = jnp.concatenate(gather_parts(out_weight[index]), axis=0)
        up = jnp.concatenate(gather_parts(up_weight[index]), axis=1)
        down = jnp.concatenate(gather_parts(down_weight[index]), axis=0)
        layers.append((qkv, out, up, down))
    wide_small = jnp.concatenate(small, axis=1)
    qv_all = wide_small[:4].reshape(2, 2, width)
    conv_all = wide_small[4:24].reshape(2, 2, 5, width)
    conv_bias_all = wide_small[24:28].reshape(2, 2, width)
    up_bias_all = jnp.stack([part[28:].reshape(2, -1) for part in small], axis=1).reshape(2, -1)
    hidden = inputs.astype(F32)
    stack = []
    for index in range(LAYERS):
        qkv, out, up, down = layers[index]
        weights = (
            qkv,
            qv_all[index],
            conv_all[index],
            conv_bias_all[index],
            out,
            up,
            up_bias_all[index],
            down,
            norm_gains[index],
            shared_biases[index],
        )
        hidden, saved = layer_forward(hidden, masks, weights)
        stack.append((weights, saved))
    gradient = cotangent.astype(F32)
    collected = [None] * LAYERS
    for index in reversed(range(LAYERS)):
        weights, saved = stack[index]
        gradient, feed, rest, split, whole = layer_backward(gradient, masks, weights, saved)
        collected[index] = (feed, rest, split, whole)
    feed = jnp.stack([part[0] for part in collected]).astype(F32)
    rest = jnp.stack([part[1] for part in collected]).astype(F32)
    small_split = jnp.stack([to_absolute(part[2]) for part in collected])
    small_whole = jnp.stack([part[3] for part in collected])
    small_total = lax.psum(jnp.concatenate([small_split, small_whole], axis=1), BOTH)
    own_small = lax.dynamic_slice_in_dim(small_total[:, :18], place * quarter, quarter, 2)
    units = down_weight.shape[1]
    return (
        hidden,
        gradient,
        rest[:, quarter:].reshape(2, 3, quarter, width).transpose(0, 1, 3, 2),
        own_small[:, :2],
        own_small[:, 2:12].reshape(2, 2, 5, quarter),
        own_small[:, 12:14],
        rest[:, :quarter],
        feed[:, units:].transpose(0, 2, 1),
        own_small[:, 14:18].reshape(2, -1),
        feed[:, :units],
        small_total[:, 18:20],
        small_total[:, 20:24],
    )


def solution(mesh):
    return jax.shard_map(
        shards,
        mesh=mesh,
        in_specs=(
            P(BOTH, None),
            P(None, "seq"),
            P(None, None, None, "mp"),
            P(None, None, "mp"),
            P(None, None, None, "mp"),
            P(None, None, "mp"),
            P(None, "mp", None),
            P(None, None, "mp"),
            P(None, "mp"),
            P(None, "mp", None),
            P(),
            P(),
            P(BOTH, None),
        ),
        out_specs=(
            P(BOTH, None),
            P(BOTH, None),
            P(None, None, None, "mp"),
            P(None, None, "mp"),
            P(None, None, None, "mp"),
            P(None, None, "mp"),
            P(None, "mp", None),
            P(None, None, "mp"),
            P(None, "mp"),
            P(None, "mp", None),
            P(),
            P(),
        ),
        check_vma=False,
    )
```

time: 1960 us -> 842 us (0.43)
  waiting for transfers between devices: 1070 us -> 288 us
  local copies, waits for them, and re-layouts: 320 us -> 101 us
  other arithmetic: 190 us -> 76 us
  matrix products: 245 us -> 169 us
  Pallas kernels: 0 us -> 71.7 us
  starting transfers between devices: 46.1 us -> 116 us
  blocking collectives: 44.6 us -> 0 us
    reduce_scatter x8 -> x0, waiting for transfers between devices: 407 us -> none  [the longest x2 116 us: layer_forward(): lax.psum_scatter(product(act, down_layer), 'mp', scatter_dimension=0, til...]
    psum x1, waiting for transfers between devices: 416 us -> 69.6 us  [shards(): lax.psum(jnp.concatenate([small_split, small_whole], axis=1), BOTH)]
    all_gather x8 -> x0, waiting for transfers between devices: 227 us -> none  [the longest x2 57.9 us: layer_backward(): lax.all_gather(grad_middle.astype(jnp.bfloat16), 'mp', axis=0, tiled=True)]
    ppermute x16 -> x67, waiting for transfers between devices: 21.6 us -> 218 us  [the longest x59 218 us: swap(): return lax.ppermute(values, axis, [(i, i ^ bit) for i in range(count)])]
    dot_general x66 -> x12, matrix products: 182 us -> 55.7 us  [product(): return jnp.dot(left, right, preferred_element_type=F32)]
    scatter-add x14 -> x0, local copies, waits for them, and re-layouts: 76.7 us -> none  [the longest x2 30.3 us: layer_backward(): grad_kv.at[WINDOW - 2:WINDOW - 2 + total]]
    ppermute x16 -> x67, starting transfers between devices: 43.6 us -> 116 us  [the longest x59 87.9 us: swap(): return lax.ppermute(values, axis, [(i, i ^ bit) for i in range(count)])]
    pallas_call x0 -> x4, Pallas kernels: none -> 71.7 us  [the longest x2 39.7 us: attend_backward(): pl.pallas_call(attend_backward_kernel, out_shape=(shape((total, width), B...]
  transfers between devices with their start and end apart: 33 -> 68, of which waited for: 26 -> 19; matrix products, arithmetic and copies ran while one was open for 4% -> 31% of each run, Pallas kernels for 0% -> 6%
where the time goes in v1:
time: 842 us; the launch traced here: 838 us
  waiting for transfers between devices  288 us (34%)
  matrix products  169 us (20%)
  starting transfers between devices  116 us (14%)
  local copies, waits for them, and re-layouts  101 us (12%)
  other arithmetic  76 us (9%)
  Pallas kernels  71.7 us (9%)
  between operations  16.5 us (2%)
    ppermute x59, waiting for transfers between devices, swap(): return lax.ppermute(values, axis, [(i, i ^ bit) for i in range(count)])  218 us
    ppermute x59, starting transfers between devices, swap(): return lax.ppermute(values, axis, [(i, i ^ bit) for i in range(count)])  87.9 us
    dot_general x12, matrix products, product_right_t(): lax.dot_general(left, right, (((1,), (1,)), ((), ())), preferred_element_...  72.4 us
    psum x1, waiting for transfers between devices, shards(): lax.psum(jnp.concatenate([small_split, small_whole], axis=1), BOTH)  69.6 us
    dot_general x12, matrix products, product(): return jnp.dot(left, right, preferred_element_type=F32)  55.7 us
    dot_general x12, matrix products, product_left_t(): lax.dot_general(left, right, (((0,), (0,)), ((), ())), preferred_element_...  41.2 us
    pallas_call x2, Pallas kernels, attend_backward(): pl.pallas_call(attend_backward_kernel, out_shape=(shape((total, width), B...  39.7 us
    pallas_call x2, Pallas kernels, attend_forward(): pl.pallas_call(attend_forward_kernel, out_shape=(shape((total, width), BF...  32 us
  transfers between devices with their start and end apart: 68, of which 19 were waited for; matrix products, arithmetic and copies ran while one was open for 31% of the time, Pallas kernels for 6%

profile of v1, /device:TPU:15, one launch (start us, length us, event | category | flops | bytes accessed | tf_op | source)
XLA Modules:
  0.0 837.6 jit_solution(6592730742566883818)
XLA Ops:
  26.9 7.5 collective-permute-done.1
  41.2 5.6 collective-permute-start.6
  54.9 20.0 %collective-permute-done.9 = bf16[192,768]{1,0:T(8,128)(2,1)S(1)} collective-permute-done((bf16[192,768]{1,0:T(8,128)(2,1)S(1)}, bf16[192,768]{1,0:T(8,128)(2,1)S(1)}, u32[]{:S(2)}, u32[]{:S(2)}) %collective-permute-start.9) | collective-permute-done | bytes 294944 | tf_op jit(solution)/shard_map/ppermute | solution.py:35
  77.2 3.9 add_convert_fusion.1.v_ref
  81.1 3.9 convolution_convert_fusion.1.k_ref
  86.7 15.9 %attend_forward.2 = (bf16[512,768]{1,0:T(8,128)(2,1)}, f32[4,6,256]{2,1,0:T(8,128)}, bf16[256,768]{1,0:T(8,128)(2,1)}, bf16[256,768]{1,0:T(8,128)(2,1)}) custom-call(bf16[512,768]{1,0:T(8,128)(2,1)} %fusion.60.q_ref, bf16[1088,768]{1,0:T(8,128)(2,1)} %convolution_convert_fusion.1.k_ref, bf16[1088,768]{1,0:T(8,128)(2,1)} %add_convert_fusion.1.v_ref, ...), custom_call_target="tpu_custom_call" | custom-call | tf_op jit(solution)/shard_map/attend_forward/pallas_call | solution.py:263
  108.0 13.9 %multiply_convert_fusion.1 = (bf16[512,3072]{1,0:T(8,128)(2,1)S(1)}, f32[512,3072]{1,0:T(8,128)}) fusion(f32[3072]{0:T(1024)S(1)} %bitcast.206, bf16[768,768]{1,0:T(8,128)(2,1)S(1)} %collective-permute-done.13, bf16[768,768]{1,0:T(8,128)(2,1)} %collective-permute-done.12, bf16[768,768]{1,0:T(8,128)(2,1)S(1)} %collective-permute-done.11, ...), kind=kOutput, calls=%fused_computation.21 | convolution fusion | flops 2488664064 | bytes 15751168 | tf_op jit(solution)/shard_map/dot_general | solution.py:22
  127.7 4.0 fusion.149
  134.9 5.0 collective-permute-start.20
  142.8 15.5 %collective-permute-done.23 = bf16[192,768]{1,0:T(8,128)(2,1)S(1)} collective-permute-done((bf16[192,768]{1,0:T(8,128)(2,1)S(1)}, bf16[192,768]{1,0:T(8,128)(2,1)S(1)}, u32[]{:S(2)}, u32[]{:S(2)}) %collective-permute-start.23) | collective-permute-done | bytes 294944 | tf_op jit(solution)/shard_map/ppermute | solution.py:35
  159.8 28.9 %collective-permute-start.24 = (bf16[192,768]{1,0:T(8,128)(2,1)S(1)}, bf16[192,768]{1,0:T(8,128)(2,1)S(1)}, u32[]{:S(2)}, u32[]{:S(2)}) collective-permute-start(bf16[192,768]{1,0:T(8,128)(2,1)S(1)} %collective-permute-done.23), channel_id=1, source_target_pairs={{0,1},{1,0},{2,3},{3,2},{4,5},{5,4},{6,7},{7,6},{8,9},{9,8},{10,11... | collective-permute-start | bytes 884744 | tf_op jit(solution)/shard_map/ppermute | solution.py:35
  195.8 16.1 %attend_forward.3 = (bf16[512,768]{1,0:T(8,128)(2,1)}, f32[4,6,256]{2,1,0:T(8,128)}, bf16[256,768]{1,0:T(8,128)(2,1)}, bf16[256,768]{1,0:T(8,128)(2,1)}) custom-call(bf16[512,768]{1,0:T(8,128)(2,1)} %add_convert_fusion.2.q_ref, bf16[1088,768]{1,0:T(8,128)(2,1)} %convolution_convert_fusion.k_ref, bf16[1088,768]{1,0:T(8,128)(2,1)} %add_convert_fusion.v_ref, ...), custom_call_target="tpu_custom_call" | custom-call | tf_op jit(solution)/shard_map/attend_forward/pallas_call | solution.py:263
  215.2 11.0 %multiply_convert_fusion = (bf16[512,3072]{1,0:T(8,128)(2,1)S(1)}, f32[512,3072]{1,0:T(8,128)S(1)}) fusion(f32[3072]{0:T(1024)S(1)} %bitcast.208, bf16[768,768]{1,0:T(8,128)(2,1)} %collective-permute-done.27, bf16[768,768]{1,0:T(8,128)(2,1)} %collective-permute-done.26, bf16[768,768]{1,0:T(8,128)(2,1)S(1)} %collective-permute-done.25, ...), kind=kOutput, calls=%fused_computation.16 | convolution fusion | flops 2488664064 | bytes 15751168 | tf_op jit(solution)/shard_map/dot_general | solution.py:22
  226.3 5.5 fusion.151
  236.1 17.1 %fusion.162 = (f32[3072]{0:T(1024)}, bf16[512,3072]{1,0:T(8,128)(2,1)S(1)}) fusion(f32[512,3072]{1,0:T(8,128)S(1)} %get-tuple-element.232, f32[3072]{0:T(1024)S(1)} %bitcast.209, bf16[768,768]{1,0:T(8,128)(2,1)S(1)} %collective-permute-done.30, bf16[768,768]{1,0:T(8,128)(2,1)} %collective-permute-done.29, ...), kind=kOutput, calls=%fused_computation.374 | convolution fusion | flops 2499671040 | bytes 15753216 | tf_op jit(solution)/shard_map/dot_general | solution.py:30
  253.2 7.1 multiply_reduce_fusion
  263.2 19.7 %attend_backward.2 = (bf16[512,768]{1,0:T(8,128)(2,1)}, bf16[1088,768]{1,0:T(8,128)(2,1)}, bf16[1088,768]{1,0:T(8,128)(2,1)}, f32[16,768]{1,0:T(8,128)}) custom-call(bf16[512,768]{1,0:T(8,128)(2,1)} %add_convert_fusion.2.q_ref, bf16[1088,768]{1,0:T(8,128)(2,1)} %convolution_convert_fusion.k_ref, bf16[1088,768]{1,0:T(8,128)(2,1)} %add_convert_fusion.v_ref, ...), custom_call_target="tpu_custom_call" | custom-call | tf_op jit(solution)/shard_map/attend_backward/pallas_call | solution.py:282
  286.4 4.6 fusion.152
  294.4 6.7 fusion.164
  301.2 6.6 fusion.165
  336.9 5.0 fusion.124
  341.9 4.0 multiply_reduce_fusion.1
  347.9 16.4 %fusion.163 = (f32[3072]{0:T(1024)S(1)}, bf16[512,3072]{1,0:T(8,128)(2,1)S(1)}) fusion(f32[512,3072]{1,0:T(8,128)S(1)} %bitcast.211, f32[3072]{0:T(1024)S(1)} %bitcast.207, bf16[768,768]{1,0:T(8,128)(2,1)S(1)} %copy-done.108, bf16[768,768]{1,0:T(8,128)(2,1)} %collective-permute-done.15, bf16[768,768]{1,0:T(8,128)(2,1)S(1)} %copy-done.106, ...), kind=kOutput, calls=%fused_computation.375 | convolution fusion | flops 2499671040 | bytes 15753216 | tf_op jit(solution)/shard_map/dot_general | solution.py:30
  364.4 6.3 multiply_reduce_fusion.2
  373.7 19.9 %attend_backward.3 = (bf16[512,768]{1,0:T(8,128)(2,1)}, bf16[1088,768]{1,0:T(8,128)(2,1)}, bf16[1088,768]{1,0:T(8,128)(2,1)}, f32[16,768]{1,0:T(8,128)}) custom-call(bf16[512,768]{1,0:T(8,128)(2,1)} %fusion.60.q_ref, bf16[1088,768]{1,0:T(8,128)(2,1)} %convolution_convert_fusion.1.k_ref, bf16[1088,768]{1,0:T(8,128)(2,1)} %add_convert_fusion.1.v_ref, ...), custom_call_target="tpu_custom_call" | custom-call | tf_op jit(solution)/shard_map/attend_backward/pallas_call | solution.py:282
  401.6 5.5 fusion.166
  407.1 5.0 fusion.167
  412.1 4.8 collective-permute-start.34
  417.0 4.4 fusion.158
  424.7 4.5 fusion.159
  453.6 5.0 fusion.123
  466.8 4.8 convert_element_type.282
  497.0 69.6 %all-reduce.7.cloned.1.call-done = f32[2,24,768]{2,1,0:T(8,128)} async-done(((f32[2,24,768]{2,1,0:T(8,128)}), f32[2,24,768]{2,1,0:T(8,128)}) %all-reduce.7.cloned.1.call-update) | async-done | bytes 147472 | tf_op jit(solution)/shard_map/psum | solution.py:542
  576.3 4.3 fusion.17
  582.6 37.3 %collective-permute-done.52 = bf16[1536,768]{1,0:T(8,128)(2,1)} collective-permute-done((bf16[1536,768]{1,0:T(8,128)(2,1)}, bf16[1536,768]{1,0:T(8,128)(2,1)}, u32[]{:S(2)}, u32[]{:S(2)}) %collective-permute-start.52) | collective-permute-done | bytes 2359328 | tf_op jit(solution)/shard_map/ppermute | solution.py:35
  620.0 4.2 fusion.21
  629.6 4.0 collective-permute-done.47
  638.7 12.4 %collective-permute-done.53 = bf16[768,768]{1,0:T(8,128)(2,1)S(1)} collective-permute-done((bf16[768,768]{1,0:T(8,128)(2,1)S(1)}, bf16[768,768]{1,0:T(8,128)(2,1)S(1)}, u32[]{:S(2)}, u32[]{:S(2)}) %collective-permute-start.53) | collective-permute-done | bytes 1179680 | tf_op jit(solution)/shard_map/ppermute | solution.py:35
  656.2 19.2 %collective-permute-done.54 = bf16[384,768]{1,0:T(8,128)(2,1)S(1)} collective-permute-done((bf16[384,768]{1,0:T(8,128)(2,1)S(1)}, bf16[384,768]{1,0:T(8,128)(2,1)S(1)}, u32[]{:S(2)}, u32[]{:S(2)}) %collective-permute-start.54) | collective-permute-done | bytes 589856 | tf_op jit(solution)/shard_map/ppermute | solution.py:35
  680.9 19.1 %collective-permute-done.55 = bf16[192,768]{1,0:T(8,128)(2,1)S(1)} collective-permute-done((bf16[192,768]{1,0:T(8,128)(2,1)S(1)}, bf16[192,768]{1,0:T(8,128)(2,1)S(1)}, u32[]{:S(2)}, u32[]{:S(2)}) %collective-permute-start.55) | collective-permute-done | bytes 294944 | tf_op jit(solution)/shard_map/ppermute | solution.py:35
  703.5 8.3 collective-permute-start.41
  711.8 4.1 collective-permute-done.64
  742.3 12.2 %collective-permute-done.57 = bf16[384,768]{1,0:T(8,128)(2,1)S(1)} collective-permute-done((bf16[384,768]{1,0:T(8,128)(2,1)S(1)}, bf16[384,768]{1,0:T(8,128)(2,1)S(1)}, u32[]{:S(2)}, u32[]{:S(2)}) %collective-permute-start.57) | collective-permute-done | bytes 589856 | tf_op jit(solution)/shard_map/ppermute | solution.py:35
  760.8 7.4 collective-permute-done.42
  772.2 21.4 %collective-permute-done.66 = bf16[768,768]{1,0:T(8,128)(2,1)S(1)} collective-permute-done((bf16[768,768]{1,0:T(8,128)(2,1)S(1)}, bf16[768,768]{1,0:T(8,128)(2,1)S(1)}, u32[]{:S(2)}, u32[]{:S(2)}) %collective-permute-start.66) | collective-permute-done | bytes 1179680 | tf_op jit(solution)/shard_map/ppermute | solution.py:35
  794.2 24.6 %collective-permute-done.58 = bf16[768,768]{1,0:T(8,128)(2,1)S(1)} collective-permute-done((bf16[768,768]{1,0:T(8,128)(2,1)S(1)}, bf16[768,768]{1,0:T(8,128)(2,1)S(1)}, u32[]{:S(2)}, u32[]{:S(2)}) %collective-permute-start.58) | collective-permute-done | bytes 1179680 | tf_op jit(solution)/shard_map/ppermute | solution.py:35
  820.1 4.4 fusion.121
  824.5 6.0 copy.52
  (611 shorter events, 258.3 us)
Async XLA Ops:
  7.2 559.3 %all-reduce.7.cloned.1.call-start = ((), (), s32[]{:S(2)}) async-start(), calls=%async_computation | async-start | bytes 294912 | tf_op jit(solution)/shard_map/psum | solution.py:542
  10.5 28.1 %collective-permute-start.3 = (f32[36,192]{1,0:T(8,128)S(1)}, f32[36,192]{1,0:T(8,128)S(1)}, u32[]{:S(2)}, u32[]{:S(2)}) collective-permute-start(f32[36,192]{1,0:T(8,128)S(1)} %pad_maximum_fusion.27), channel_id=1, source_target_pairs={{0,1},{1,0},{2,3},{3,2},{4,5},{5,4},{6,7},{7,6},{8,9},{9,8},{10,11... | collective-permute-start | bytes 82952 | tf_op jit(solution)/shard_map/ppermute | solution.py:35
  14.3 38.5 %collective-permute-start = (bf16[3,768,192]{1,2,0:T(8,128)(2,1)S(1)}, bf16[3,768,192]{1,2,0:T(8,128)(2,1)}, u32[]{:S(2)}, u32[]{:S(2)}) collective-permute-start(bf16[3,768,192]{1,2,0:T(8,128)(2,1)S(1)} %get-tuple-element.183), channel_id=1, source_target_pairs={{0,1},{1,0},{2,3},{3,2},{4,5},{5,4},{6,7},{7,6},{8,9},{9,8},{10,11... | collective-permute-start | bytes 2654216 | tf_op jit(solution)/shard_map/ppermute | solution.py:35
  16.1 60.9 %collective-permute-start.12 = (bf16[768,768]{1,0:T(8,128)(2,1)}, bf16[768,768]{1,0:T(8,128)(2,1)}, u32[]{:S(2)}, u32[]{:S(2)}) collective-permute-start(bf16[768,768]{1,0:T(8,128)(2,1)} %get-tuple-element.180), channel_id=1, source_target_pairs={{0,2},{1,3},{2,0},{3,1},{4,6},{5,7},{6,4},{7,5},{8,10},{9,11},{10,... | collective-permute-start | bytes 3538952 | tf_op jit(solution)/shard_map/ppermute | solution.py:35
  38.6 36.9 %collective-permute-start.7 = (bf16[256,768]{1,0:T(8,128)(2,1)}, bf16[256,768]{1,0:T(8,128)(2,1)}, u32[]{:S(2)}, u32[]{:S(2)}) collective-permute-start(bf16[256,768]{1,0:T(8,128)(2,1)} %slice.345), channel_id=1, source_target_pairs={{1,0},{2,1},{3,2},{4,3},{5,4},{6,5},{7,6},{8,7},{9,8},{10,9},{11,1... | collective-permute-start | bytes 1179656 | tf_op jit(solution)/shard_map/ppermute | solution.py:40
  41.2 35.5 %collective-permute-start.6 = (bf16[272,768]{1,0:T(8,128)(2,1)S(1)}, bf16[272,768]{1,0:T(8,128)(2,1)}, u32[]{:S(2)}, u32[]{:S(2)}) collective-permute-start(bf16[272,768]{1,0:T(8,128)(2,1)S(1)} %slice.344), channel_id=1, source_target_pairs={{0,1},{1,2},{2,3},{3,4},{4,5},{5,6},{6,7},{7,8},{8,9},{9,10},{10,1... | collective-permute-start | bytes 1253384 | tf_op jit(solution)/shard_map/ppermute | solution.py:40
  52.8 53.1 %collective-permute-start.11 = (bf16[768,768]{1,0:T(8,128)(2,1)}, bf16[768,768]{1,0:T(8,128)(2,1)S(1)}, u32[]{:S(2)}, u32[]{:S(2)}) collective-permute-start(bf16[768,768]{1,0:T(8,128)(2,1)} %get-tuple-element.180), channel_id=1, source_target_pairs={{0,1},{1,0},{2,3},{3,2},{4,5},{5,4},{6,7},{7,6},{8,9},{9,8},{10,11... | collective-permute-start | bytes 3538952 | tf_op jit(solution)/shard_map/ppermute | solution.py:35
  74.9 27.8 %collective-permute-start.8 = (bf16[192,768]{1,0:T(8,128)(2,1)S(1)}, bf16[192,768]{1,0:T(8,128)(2,1)S(1)}, u32[]{:S(2)}, u32[]{:S(2)}) collective-permute-start(bf16[192,768]{1,0:T(8,128)(2,1)S(1)} %get-tuple-element.202), channel_id=1, source_target_pairs={{0,1},{1,0},{2,3},{3,2},{4,5},{5,4},{6,7},{7,6},{8,9},{9,8},{10,11... | collective-permute-start | bytes 884744 | tf_op jit(solution)/shard_map/ppermute | solution.py:35
  75.5 30.9 %collective-permute-start.15 = (bf16[768,768]{1,0:T(8,128)(2,1)S(1)}, bf16[768,768]{1,0:T(8,128)(2,1)}, u32[]{:S(2)}, u32[]{:S(2)}) collective-permute-start(bf16[768,768]{1,0:T(8,128)(2,1)S(1)} %copy-done.52), channel_id=1, source_target_pairs={{0,2},{1,3},{2,0},{3,1},{4,6},{5,7},{6,4},{7,5},{8,10},{9,11},{10,... | collective-permute-start | bytes 3538952 | tf_op jit(solution)/shard_map/ppermute | solution.py:35
  76.7 26.4 %collective-permute-start.10 = (bf16[192,768]{1,0:T(8,128)(2,1)S(1)}, bf16[192,768]{1,0:T(8,128)(2,1)S(1)}, u32[]{:S(2)}, u32[]{:S(2)}) collective-permute-start(bf16[192,768]{1,0:T(8,128)(2,1)S(1)} %collective-permute-done.9), channel_id=1, source_target_pairs={{0,1},{1,0},{2,3},{3,2},{4,5},{5,4},{6,7},{7,6},{8,9},{9,8},{10,11... | collective-permute-start | bytes 884744 | tf_op jit(solution)/shard_map/ppermute | solution.py:35
  77.0 30.5 %collective-permute-start.13 = (bf16[768,768]{1,0:T(8,128)(2,1)}, bf16[768,768]{1,0:T(8,128)(2,1)S(1)}, u32[]{:S(2)}, u32[]{:S(2)}) collective-permute-start(bf16[768,768]{1,0:T(8,128)(2,1)} %collective-permute-done.12), channel_id=1, source_target_pairs={{0,1},{1,0},{2,3},{3,2},{4,5},{5,4},{6,7},{7,6},{8,9},{9,8},{10,11... | collective-permute-start | bytes 3538952 | tf_op jit(solution)/shard_map/ppermute | solution.py:35
  105.8 26.7 %collective-permute-start.17 = (bf16[3,768,192]{1,2,0:T(8,128)(2,1)S(1)}, bf16[3,768,192]{1,2,0:T(8,128)(2,1)S(1)}, u32[]{:S(2)}, u32[]{:S(2)}) collective-permute-start(bf16[3,768,192]{1,2,0:T(8,128)(2,1)S(1)} %get-tuple-element.182), channel_id=1, source_target_pairs={{0,1},{1,0},{2,3},{3,2},{4,5},{5,4},{6,7},{7,6},{8,9},{9,8},{10,11... | collective-permute-start | bytes 2654216 | tf_op jit(solution)/shard_map/ppermute | solution.py:35
  106.3 53.5 %collective-permute-start.26 = (bf16[768,768]{1,0:T(8,128)(2,1)S(1)}, bf16[768,768]{1,0:T(8,128)(2,1)}, u32[]{:S(2)}, u32[]{:S(2)}) collective-permute-start(bf16[768,768]{1,0:T(8,128)(2,1)S(1)} %copy-done.54), channel_id=1, source_target_pairs={{0,2},{1,3},{2,0},{3,1},{4,6},{5,7},{6,4},{7,5},{8,10},{9,11},{10,... | collective-permute-start | bytes 3538952 | tf_op jit(solution)/shard_map/ppermute | solution.py:35
  124.1 34.1 %collective-permute-start.23 = (bf16[192,768]{1,0:T(8,128)(2,1)S(1)}, bf16[192,768]{1,0:T(8,128)(2,1)S(1)}, u32[]{:S(2)}, u32[]{:S(2)}) collective-permute-start(bf16[192,768]{1,0:T(8,128)(2,1)S(1)} %copy-done.63), channel_id=1, source_target_pairs={{0,2},{1,3},{2,0},{3,1},{4,6},{5,7},{6,4},{7,5},{8,10},{9,11},{10,... | collective-permute-start | bytes 884744 | tf_op jit(solution)/shard_map/ppermute | solution.py:35
  124.4 87.6 %collective-permute-start.29 = (bf16[768,768]{1,0:T(8,128)(2,1)}, bf16[768,768]{1,0:T(8,128)(2,1)}, u32[]{:S(2)}, u32[]{:S(2)}) collective-permute-start(bf16[768,768]{1,0:T(8,128)(2,1)} %get-tuple-element.178), channel_id=1, source_target_pairs={{0,2},{1,3},{2,0},{3,1},{4,6},{5,7},{6,4},{7,5},{8,10},{9,11},{10,... | collective-permute-start | bytes 3538952 | tf_op jit(solution)/shard_map/ppermute | solution.py:35
  132.5 27.3 %collective-permute-start.21 = (bf16[256,768]{1,0:T(8,128)(2,1)S(1)}, bf16[256,768]{1,0:T(8,128)(2,1)S(1)}, u32[]{:S(2)}, u32[]{:S(2)}) collective-permute-start(bf16[256,768]{1,0:T(8,128)(2,1)S(1)} %slice.443), channel_id=1, source_target_pairs={{1,0},{2,1},{3,2},{4,3},{5,4},{6,5},{7,6},{8,7},{9,8},{10,9},{11,1... | collective-permute-start | bytes 1179656 | tf_op jit(solution)/shard_map/ppermute | solution.py:40
  134.9 53.9 %collective-permute-start.20 = (bf16[272,768]{1,0:T(8,128)(2,1)S(1)}, bf16[272,768]{1,0:T(8,128)(2,1)S(1)}, u32[]{:S(2)}, u32[]{:S(2)}) collective-permute-start(bf16[272,768]{1,0:T(8,128)(2,1)S(1)} %slice.442), channel_id=1, source_target_pairs={{0,1},{1,2},{2,3},{3,4},{4,5},{5,6},{6,7},{7,8},{8,9},{9,10},{10,1... | collective-permute-start | bytes 1253384 | tf_op jit(solution)/shard_map/ppermute | solution.py:40
  158.3 56.9 %collective-permute-start.25 = (bf16[768,768]{1,0:T(8,128)(2,1)S(1)}, bf16[768,768]{1,0:T(8,128)(2,1)S(1)}, u32[]{:S(2)}, u32[]{:S(2)}) collective-permute-start(bf16[768,768]{1,0:T(8,128)(2,1)S(1)} %copy-done.54), channel_id=1, source_target_pairs={{0,1},{1,0},{2,3},{3,2},{4,5},{5,4},{6,7},{7,6},{8,9},{9,8},{10,11... | collective-permute-start | bytes 3538952 | tf_op jit(solution)/shard_map/ppermute | solution.py:35
  159.8 52.1 %collective-permute-start.22 = (bf16[192,768]{1,0:T(8,128)(2,1)S(1)}, bf16[192,768]{1,0:T(8,128)(2,1)S(1)}, u32[]{:S(2)}, u32[]{:S(2)}) collective-permute-start(bf16[192,768]{1,0:T(8,128)(2,1)S(1)} %copy-done.63), channel_id=1, source_target_pairs={{0,1},{1,0},{2,3},{3,2},{4,5},{5,4},{6,7},{7,6},{8,9},{9,8},{10,11... | collective-permute-start | bytes 884744 | tf_op jit(solution)/shard_map/ppermute | solution.py:35
  159.8 52.7 %collective-permute-start.24 = (bf16[192,768]{1,0:T(8,128)(2,1)S(1)}, bf16[192,768]{1,0:T(8,128)(2,1)S(1)}, u32[]{:S(2)}, u32[]{:S(2)}) collective-permute-start(bf16[192,768]{1,0:T(8,128)(2,1)S(1)} %collective-permute-done.23), channel_id=1, source_target_pairs={{0,1},{1,0},{2,3},{3,2},{4,5},{5,4},{6,7},{7,6},{8,9},{9,8},{10,11... | collective-permute-start | bytes 884744 | tf_op jit(solution)/shard_map/ppermute | solution.py:35
  188.7 26.5 %collective-permute-start.27 = (bf16[768,768]{1,0:T(8,128)(2,1)}, bf16[768,768]{1,0:T(8,128)(2,1)}, u32[]{:S(2)}, u32[]{:S(2)}) collective-permute-start(bf16[768,768]{1,0:T(8,128)(2,1)} %collective-permute-done.26), channel_id=1, source_target_pairs={{0,1},{1,0},{2,3},{3,2},{4,5},{5,4},{6,7},{7,6},{8,9},{9,8},{10,11... | collective-permute-start | bytes 3538952 | tf_op jit(solution)/shard_map/ppermute | solution.py:35
  307.7 34.2 %collective-permute-start.32 = (bf16[256,768]{1,0:T(8,128)(2,1)S(1)}, bf16[256,768]{1,0:T(8,128)(2,1)S(1)}, u32[]{:S(2)}, u32[]{:S(2)}) collective-permute-start(bf16[256,768]{1,0:T(8,128)(2,1)S(1)} %slice.450), channel_id=1, source_target_pairs={{0,1},{1,2},{2,3},{3,4},{4,5},{5,6},{6,7},{7,8},{8,9},{9,10},{10,1... | collective-permute-start | bytes 1179656 | tf_op jit(solution)/shard_map/ppermute | solution.py:40
  310.7 31.2 %collective-permute-start.31 = (bf16[272,768]{1,0:T(8,128)(2,1)}, bf16[272,768]{1,0:T(8,128)(2,1)}, u32[]{:S(2)}, u32[]{:S(2)}) collective-permute-start(bf16[272,768]{1,0:T(8,128)(2,1)} %slice.449), channel_id=1, source_target_pairs={{1,0},{2,1},{3,2},{4,3},{5,4},{6,5},{7,6},{8,7},{9,8},{10,9},{11,1... | collective-permute-start | bytes 1253384 | tf_op jit(solution)/shard_map/ppermute | solution.py:40
  319.4 141.8 %collective-permute-start.43 = (bf16[2,768,768]{2,1,0:T(8,128)(2,1)}, bf16[2,768,768]{2,1,0:T(8,128)(2,1)}, u32[]{:S(2)}, u32[]{:S(2)}) collective-permute-start(bf16[2,768,768]{2,1,0:T(8,128)(2,1)} %pad_maximum_fusion.9), channel_id=1, source_target_pairs={{0,1},{1,0},{2,3},{3,2},{4,5},{5,4},{6,7},{7,6},{8,9},{9,8},{10,11... | collective-permute-start | bytes 7077896 | tf_op jit(solution)/shard_map/ppermute | solution.py:35
  331.7 135.1 %collective-permute-start.59 = (bf16[2,1536,768]{2,1,0:T(8,128)(2,1)}, bf16[2,1536,768]{2,1,0:T(8,128)(2,1)}, u32[]{:S(2)}, u32[]{:S(2)}) collective-permute-start(bf16[2,1536,768]{2,1,0:T(8,128)(2,1)} %pad_maximum_fusion.5), channel_id=1, source_target_pairs={{0,1},{1,0},{2,3},{3,2},{4,5},{5,4},{6,7},{7,6},{8,9},{9,8},{10,11... | collective-permute-start | bytes 14155784 | tf_op jit(solution)/shard_map/ppermute | solution.py:35
  412.1 342.9 %collective-permute-start.34 = (bf16[256,768]{1,0:T(8,128)(2,1)}, bf16[256,768]{1,0:T(8,128)(2,1)}, u32[]{:S(2)}, u32[]{:S(2)}) collective-permute-start(bf16[256,768]{1,0:T(8,128)(2,1)} %slice.453), channel_id=1, source_target_pairs={{0,1},{1,2},{2,3},{3,4},{4,5},{5,6},{6,7},{7,8},{8,9},{9,10},{10,1... | collective-permute-start | bytes 1179656 | tf_op jit(solution)/shard_map/ppermute | solution.py:40
  424.7 55.7 %collective-permute-start.51 = (bf16[2,1536,768]{2,1,0:T(8,128)(2,1)}, bf16[2,1536,768]{2,1,0:T(8,128)(2,1)}, u32[]{:S(2)}, u32[]{:S(2)}) collective-permute-start(bf16[2,1536,768]{2,1,0:T(8,128)(2,1)} %pad_maximum_fusion.4), channel_id=1, source_target_pairs={{0,1},{1,0},{2,3},{3,2},{4,5},{5,4},{6,7},{7,6},{8,9},{9,8},{10,11... | collective-permute-start | bytes 14155784 | tf_op jit(solution)/shard_map/ppermute | solution.py:35
  434.5 30.3 %collective-permute-start.35 = (bf16[2,768,768]{2,1,0:T(8,128)(2,1)}, bf16[2,768,768]{2,1,0:T(8,128)(2,1)}, u32[]{:S(2)}, u32[]{:S(2)}) collective-permute-start(bf16[2,768,768]{2,1,0:T(8,128)(2,1)} %pad_maximum_fusion.8), channel_id=1, source_target_pairs={{0,1},{1,0},{2,3},{3,2},{4,5},{5,4},{6,7},{7,6},{8,9},{9,8},{10,11... | collective-permute-start | bytes 7077896 | tf_op jit(solution)/shard_map/ppermute | solution.py:35
  464.8 28.0 %collective-permute-start.44 = (bf16[768,768]{1,0:T(8,128)(2,1)}, bf16[768,768]{1,0:T(8,128)(2,1)}, u32[]{:S(2)}, u32[]{:S(2)}) collective-permute-start(bf16[768,768]{1,0:T(8,128)(2,1)} %fusion.23), channel_id=1, source_target_pairs={{0,2},{1,3},{2,0},{3,1},{4,6},{5,7},{6,4},{7,5},{8,10},{9,11},{10,... | collective-permute-start | bytes 3538952 | tf_op jit(solution)/shard_map/ppermute | solution.py:35
  476.0 100.3 %collective-permute-start.60 = (bf16[1536,768]{1,0:T(8,128)(2,1)}, bf16[1536,768]{1,0:T(8,128)(2,1)}, u32[]{:S(2)}, u32[]{:S(2)}) collective-permute-start(bf16[1536,768]{1,0:T(8,128)(2,1)} %fusion.15), channel_id=1, source_target_pairs={{0,2},{1,3},{2,0},{3,1},{4,6},{5,7},{6,4},{7,5},{8,10},{9,11},{10,... | collective-permute-start | bytes 7077896 | tf_op jit(solution)/shard_map/ppermute | solution.py:35
  480.4 89.0 %collective-permute-start.36 = (bf16[768,768]{1,0:T(8,128)(2,1)}, bf16[768,768]{1,0:T(8,128)(2,1)}, u32[]{:S(2)}, u32[]{:S(2)}) collective-permute-start(bf16[768,768]{1,0:T(8,128)(2,1)} %fusion.27), channel_id=1, source_target_pairs={{0,2},{1,3},{2,0},{3,1},{4,6},{5,7},{6,4},{7,5},{8,10},{9,11},{10,... | collective-permute-start | bytes 3538952 | tf_op jit(solution)/shard_map/ppermute | solution.py:35
  488.4 131.6 %collective-permute-start.52 = (bf16[1536,768]{1,0:T(8,128)(2,1)}, bf16[1536,768]{1,0:T(8,128)(2,1)}, u32[]{:S(2)}, u32[]{:S(2)}) collective-permute-start(bf16[1536,768]{1,0:T(8,128)(2,1)} %fusion.19), channel_id=1, source_target_pairs={{0,2},{1,3},{2,0},{3,1},{4,6},{5,7},{6,4},{7,5},{8,10},{9,11},{10,... | collective-permute-start | bytes 7077896 | tf_op jit(solution)/shard_map/ppermute | solution.py:35
  497.0 76.0 %collective-permute-start.45 = (bf16[384,768]{1,0:T(8,128)(2,1)}, bf16[384,768]{1,0:T(8,128)(2,1)}, u32[]{:S(2)}, u32[]{:S(2)}) collective-permute-start(bf16[384,768]{1,0:T(8,128)(2,1)} %dynamic-slice_convert_fusion.4), channel_id=1, source_target_pairs={{0,4},{4,0},{8,12},{12,8},{16,20},{20,16},{24,28},{28,24},{1,5},{5... | collective-permute-start | bytes 1769480 | tf_op jit(solution)/shard_map/ppermute | solution.py:35
  572.9 54.6 %collective-permute-start.37 = (bf16[384,768]{1,0:T(8,128)(2,1)}, bf16[384,768]{1,0:T(8,128)(2,1)}, u32[]{:S(2)}, u32[]{:S(2)}) collective-permute-start(bf16[384,768]{1,0:T(8,128)(2,1)} %dynamic-slice_convert_fusion.5), channel_id=1, source_target_pairs={{0,4},{4,0},{8,12},{12,8},{16,20},{20,16},{24,28},{28,24},{1,5},{5... | collective-permute-start | bytes 1769480 | tf_op jit(solution)/shard_map/ppermute | solution.py:35
  575.4 49.0 %collective-permute-start.46 = (bf16[192,768]{1,0:T(8,128)(2,1)S(1)}, bf16[192,768]{1,0:T(8,128)(2,1)}, u32[]{:S(2)}, u32[]{:S(2)}) collective-permute-start(bf16[192,768]{1,0:T(8,128)(2,1)S(1)} %dynamic-slice_convert_fusion.8), channel_id=1, source_target_pairs={{0,8},{4,12},{8,0},{12,4},{16,24},{20,28},{24,16},{28,20},{1,9},{5... | collective-permute-start | bytes 884744 | tf_op jit(solution)/shard_map/ppermute | solution.py:35
  581.8 55.1 %collective-permute-start.61 = (bf16[768,768]{1,0:T(8,128)(2,1)}, bf16[768,768]{1,0:T(8,128)(2,1)}, u32[]{:S(2)}, u32[]{:S(2)}) collective-permute-start(bf16[768,768]{1,0:T(8,128)(2,1)} %dynamic-slice_convert_fusion), channel_id=1, source_target_pairs={{0,4},{4,0},{8,12},{12,8},{16,20},{20,16},{24,28},{28,24},{1,5},{5... | collective-permute-start | bytes 3538952 | tf_op jit(solution)/shard_map/ppermute | solution.py:35
  624.3 26.7 %collective-permute-start.53 = (bf16[768,768]{1,0:T(8,128)(2,1)S(1)}, bf16[768,768]{1,0:T(8,128)(2,1)S(1)}, u32[]{:S(2)}, u32[]{:S(2)}) collective-permute-start(bf16[768,768]{1,0:T(8,128)(2,1)S(1)} %dynamic-slice_convert_fusion.1), channel_id=1, source_target_pairs={{0,4},{4,0},{8,12},{12,8},{16,20},{20,16},{24,28},{28,24},{1,5},{5... | collective-permute-start | bytes 3538952 | tf_op jit(solution)/shard_map/ppermute | solution.py:35
  633.6 69.7 %collective-permute-start.48 = (bf16[96,768]{1,0:T(8,128)(2,1)S(1)}, bf16[96,768]{1,0:T(8,128)(2,1)S(1)}, u32[]{:S(2)}, u32[]{:S(2)}) collective-permute-start(bf16[96,768]{1,0:T(8,128)(2,1)S(1)} %add_convert_fusion.6), channel_id=1, source_target_pairs={{0,16},{4,20},{8,24},{12,28},{16,0},{20,4},{24,8},{28,12},{1,17},{... | collective-permute-start | bytes 442376 | tf_op jit(solution)/shard_map/ppermute | solution.py:35
  651.7 26.6 %collective-permute-start.39 = (bf16[96,768]{1,0:T(8,128)(2,1)S(1)}, bf16[96,768]{1,0:T(8,128)(2,1)S(1)}, u32[]{:S(2)}, u32[]{:S(2)}) collective-permute-start(bf16[96,768]{1,0:T(8,128)(2,1)S(1)} %dynamic-slice_convert_fusion.11), channel_id=1, source_target_pairs={{0,16},{4,20},{8,24},{12,28},{16,0},{20,4},{24,8},{28,12},{1,17},{... | collective-permute-start | bytes 442376 | tf_op jit(solution)/shard_map/ppermute | solution.py:35
  678.3 25.1 %collective-permute-start.40 = (bf16[96,768]{1,0:T(8,128)(2,1)S(1)}, bf16[96,768]{1,0:T(8,128)(2,1)S(1)}, u32[]{:S(2)}, u32[]{:S(2)}) collective-permute-start(bf16[96,768]{1,0:T(8,128)(2,1)S(1)} %add_convert_fusion.7), channel_id=1, source_target_pairs={{0,16},{4,20},{8,24},{12,28},{16,0},{20,4},{24,8},{28,12},{1,17},{... | collective-permute-start | bytes 442376 | tf_op jit(solution)/shard_map/ppermute | solution.py:35
  678.5 37.4 %collective-permute-start.64 = (bf16[192,768]{1,0:T(8,128)(2,1)S(1)}, bf16[192,768]{1,0:T(8,128)(2,1)S(1)}, u32[]{:S(2)}, u32[]{:S(2)}) collective-permute-start(bf16[192,768]{1,0:T(8,128)(2,1)S(1)} %add_convert_fusion.4), channel_id=1, source_target_pairs={{0,16},{4,20},{8,24},{12,28},{16,0},{20,4},{24,8},{28,12},{1,17},{... | collective-permute-start | bytes 884744 | tf_op jit(solution)/shard_map/ppermute | solution.py:35
  703.3 28.2 %collective-permute-start.49 = (bf16[192,768]{1,0:T(8,128)(2,1)S(1)}, bf16[192,768]{1,0:T(8,128)(2,1)}, u32[]{:S(2)}, u32[]{:S(2)}) collective-permute-start(bf16[192,768]{1,0:T(8,128)(2,1)S(1)} %maximum_select_fusion.11), channel_id=1, source_target_pairs={{0,8},{4,12},{8,0},{12,4},{16,24},{20,28},{24,16},{28,20},{1,9},{5... | collective-permute-start | bytes 884744 | tf_op jit(solution)/shard_map/ppermute | solution.py:35
  703.5 32.4 %collective-permute-start.41 = (bf16[192,768]{1,0:T(8,128)(2,1)S(1)}, bf16[192,768]{1,0:T(8,128)(2,1)}, u32[]{:S(2)}, u32[]{:S(2)}) collective-permute-start(bf16[192,768]{1,0:T(8,128)(2,1)S(1)} %maximum_select_fusion.10), channel_id=1, source_target_pairs={{0,8},{4,12},{8,0},{12,4},{16,24},{20,28},{24,16},{28,20},{1,9},{5... | collective-permute-start | bytes 884744 | tf_op jit(solution)/shard_map/ppermute | solution.py:35
  716.1 25.8 %collective-permute-start.65 = (bf16[384,768]{1,0:T(8,128)(2,1)S(1)}, bf16[384,768]{1,0:T(8,128)(2,1)S(1)}, u32[]{:S(2)}, u32[]{:S(2)}) collective-permute-start(bf16[384,768]{1,0:T(8,128)(2,1)S(1)} %maximum_select_fusion.9), channel_id=1, source_target_pairs={{0,8},{4,12},{8,0},{12,4},{16,24},{20,28},{24,16},{28,20},{1,9},{5... | collective-permute-start | bytes 1769480 | tf_op jit(solution)/shard_map/ppermute | solution.py:35
  722.4 32.1 %collective-permute-start.57 = (bf16[384,768]{1,0:T(8,128)(2,1)S(1)}, bf16[384,768]{1,0:T(8,128)(2,1)S(1)}, u32[]{:S(2)}, u32[]{:S(2)}) collective-permute-start(bf16[384,768]{1,0:T(8,128)(2,1)S(1)} %maximum_select_fusion.8), channel_id=1, source_target_pairs={{0,8},{4,12},{8,0},{12,4},{16,24},{20,28},{24,16},{28,20},{1,9},{5... | collective-permute-start | bytes 1769480 | tf_op jit(solution)/shard_map/ppermute | solution.py:35
  741.9 26.4 %collective-permute-start.42 = (bf16[384,768]{1,0:T(8,128)(2,1)S(1)}, bf16[384,768]{1,0:T(8,128)(2,1)S(1)}, u32[]{:S(2)}, u32[]{:S(2)}) collective-permute-start(bf16[384,768]{1,0:T(8,128)(2,1)S(1)} %maximum_select_fusion.6), channel_id=1, source_target_pairs={{0,4},{4,0},{8,12},{12,8},{16,20},{20,16},{24,28},{28,24},{1,5},{5... | collective-permute-start | bytes 1769480 | tf_op jit(solution)/shard_map/ppermute | solution.py:35
  754.5 39.0 %collective-permute-start.66 = (bf16[768,768]{1,0:T(8,128)(2,1)S(1)}, bf16[768,768]{1,0:T(8,128)(2,1)S(1)}, u32[]{:S(2)}, u32[]{:S(2)}) collective-permute-start(bf16[768,768]{1,0:T(8,128)(2,1)S(1)} %maximum_select_fusion.5), channel_id=1, source_target_pairs={{0,4},{4,0},{8,12},{12,8},{16,20},{20,16},{24,28},{28,24},{1,5},{5... | collective-permute-start | bytes 3538952 | tf_op jit(solution)/shard_map/ppermute | solution.py:35
  755.0 63.8 %collective-permute-start.58 = (bf16[768,768]{1,0:T(8,128)(2,1)S(1)}, bf16[768,768]{1,0:T(8,128)(2,1)S(1)}, u32[]{:S(2)}, u32[]{:S(2)}) collective-permute-start(bf16[768,768]{1,0:T(8,128)(2,1)S(1)} %maximum_select_fusion.4), channel_id=1, source_target_pairs={{0,4},{4,0},{8,12},{12,8},{16,20},{20,16},{24,28},{28,24},{1,5},{5... | collective-permute-start | bytes 3538952 | tf_op jit(solution)/shard_map/ppermute | solution.py:35
  (156 other events, 2101.4 us)
Sparse Core Ops, SparseCore 0:
  446.7 119.7 all-reduce.6

commit v2 on v1

--- a/solution.py
+++ b/solution.py
@@ -1,3 +1,5 @@
+import functools
+
 import jax
 import jax.numpy as jnp
 from jax import lax
@@ -355,37 +357,202 @@
     return result, saved
 
 
-def split_rows(values):
-    return jnp.split(values, 4, axis=0)
+CHUNK = 256
+LAG = 2
+
+
+def partner(seq=None, mp=None):
+    return {"seq": lax.axis_index("seq") if seq is None else seq,
+            "mp": lax.axis_index("mp") if mp is None else mp}
+
+
+def peers_of(place, seat, group):
+    low, high = place % 2, place // 2
+    others = [partner(seq=((high + step) % group) * 2 + low) for step in range(1, group)]
+    return (
+        partner(mp=seat + 1 - 2 * (seat % 2)),
+        partner(mp=(seat + 2) % 4),
+        partner(seq=place + 1 - 2 * low),
+        others,
+    )
+
+
+def reduce_kernel(
+    group, count, parts_ref, out_ref,
+    own_v, core_v, across_v, cross_v, first_v, give_v, half_v, keep_v, piece_v, slab_v, sum_v, done_v,
+    local_sem, core_send, core_recv, x_send, x_recv, y_send, y_recv, z_send, z_recv,
+    g_send, g_recv, f_send, f_recv, f_local,
+):
+    place, seat = lax.axis_index("seq"), lax.axis_index("mp")
+    low, high = place % 2, place // 2
+    core, across, beside, others = peers_of(place, seat, group)
+    rows = CHUNK // group
+    width = parts_ref.shape[-1]
+    half = width // 2
+    barrier = pltpu.get_barrier_semaphore()
+    for device in [core, across, beside] + others:
+        pl.semaphore_signal(barrier, inc=1, device_id=device, device_id_type=pl.DeviceIdType.MESH)
+    pl.semaphore_wait(barrier, 3 + len(others))
+
+    def remote(source, target, send, recv, device):
+        return pltpu.make_async_remote_copy(
+            src_ref=source, dst_ref=target, send_sem=send, recv_sem=recv,
+            device_id=device, device_id_type=pl.DeviceIdType.MESH,
+        )
+
+    def local_copy(c):
+        return pltpu.make_async_copy(parts_ref.at[c, pl.ds(0, 2)], own_v.at[c % 2], local_sem.at[c % 2])
+
+    def core_copy(c):
+        return remote(parts_ref.at[c, pl.ds(2, 2)], core_v.at[c], core_send.at[c], core_recv.at[c], core)
+
+    def x_copy(c):
+        return remote(across_v.at[c % 4], cross_v.at[c], x_send.at[c], x_recv.at[c], across)
+
+    def y_copy(c):
+        return remote(give_v.at[c % 4], half_v.at[c], y_send.at[c], y_recv.at[c], beside)
+
+    def z_copy(c, step):
+        to = (high + step) % group
+        return remote(
+            slab_v.at[c % 4, pl.ds(pl.multiple_of(to * rows, rows), rows)],
+            piece_v.at[c, step - 1],
+            z_send.at[c, step - 1], z_recv.at[c, step - 1], others[step - 1],
+        )
+
+    def own_rows():
+        return pl.ds(pl.multiple_of(high * rows, rows), rows)
+
+    def g_copy(c, step):
+        mine = done_v.at[c, own_rows()]
+        return remote(mine, mine, g_send.at[c, step - 1], g_recv.at[c, step - 1], others[step - 1])
+
+    def lanes():
+        return pl.ds(pl.multiple_of(low * half, 128), half)
+
+    def f_copy(c):
+        return remote(done_v.at[c], out_ref.at[c, :, lanes()], f_send.at[c], f_recv.at[c], beside)
+
+    def f_own(c):
+        return pltpu.make_async_copy(done_v.at[c], out_ref.at[c, :, lanes()], f_local.at[c])
+
+    def step_zero(c):
+        local_copy(c).start()
+        core_copy(c).start()
+
+    def step_core(c):
+        local_copy(c).wait()
+        core_copy(c).wait()
+        first_v[c % 4] = own_v[c % 2, 0].astype(F32) + core_v[c, 0].astype(F32)
+        across_v[c % 4] = (own_v[c % 2, 1].astype(F32) + core_v[c, 1].astype(F32)).astype(BF16)
+        x_copy(c).start()
+
+    def step_x(c):
+        x_copy(c).wait()
+        total = first_v[c % 4] + cross_v[c].astype(F32)
+        left, right = total[:, :half], total[:, half:]
+        keep_v[c % 4] = jnp.where(low == 0, left, right)
+        give_v[c % 4] = jnp.where(low == 0, right, left).astype(BF16)
+        y_copy(c).start()
+
+    def step_y(c):
+        y_copy(c).wait()
+        total = keep_v[c % 4] + half_v[c].astype(F32)
+        sum_v[c % 4] = total
+        slab_v[c % 4] = total.astype(BF16)
+        for step in range(1, group):
+            z_copy(c, step).start()
+
+    def step_z(c):
+        total = sum_v[c % 4, own_rows(), :]
+        for step in range(1, group):
+            z_copy(c, step).wait()
+            total = total + piece_v[c, step - 1].astype(F32)
+        done_v[c, own_rows(), :] = total.astype(BF16)
+        for step in range(1, group):
+            g_copy(c, step).start()
+
+    def step_gather(c):
+        for step in range(1, group):
+            g_copy(c, step).wait()
+        f_copy(c).start()
+        f_own(c).start()
+
+    def step_end(c):
+        local = f_own(c)
+        local.wait()
+        f_copy(c).wait()
+
+    stages = [(step_zero, 0), (step_core, 1)]
+    for k, stage in enumerate((step_x, step_y, step_z, step_gather, step_end)):
+        stages.append((stage, 1 + LAG * (k + 1)))
+    last = stages[-1][1]
+
+    @pl.loop(0, count + last)
+    def _(slot):
+        for stage, delay in stages:
+            at = slot - delay
+
+            @pl.when((at >= 0) & (at < count))
+            def _():
+                stage(at)
 
 
 def reduce_parts(parts):
-    sent = jnp.stack([parts[1], parts[3]]).astype(BF16)
-    received = swap(sent, "mp", 1).astype(F32)
-    own = parts[0] + received[0]
-    across = parts[2] + received[1]
-    own = own + swap(across.astype(BF16), "mp", 2).astype(F32)
-    place = lax.axis_index("seq")
-    count = lax.axis_size("seq")
-    bit = 1
-    while bit < count:
-        half = own.shape[0] // 2
-        side = (place // bit) % 2
-        kept = lax.dynamic_slice_in_dim(own, side * half, half, 0)
-        given = lax.dynamic_slice_in_dim(own, (1 - side) * half, half, 0).astype(BF16)
-        own = kept + swap(given, "seq", bit).astype(F32)
-        bit *= 2
-    whole = own.astype(BF16)
-    while bit > 1:
-        bit //= 2
-        side = (place // bit) % 2
-        other = swap(whole, "seq", bit)
-        whole = jnp.where(
-            side == 0,
-            jnp.concatenate([whole, other], axis=0),
-            jnp.concatenate([other, whole], axis=0),
-        )
-    return whole
+    count, _, rows, width = parts.shape
+    group = lax.axis_size("seq") // 2
+    half = width // 2
+    piece = rows // group
+    vmem, dma = pltpu.VMEM, pltpu.SemaphoreType.DMA
+    return pl.pallas_call(
+        functools.partial(reduce_kernel, group, count),
+        out_shape=jax.ShapeDtypeStruct((count, rows, width), BF16),
+        in_specs=[pl.BlockSpec(memory_space=pl.ANY)],
+        out_specs=pl.BlockSpec(memory_space=pl.ANY),
+        scratch_shapes=[
+            vmem((2, 2, rows, width), BF16),
+            vmem((count, 2, rows, width), BF16),
+            vmem((4, rows, width), BF16),
+            vmem((count, rows, width), BF16),
+            vmem((4, rows, width), F32),
+            vmem((4, rows, half), BF16),
+            vmem((count, rows, half), BF16),
+            vmem((4, rows, half), F32),
+            vmem((count, group - 1, piece, half), BF16),
+            vmem((4, rows, half), BF16),
+            vmem((4, rows, half), F32),
+            vmem((count, rows, half), BF16),
+            dma((2,)),
+            dma((count,)),
+            dma((count,)),
+            dma((count,)),
+            dma((count,)),
+            dma((count,)),
+            dma((count,)),
+            dma((count, group - 1)),
+            dma((count, group - 1)),
+            dma((count, group - 1)),
+            dma((count, group - 1)),
+            dma((count,)),
+            dma((count,)),
+            dma((count,)),
+        ],
+        compiler_params=pltpu.CompilerParams(
+            collective_id=0, has_side_effects=True, vmem_limit_bytes=VMEM_LIMIT
+        ),
+        name="reduce_parts",
+    )(parts)
+
+
+ORDER = (0, 2, 1, 3)
+
+
+def layer_parts(down, up_t, *rest):
+    rows = CHUNK // 4
+    big = [piece.astype(BF16).reshape(4, 3, CHUNK, -1) for piece in (down, up_t)]
+    small = [piece.astype(BF16).reshape(4, 3, rows, piece.shape[1]) for piece in rest]
+    joined = jnp.concatenate(big + [jnp.concatenate(small, axis=2)], axis=1)
+    return jnp.stack([joined[k] for k in ORDER], axis=1)
 
 
 def layer_backward(grad_out, masks, weights, saved):
@@ -417,11 +584,6 @@
     grad_b_up = jnp.sum(grad_pre, axis=0)
     grad_pre_low = grad_pre.astype(BF16)
     grad_w_up_t = product_left_t(grad_pre_low, normed_low)
-    feed_parts = [
-        jnp.concatenate(pair, axis=0)
-        for pair in zip(split_rows(grad_w_down), split_rows(grad_w_up_t))
-    ]
-    feed = reduce_parts(feed_parts)
     grad_normed = product_right_t(grad_pre_low, up) + grad_middle
     grad_resid, gain_one, shift_one = norm_backward(grad_normed, unit_one, inverse_one, gains[0])
     bias_out = jnp.sum(grad_resid, axis=0)
@@ -435,11 +597,7 @@
     w_q = product_left_t(grad_q_low, entry)
     w_k = product_left_t(grad_k_low, entry_wide)
     w_v = product_left_t(grad_v_low, entry_wide)
-    rest_parts = [
-        jnp.concatenate(pieces, axis=0)
-        for pieces in zip(*(split_rows(piece) for piece in (grad_w_out, w_q, w_k, w_v)))
-    ]
-    rest = reduce_parts(rest_parts)
+    parts = layer_parts(grad_w_down, grad_w_up_t, grad_w_out, w_q, w_k, w_v)
     wide_grad = product_right_t(grad_k_low, qkv[1]) + product_right_t(grad_v_low, qkv[2])
     from_right = shift(wide_grad[LEFT - LEFT_SENT : LEFT].astype(BF16), -1).astype(F32)
     from_left = shift(wide_grad[LEFT + total :].astype(BF16), 1).astype(F32)
@@ -453,17 +611,7 @@
     grad_b_up_rows = grad_b_up.reshape(4, -1, width // 4).transpose(1, 0, 2).reshape(-1, width)
     small_split = jnp.concatenate([small[:14], grad_b_up_rows], axis=0)
     small_whole = jnp.stack([gain_one, gain_two, bias_out, shift_one, bias_down, shift_two])
-    return grad_hidden, feed, rest, small_split, small_whole
-
-
-def to_absolute(rows):
-    quarter = rows.shape[1] // 4
-    parts = [rows[:, k * quarter : (k + 1) * quarter] for k in range(4)]
-    place = lax.axis_index("mp")
-    odd, high = place % 2 == 1, place // 2 == 1
-    parts = [jnp.where(odd, parts[k ^ 1], parts[k]) for k in range(4)]
-    parts = [jnp.where(high, parts[k ^ 2], parts[k]) for k in range(4)]
-    return jnp.concatenate(parts, axis=1)
+    return grad_hidden, parts, small_split, small_whole
 
 
 def shards(
@@ -533,28 +681,47 @@
     collected = [None] * LAYERS
     for index in reversed(range(LAYERS)):
         weights, saved = stack[index]
-        gradient, feed, rest, split, whole = layer_backward(gradient, masks, weights, saved)
-        collected[index] = (feed, rest, split, whole)
-    feed = jnp.stack([part[0] for part in collected]).astype(F32)
-    rest = jnp.stack([part[1] for part in collected]).astype(F32)
-    small_split = jnp.stack([to_absolute(part[2]) for part in collected])
-    small_whole = jnp.stack([part[3] for part in collected])
-    small_total = lax.psum(jnp.concatenate([small_split, small_whole], axis=1), BOTH)
-    own_small = lax.dynamic_slice_in_dim(small_total[:, :18], place * quarter, quarter, 2)
+        gradient, parts, split, whole = layer_backward(gradient, masks, weights, saved)
+        collected[index] = (parts, split, whole)
+    split = jnp.concatenate([part[1] for part in collected], axis=0).astype(BF16)
+    whole = jnp.concatenate([part[2] for part in collected], axis=0).astype(BF16)
+    extra = []
+    for part in ORDER:
+        own_split = jnp.pad(
+            split[:, part * quarter : (part + 1) * quarter],
+            ((0, 64 - split.shape[0]), (0, width - quarter)),
+        )
+        extra.append(
+            jnp.pad(
+                jnp.concatenate([own_split, whole], axis=0),
+                ((0, CHUNK - 64 - whole.shape[0]), (0, 0)),
+            )
+        )
+    total_parts = jnp.concatenate(
+        [collected[1][0], collected[0][0], jnp.stack(extra)[None]], axis=0
+    )
+    sums = reduce_parts(total_parts).astype(F32)
+    per_layer = sums[:18].reshape(2, 3, 3, 4, CHUNK // 4, width)
+    per_layer = jnp.stack([per_layer[1], per_layer[0]])
     units = down_weight.shape[1]
+    grad_down = per_layer[:, 0].reshape(2, units, width)
+    grad_up = per_layer[:, 1].reshape(2, units, width).transpose(0, 2, 1)
+    rest = per_layer[:, 2].transpose(0, 2, 1, 3, 4).reshape(2, 4, quarter, width)
+    small_split = sums[18, :36, :quarter].reshape(2, 18, quarter)
+    small_whole = sums[18, 64:76].reshape(2, 6, width)
     return (
         hidden,
         gradient,
-        rest[:, quarter:].reshape(2, 3, quarter, width).transpose(0, 1, 3, 2),
-        own_small[:, :2],
-        own_small[:, 2:12].reshape(2, 2, 5, quarter),
-        own_small[:, 12:14],
-        rest[:, :quarter],
-        feed[:, units:].transpose(0, 2, 1),
-        own_small[:, 14:18].reshape(2, -1),
-        feed[:, :units],
-        small_total[:, 18:20],
-        small_total[:, 20:24],
+        rest[:, 1:].transpose(0, 1, 3, 2),
+        small_split[:, :2],
+        small_split[:, 2:12].reshape(2, 2, 5, quarter),
+        small_split[:, 12:14],
+        rest[:, 0],
+        grad_up,
+        small_split[:, 14:18].reshape(2, -1),
+        grad_down,
+        small_whole[:, :2],
+        small_whole[:, 2:],
     )
 
 

time: 842 us -> 726 us (0.86)
  waiting for transfers between devices: 288 us -> 43.5 us
  Pallas kernels: 71.7 us -> 286 us
  starting transfers between devices: 116 us -> 71.6 us
  other arithmetic: 76 us -> 52.2 us
  between operations: 16.5 us -> 2.52 us
  local copies, waits for them, and re-layouts: 101 us -> 91.8 us
    pallas_call x0 -> x1, Pallas kernels: none -> 215 us  [reduce_parts(): pl.pallas_call(functools.partial(reduce_kernel, group, count), out_shape=...]
    ppermute x59 -> x27, waiting for transfers between devices: 218 us -> 43.5 us  [swap(): return lax.ppermute(values, axis, [(i, i ^ bit) for i in range(count)])]
    psum x1 -> x0, waiting for transfers between devices: 69.6 us -> none  [shards(): lax.psum(jnp.concatenate([small_split, small_whole], axis=1), BOTH)]
    ppermute x59 -> x27, starting transfers between devices: 87.9 us -> 46 us  [swap(): return lax.ppermute(values, axis, [(i, i ^ bit) for i in range(count)])]
    split x24 -> x0, local copies, waits for them, and re-layouts: 30.8 us -> none  [split_rows(): return jnp.split(values, 4, axis=0)]
    concatenate x1 -> x4, other arithmetic: 1.43 us -> 27.9 us  [the longest x1 20.7 us: shards(): jnp.concatenate([collected[1][0], collected[0][0], jnp.stack(extra)[None]...]
    convert_element_type x14 -> x0, other arithmetic: 22 us -> none  [the longest x4 12.2 us: reduce_parts(): received = swap(sent, 'mp', 1).astype(F32)]
    add x12 -> x0, other arithmetic: 19.9 us -> none  [the longest x4 12.9 us: reduce_parts(): own = own + swap(across.astype(BF16), 'mp', 2).astype(F32)]
  transfers between devices with their start and end apart: 68 -> 35, of which waited for: 19 -> 4; matrix products, arithmetic and copies ran while one was open for 31% -> 17% of each run, Pallas kernels for 6% -> 4%
where the time goes in v2:
time: 726 us; the launch traced here: 718 us
  Pallas kernels  286 us (39%)
  matrix products  171 us (24%)
  local copies, waits for them, and re-layouts  91.8 us (13%)
  starting transfers between devices  71.6 us (10%)
  other arithmetic  52.2 us (7%)
  waiting for transfers between devices  43.5 us (6%)
    pallas_call x1, Pallas kernels, reduce_parts(): pl.pallas_call(functools.partial(reduce_kernel, group, count), out_shape=...  215 us
    dot_general x12, matrix products, product_right_t(): lax.dot_general(left, right, (((1,), (1,)), ((), ())), preferred_element_...  75.8 us
    dot_general x12, matrix products, product(): return jnp.dot(left, right, preferred_element_type=F32)  58.2 us
    ppermute x27, starting transfers between devices, swap(): return lax.ppermute(values, axis, [(i, i ^ bit) for i in range(count)])  46 us
    ppermute x27, waiting for transfers between devices, swap(): return lax.ppermute(values, axis, [(i, i ^ bit) for i in range(count)])  43.5 us
    pallas_call x2, Pallas kernels, attend_backward(): pl.pallas_call(attend_backward_kernel, out_shape=(shape((total, width), B...  39.5 us
    dot_general x12, matrix products, product_left_t(): lax.dot_general(left, right, (((0,), (0,)), ((), ())), preferred_element_...  36.7 us
    pallas_call x2, Pallas kernels, attend_forward(): pl.pallas_call(attend_forward_kernel, out_shape=(shape((total, width), BF...  31.9 us
  transfers between devices with their start and end apart: 35, of which 4 were waited for; matrix products, arithmetic and copies ran while one was open for 17% of the time, Pallas kernels for 4%

profile of v2, /device:TPU:15, one launch (start us, length us, event | category | flops | bytes accessed | tf_op | source)
XLA Modules:
  0.0 718.4 jit_solution(16164755319913693989)
XLA Ops:
  16.5 3.4 slice_bitcast_fusion.16
  21.1 7.3 %collective-permute-done.1 = bf16[3,768,192]{1,2,0:T(8,128)(2,1)} collective-permute-done((bf16[3,768,192]{1,2,0:T(8,128)(2,1)S(1)}, bf16[3,768,192]{1,2,0:T(8,128)(2,1)}, u32[]{:S(2)}, u32[]{:S(2)}) %collective-permute-start.1) | collective-permute-done | bytes 884768 | tf_op jit(solution)/shard_map/ppermute | solution.py:37
  36.5 5.7 collective-permute-start.6
  51.5 17.4 %collective-permute-done.9 = bf16[192,768]{1,0:T(8,128)(2,1)S(1)} collective-permute-done((bf16[192,768]{1,0:T(8,128)(2,1)S(1)}, bf16[192,768]{1,0:T(8,128)(2,1)S(1)}, u32[]{:S(2)}, u32[]{:S(2)}) %collective-permute-start.9) | collective-permute-done | bytes 294944 | tf_op jit(solution)/shard_map/ppermute | solution.py:37
  71.2 3.8 add_convert_fusion.1.v_ref
  75.0 3.8 convolution_convert_fusion.5.k_ref
  80.5 15.9 %attend_forward.2 = (bf16[512,768]{1,0:T(8,128)(2,1)}, f32[4,6,256]{2,1,0:T(8,128)}, bf16[256,768]{1,0:T(8,128)(2,1)}, bf16[256,768]{1,0:T(8,128)(2,1)}) custom-call(bf16[512,768]{1,0:T(8,128)(2,1)} %fusion.44.q_ref, bf16[1088,768]{1,0:T(8,128)(2,1)} %convolution_convert_fusion.5.k_ref, bf16[1088,768]{1,0:T(8,128)(2,1)} %add_convert_fusion.1.v_ref, ...), custom_call_target="tpu_custom_call" | custom-call | tf_op jit(solution)/shard_map/attend_forward/pallas_call | solution.py:265
  101.8 14.3 %multiply_convert_fusion.1 = (bf16[512,3072]{1,0:T(8,128)(2,1)S(1)}, f32[512,3072]{1,0:T(8,128)}) fusion(f32[3072]{0:T(1024)S(1)} %bitcast.188, bf16[768,768]{1,0:T(8,128)(2,1)S(1)} %collective-permute-done.13, bf16[768,768]{1,0:T(8,128)(2,1)} %collective-permute-done.12, bf16[768,768]{1,0:T(8,128)(2,1)S(1)} %collective-permute-done.11, ...), kind=kOutput, calls=%fused_computation.28 | convolution fusion | flops 2488664064 | bytes 15751168 | tf_op jit(solution)/shard_map/dot_general | solution.py:24
  121.6 2.7 fusion.89
  127.1 5.4 collective-permute-start.20
  135.2 16.9 %collective-permute-done.23 = bf16[192,768]{1,0:T(8,128)(2,1)} collective-permute-done((bf16[192,768]{1,0:T(8,128)(2,1)S(1)}, bf16[192,768]{1,0:T(8,128)(2,1)}, u32[]{:S(2)}, u32[]{:S(2)}) %collective-permute-start.23) | collective-permute-done | bytes 294944 | tf_op jit(solution)/shard_map/ppermute | solution.py:37
  153.6 28.9 %collective-permute-start.24 = (bf16[192,768]{1,0:T(8,128)(2,1)}, bf16[192,768]{1,0:T(8,128)(2,1)S(1)}, u32[]{:S(2)}, u32[]{:S(2)}) collective-permute-start(bf16[192,768]{1,0:T(8,128)(2,1)} %collective-permute-done.23), channel_id=1, source_target_pairs={{0,1},{1,0},{2,3},{3,2},{4,5},{5,4},{6,7},{7,6},{8,9},{9,8},{10,11... | collective-permute-start | bytes 884744 | tf_op jit(solution)/shard_map/ppermute | solution.py:37
  184.2 2.7 add_convert_fusion.v_ref
  186.9 2.7 convolution_convert_fusion.4.k_ref
  189.6 15.9 %attend_forward.3 = (bf16[512,768]{1,0:T(8,128)(2,1)}, f32[4,6,256]{2,1,0:T(8,128)}, bf16[256,768]{1,0:T(8,128)(2,1)}, bf16[256,768]{1,0:T(8,128)(2,1)}) custom-call(bf16[512,768]{1,0:T(8,128)(2,1)} %add_convert_fusion.2.q_ref, bf16[1088,768]{1,0:T(8,128)(2,1)} %convolution_convert_fusion.4.k_ref, bf16[1088,768]{1,0:T(8,128)(2,1)} %add_convert_fusion.v_ref, ...), custom_call_target="tpu_custom_call" | custom-call | tf_op jit(solution)/shard_map/attend_forward/pallas_call | solution.py:265
  208.9 14.4 %multiply_convert_fusion = (bf16[512,3072]{1,0:T(8,128)(2,1)S(1)}, f32[512,3072]{1,0:T(8,128)}) fusion(f32[3072]{0:T(1024)S(1)} %bitcast.190, bf16[768,768]{1,0:T(8,128)(2,1)} %collective-permute-done.27, bf16[768,768]{1,0:T(8,128)(2,1)} %collective-permute-done.26, bf16[768,768]{1,0:T(8,128)(2,1)} %collective-permute-done.25, ...), kind=kOutput, calls=%fused_computation.23 | convolution fusion | flops 2488664064 | bytes 15751168 | tf_op jit(solution)/shard_map/dot_general | solution.py:24
  223.3 5.5 fusion.91
  232.9 17.4 %fusion.94 = (bf16[3072]{0:T(1024)(128)(2,1)S(1)}, bf16[512,3072]{1,0:T(8,128)(2,1)S(1)}) fusion(f32[512,3072]{1,0:T(8,128)} %get-tuple-element.194, f32[3072]{0:T(1024)S(1)} %bitcast.191, bf16[768,768]{1,0:T(8,128)(2,1)S(1)} %collective-permute-done.30, bf16[768,768]{1,0:T(8,128)(2,1)} %collective-permute-done.29, ...), kind=kOutput, calls=%fused_computation.252 | convolution fusion | flops 2499671040 | bytes 15747072 | tf_op jit(solution)/shard_map/dot_general | solution.py:32
  250.4 7.7 %multiply_reduce_fusion = (bf16[768]{0:T(1024)(128)(2,1)}, f32[512]{0:T(512)S(1)}, f32[512]{0:T(512)S(1)}, bf16[768]{0:T(1024)(128)(2,1)}, f32[512,768]{1,0:T(8,128)S(1)}) fusion(f32[512,768]{1,0:T(8,128)S(1)} %get-tuple-element.192, f32[512]{0:T(512)S(1)} %add_rsqrt_fusion.1, f32[512]{0:T(512)S(1)} %broadcast_multiply_fusion.9, f32[768]{0:T(1024)S(1)} %copy-done.58, ...), kind=kOutput, calls=%fused_computation.81 | convolution fusion | flops 2438723072 | bytes 12597248 | tf_op jit(solution)/shard_map/dot_general | solution.py:32
  259.2 2.7 convolution_convert_fusion.15.grad_ref
  261.9 19.6 %attend_backward.2 = (bf16[512,768]{1,0:T(8,128)(2,1)}, bf16[1088,768]{1,0:T(8,128)(2,1)}, bf16[1088,768]{1,0:T(8,128)(2,1)}, f32[16,768]{1,0:T(8,128)}) custom-call(bf16[512,768]{1,0:T(8,128)(2,1)} %add_convert_fusion.2.q_ref, bf16[1088,768]{1,0:T(8,128)(2,1)} %convolution_convert_fusion.4.k_ref, bf16[1088,768]{1,0:T(8,128)(2,1)} %add_convert_fusion.v_ref, ...), custom_call_target="tpu_custom_call" | custom-call | tf_op jit(solution)/shard_map/attend_backward/pallas_call | solution.py:284
  281.5 3.0 fusion.47
  284.6 3.3 fusion.92
  290.5 4.7 convolution_convert_fusion.2
  295.3 4.3 convolution_convert_fusion.3
  299.6 3.0 collective-permute-start.32
  319.7 5.4 slice_bitcast_fusion.8
  325.2 3.4 multiply_reduce_fusion.1
  331.6 19.9 %fusion.95 = (bf16[3072]{0:T(1024)(128)(2,1)S(1)}, bf16[512,3072]{1,0:T(8,128)(2,1)S(1)}) fusion(f32[512,3072]{1,0:T(8,128)} %get-tuple-element.188, f32[3072]{0:T(1024)S(1)} %bitcast.189, bf16[768,768]{1,0:T(8,128)(2,1)S(1)} %copy-done.89, bf16[768,768]{1,0:T(8,128)(2,1)S(1)} %copy-done.83, bf16[768,768]{1,0:T(8,128)(2,1)S(1)} %copy-done.87, ...), kind=kOutput, calls=%fused_computation.253 | convolution fusion | flops 2499671040 | bytes 15747072 | tf_op jit(solution)/shard_map/dot_general | solution.py:32
  351.6 5.8 multiply_reduce_fusion.2
  358.5 2.8 convolution_convert_fusion.14.grad_ref
  361.3 19.9 %attend_backward.3 = (bf16[512,768]{1,0:T(8,128)(2,1)}, bf16[1088,768]{1,0:T(8,128)(2,1)}, bf16[1088,768]{1,0:T(8,128)(2,1)}, f32[16,768]{1,0:T(8,128)}) custom-call(bf16[512,768]{1,0:T(8,128)(2,1)} %fusion.44.q_ref, bf16[1088,768]{1,0:T(8,128)(2,1)} %convolution_convert_fusion.5.k_ref, bf16[1088,768]{1,0:T(8,128)(2,1)} %add_convert_fusion.1.v_ref, ...), custom_call_target="tpu_custom_call" | custom-call | tf_op jit(solution)/shard_map/attend_backward/pallas_call | solution.py:284
  381.2 3.4 fusion.45
  384.5 2.9 fusion.93
  390.9 4.7 convolution_convert_fusion
  395.6 4.5 convolution_convert_fusion.1
  417.7 3.2 convolution_convert_fusion.6
  420.9 3.1 convolution_convert_fusion.7
  424.1 5.5 maximum_maximum_fusion.1
  429.6 5.6 slice_bitcast_fusion.4
  436.5 20.7 %pad_maximum_fusion.parts_ref = bf16[19,4,256,768]{3,2,1,0:T(8,128)(2,1)} fusion(bf16[1,4,256,768]{3,2,1,0:T(8,128)(2,1)} %maximum_bitcast_fusion, bf16[9,1,256,768]{3,2,1,0:T(8,128)(2,1)} %get-tuple-element.153, bf16[9,1,256,768]{3,2,1,0:T(8,128)(2,1)} %get-tuple-element.154, bf16[9,1,256,768]{3,2,1,0:T(8,128)(2,1)} %get-tuple-element.155, ...), kind=kLoop, calls=%fused_computation | loop fusion | flops 119537664 | bytes 59768832 | tf_op jit(solution)/shard_map/concatenate | solution.py:700
  457.2 214.7 %reduce_parts.1 = bf16[19,256,768]{2,1,0:T(8,128)(2,1)} custom-call(bf16[19,4,256,768]{3,2,1,0:T(8,128)(2,1)} %pad_maximum_fusion.parts_ref), custom_call_target="tpu_custom_call" | custom-call | tf_op jit(solution)/shard_map/reduce_parts/pallas_call | solution.py:507
  672.0 9.7 %fusion.83 = (f32[9,256,768]{2,1,0:T(8,128)}, f32[9,256,768]{2,1,0:T(8,128)}) fusion(bf16[19,256,768]{2,1,0:T(8,128)(2,1)} %reduce_parts.1), kind=kLoop, calls=%fused_computation.241 | loop fusion | bytes 28311552 | tf_op jit(solution)/shard_map/slice | solution.py:705
  683.0 3.6 collective-permute-start.34
  688.5 8.9 %pad_maximum_fusion.1 = (f32[2,1,3,4,64,768]{5,4,3,2,1,0:T(8,128)}, f32[2,1,3,4,64,768]{5,4,3,2,1,0:T(8,128)S(1)}, f32[2,1,3,4,64,768]{5,4,3,2,1,0:T(8,128)}) fusion(f32[1,3,3,4,64,768]{5,4,3,2,1,0:T(8,128)} %bitcast.162, f32[1,3,3,4,64,768]{5,4,3,2,1,0:T(8,128)} %bitcast.163), kind=kLoop, calls=%fused_computation.39 | loop fusion | flops 3538944 | bytes 28311552 | tf_op jit(solution)/shard_map/stack | solution.py:705
  703.6 6.0 copy.104
  710.3 4.3 slice_bitcast_fusion
  714.7 3.5 fusion.25
  (431 shorter events, 121.6 us)
Async XLA Ops:
  4.2 16.4 %collective-permute-start.4 = (f32[36,192]{1,0:T(8,128)}, f32[36,192]{1,0:T(8,128)S(1)}, u32[]{:S(2)}, u32[]{:S(2)}) collective-permute-start(f32[36,192]{1,0:T(8,128)} %pad_maximum_fusion.26), channel_id=1, source_target_pairs={{0,2},{1,3},{2,0},{3,1},{4,6},{5,7},{6,4},{7,5},{8,10},{9,11},{10,... | collective-permute-start | bytes 82952 | tf_op jit(solution)/shard_map/ppermute | solution.py:37
  4.4 29.4 %collective-permute-start.3 = (f32[36,192]{1,0:T(8,128)}, f32[36,192]{1,0:T(8,128)S(1)}, u32[]{:S(2)}, u32[]{:S(2)}) collective-permute-start(f32[36,192]{1,0:T(8,128)} %pad_maximum_fusion.26), channel_id=1, source_target_pairs={{0,1},{1,0},{2,3},{3,2},{4,5},{5,4},{6,7},{7,6},{8,9},{9,8},{10,11... | collective-permute-start | bytes 82952 | tf_op jit(solution)/shard_map/ppermute | solution.py:37
  7.0 21.4 %collective-permute-start.1 = (bf16[3,768,192]{1,2,0:T(8,128)(2,1)S(1)}, bf16[3,768,192]{1,2,0:T(8,128)(2,1)}, u32[]{:S(2)}, u32[]{:S(2)}) collective-permute-start(bf16[3,768,192]{1,2,0:T(8,128)(2,1)S(1)} %get-tuple-element.163), channel_id=1, source_target_pairs={{0,2},{1,3},{2,0},{3,1},{4,6},{5,7},{6,4},{7,5},{8,10},{9,11},{10,... | collective-permute-start | bytes 2654216 | tf_op jit(solution)/shard_map/ppermute | solution.py:37
  8.3 41.0 %collective-permute-start = (bf16[3,768,192]{1,2,0:T(8,128)(2,1)S(1)}, bf16[3,768,192]{1,2,0:T(8,128)(2,1)}, u32[]{:S(2)}, u32[]{:S(2)}) collective-permute-start(bf16[3,768,192]{1,2,0:T(8,128)(2,1)S(1)} %get-tuple-element.163), channel_id=1, source_target_pairs={{0,1},{1,0},{2,3},{3,2},{4,5},{5,4},{6,7},{7,6},{8,9},{9,8},{10,11... | collective-permute-start | bytes 2654216 | tf_op jit(solution)/shard_map/ppermute | solution.py:37
  10.1 60.9 %collective-permute-start.12 = (bf16[768,768]{1,0:T(8,128)(2,1)}, bf16[768,768]{1,0:T(8,128)(2,1)}, u32[]{:S(2)}, u32[]{:S(2)}) collective-permute-start(bf16[768,768]{1,0:T(8,128)(2,1)} %get-tuple-element.160), channel_id=1, source_target_pairs={{0,2},{1,3},{2,0},{3,1},{4,6},{5,7},{6,4},{7,5},{8,10},{9,11},{10,... | collective-permute-start | bytes 3538952 | tf_op jit(solution)/shard_map/ppermute | solution.py:37
  16.5 80.6 %copy-start.37 = (bf16[192,768]{1,0:T(8,128)(2,1)}, bf16[192,768]{1,0:T(8,128)(2,1)S(1)}, u32[]{:S(2)}) copy-start(bf16[192,768]{1,0:T(8,128)(2,1)S(1)} %get-tuple-element.166) | copy-start | bytes 884740
  20.6 15.9 %collective-permute-start.5 = (f32[36,192]{1,0:T(8,128)S(1)}, f32[36,192]{1,0:T(8,128)S(1)}, u32[]{:S(2)}, u32[]{:S(2)}) collective-permute-start(f32[36,192]{1,0:T(8,128)S(1)} %collective-permute-done.4), channel_id=1, source_target_pairs={{0,1},{1,0},{2,3},{3,2},{4,5},{5,4},{6,7},{7,6},{8,9},{9,8},{10,11... | collective-permute-start | bytes 82952 | tf_op jit(solution)/shard_map/ppermute | solution.py:37
  28.4 20.9 %collective-permute-start.2 = (bf16[3,768,192]{1,2,0:T(8,128)(2,1)}, bf16[3,768,192]{1,2,0:T(8,128)(2,1)}, u32[]{:S(2)}, u32[]{:S(2)}) collective-permute-start(bf16[3,768,192]{1,2,0:T(8,128)(2,1)} %collective-permute-done.1), channel_id=1, source_target_pairs={{0,1},{1,0},{2,3},{3,2},{4,5},{5,4},{6,7},{7,6},{8,9},{9,8},{10,11... | collective-permute-start | bytes 2654216 | tf_op jit(solution)/shard_map/ppermute | solution.py:37
  33.8 35.6 %collective-permute-start.7 = (bf16[256,768]{1,0:T(8,128)(2,1)}, bf16[256,768]{1,0:T(8,128)(2,1)}, u32[]{:S(2)}, u32[]{:S(2)}) collective-permute-start(bf16[256,768]{1,0:T(8,128)(2,1)} %slice.356), channel_id=1, source_target_pairs={{1,0},{2,1},{3,2},{4,3},{5,4},{6,5},{7,6},{8,7},{9,8},{10,9},{11,1... | collective-permute-start | bytes 1179656 | tf_op jit(solution)/shard_map/ppermute | solution.py:42
  36.5 34.2 %collective-permute-start.6 = (bf16[272,768]{1,0:T(8,128)(2,1)S(1)}, bf16[272,768]{1,0:T(8,128)(2,1)}, u32[]{:S(2)}, u32[]{:S(2)}) collective-permute-start(bf16[272,768]{1,0:T(8,128)(2,1)S(1)} %slice.355), channel_id=1, source_target_pairs={{0,1},{1,2},{2,3},{3,4},{4,5},{5,6},{6,7},{7,8},{8,9},{9,10},{10,1... | collective-permute-start | bytes 1253384 | tf_op jit(solution)/shard_map/ppermute | solution.py:42
  48.6 53.2 %copy-start.60 = (f32[1,4,768]{2,0,1:T(1,128)}, f32[1,4,768]{2,0,1:T(1,128)S(1)}, u32[]{:S(2)}) copy-start(f32[1,4,768]{2,0,1:T(1,128)S(1)} %get-tuple-element.178) | copy-start | bytes 36868
  49.3 50.4 %collective-permute-start.11 = (bf16[768,768]{1,0:T(8,128)(2,1)}, bf16[768,768]{1,0:T(8,128)(2,1)S(1)}, u32[]{:S(2)}, u32[]{:S(2)}) collective-permute-start(bf16[768,768]{1,0:T(8,128)(2,1)} %get-tuple-element.160), channel_id=1, source_target_pairs={{0,1},{1,0},{2,3},{3,2},{4,5},{5,4},{6,7},{7,6},{8,9},{9,8},{10,11... | collective-permute-start | bytes 3538952 | tf_op jit(solution)/shard_map/ppermute | solution.py:37
  49.3 19.6 %collective-permute-start.9 = (bf16[192,768]{1,0:T(8,128)(2,1)S(1)}, bf16[192,768]{1,0:T(8,128)(2,1)S(1)}, u32[]{:S(2)}, u32[]{:S(2)}) collective-permute-start(bf16[192,768]{1,0:T(8,128)(2,1)S(1)} %get-tuple-element.166), channel_id=1, source_target_pairs={{0,2},{1,3},{2,0},{3,1},{4,6},{5,7},{6,4},{7,5},{8,10},{9,11},{10,... | collective-permute-start | bytes 884744 | tf_op jit(solution)/shard_map/ppermute | solution.py:37
  51.5 27.4 %copy-start.3 = (bf16[3,768,768]{1,2,0:T(8,128)(2,1)}, bf16[3,768,768]{1,2,0:T(8,128)(2,1)S(1)}, u32[]{:S(2)}) copy-start(bf16[3,768,768]{1,2,0:T(8,128)(2,1)S(1)} %pad_maximum_fusion.6) | copy-start | bytes 10616836
  68.9 28.2 %copy-start.95 = (bf16[192,768]{1,0:T(8,128)(2,1)}, bf16[192,768]{1,0:T(8,128)(2,1)S(1)}, u32[]{:S(2)}) copy-start(bf16[192,768]{1,0:T(8,128)(2,1)S(1)} %collective-permute-done.9) | copy-start | bytes 884740
  68.9 27.6 %collective-permute-start.8 = (bf16[192,768]{1,0:T(8,128)(2,1)S(1)}, bf16[192,768]{1,0:T(8,128)(2,1)}, u32[]{:S(2)}, u32[]{:S(2)}) collective-permute-start(bf16[192,768]{1,0:T(8,128)(2,1)S(1)} %get-tuple-element.166), channel_id=1, source_target_pairs={{0,1},{1,0},{2,3},{3,2},{4,5},{5,4},{6,7},{7,6},{8,9},{9,8},{10,11... | collective-permute-start | bytes 884744 | tf_op jit(solution)/shard_map/ppermute | solution.py:37
  69.4 30.8 %collective-permute-start.15 = (bf16[768,768]{1,0:T(8,128)(2,1)S(1)}, bf16[768,768]{1,0:T(8,128)(2,1)S(1)}, u32[]{:S(2)}, u32[]{:S(2)}) collective-permute-start(bf16[768,768]{1,0:T(8,128)(2,1)S(1)} %copy-done.28), channel_id=1, source_target_pairs={{0,2},{1,3},{2,0},{3,1},{4,6},{5,7},{6,4},{7,5},{8,10},{9,11},{10,... | collective-permute-start | bytes 3538952 | tf_op jit(solution)/shard_map/ppermute | solution.py:37
  70.6 26.2 %collective-permute-start.10 = (bf16[192,768]{1,0:T(8,128)(2,1)S(1)}, bf16[192,768]{1,0:T(8,128)(2,1)}, u32[]{:S(2)}, u32[]{:S(2)}) collective-permute-start(bf16[192,768]{1,0:T(8,128)(2,1)S(1)} %collective-permute-done.9), channel_id=1, source_target_pairs={{0,1},{1,0},{2,3},{3,2},{4,5},{5,4},{6,7},{7,6},{8,9},{9,8},{10,11... | collective-permute-start | bytes 884744 | tf_op jit(solution)/shard_map/ppermute | solution.py:37
  71.0 30.4 %collective-permute-start.13 = (bf16[768,768]{1,0:T(8,128)(2,1)}, bf16[768,768]{1,0:T(8,128)(2,1)S(1)}, u32[]{:S(2)}, u32[]{:S(2)}) collective-permute-start(bf16[768,768]{1,0:T(8,128)(2,1)} %collective-permute-done.12), channel_id=1, source_target_pairs={{0,1},{1,0},{2,3},{3,2},{4,5},{5,4},{6,7},{7,6},{8,9},{9,8},{10,11... | collective-permute-start | bytes 3538952 | tf_op jit(solution)/shard_map/ppermute | solution.py:37
  96.4 21.8 %collective-permute-start.14 = (bf16[768,768]{1,0:T(8,128)(2,1)S(1)}, bf16[768,768]{1,0:T(8,128)(2,1)S(1)}, u32[]{:S(2)}, u32[]{:S(2)}) collective-permute-start(bf16[768,768]{1,0:T(8,128)(2,1)S(1)} %copy-done.28), channel_id=1, source_target_pairs={{0,1},{1,0},{2,3},{3,2},{4,5},{5,4},{6,7},{7,6},{8,9},{9,8},{10,11... | collective-permute-start | bytes 3538952 | tf_op jit(solution)/shard_map/ppermute | solution.py:37
  96.8 21.1 %collective-permute-start.18 = (bf16[3,768,192]{1,2,0:T(8,128)(2,1)S(1)}, bf16[3,768,192]{1,2,0:T(8,128)(2,1)S(1)}, u32[]{:S(2)}, u32[]{:S(2)}) collective-permute-start(bf16[3,768,192]{1,2,0:T(8,128)(2,1)S(1)} %get-tuple-element.162), channel_id=1, source_target_pairs={{0,2},{1,3},{2,0},{3,1},{4,6},{5,7},{6,4},{7,5},{8,10},{9,11},{10,... | collective-permute-start | bytes 2654216 | tf_op jit(solution)/shard_map/ppermute | solution.py:37
  99.7 25.5 %collective-permute-start.17 = (bf16[3,768,192]{1,2,0:T(8,128)(2,1)S(1)}, bf16[3,768,192]{1,2,0:T(8,128)(2,1)S(1)}, u32[]{:S(2)}, u32[]{:S(2)}) collective-permute-start(bf16[3,768,192]{1,2,0:T(8,128)(2,1)S(1)} %get-tuple-element.162), channel_id=1, source_target_pairs={{0,1},{1,0},{2,3},{3,2},{4,5},{5,4},{6,7},{7,6},{8,9},{9,8},{10,11... | collective-permute-start | bytes 2654216 | tf_op jit(solution)/shard_map/ppermute | solution.py:37
  100.2 53.4 %collective-permute-start.26 = (bf16[768,768]{1,0:T(8,128)(2,1)}, bf16[768,768]{1,0:T(8,128)(2,1)}, u32[]{:S(2)}, u32[]{:S(2)}) collective-permute-start(bf16[768,768]{1,0:T(8,128)(2,1)} %get-tuple-element.161), channel_id=1, source_target_pairs={{0,2},{1,3},{2,0},{3,1},{4,6},{5,7},{6,4},{7,5},{8,10},{9,11},{10,... | collective-permute-start | bytes 3538952 | tf_op jit(solution)/shard_map/ppermute | solution.py:37
  101.4 18.0 %collective-permute-start.16 = (bf16[768,768]{1,0:T(8,128)(2,1)S(1)}, bf16[768,768]{1,0:T(8,128)(2,1)S(1)}, u32[]{:S(2)}, u32[]{:S(2)}) collective-permute-start(bf16[768,768]{1,0:T(8,128)(2,1)S(1)} %collective-permute-done.15), channel_id=1, source_target_pairs={{0,1},{1,0},{2,3},{3,2},{4,5},{5,4},{6,7},{7,6},{8,9},{9,8},{10,11... | collective-permute-start | bytes 3538952 | tf_op jit(solution)/shard_map/ppermute | solution.py:37
  117.9 34.1 %collective-permute-start.23 = (bf16[192,768]{1,0:T(8,128)(2,1)S(1)}, bf16[192,768]{1,0:T(8,128)(2,1)}, u32[]{:S(2)}, u32[]{:S(2)}) collective-permute-start(bf16[192,768]{1,0:T(8,128)(2,1)S(1)} %copy-done.39), channel_id=1, source_target_pairs={{0,2},{1,3},{2,0},{3,1},{4,6},{5,7},{6,4},{7,5},{8,10},{9,11},{10,... | collective-permute-start | bytes 884744 | tf_op jit(solution)/shard_map/ppermute | solution.py:37
  118.2 87.4 %collective-permute-start.29 = (bf16[768,768]{1,0:T(8,128)(2,1)}, bf16[768,768]{1,0:T(8,128)(2,1)}, u32[]{:S(2)}, u32[]{:S(2)}) collective-permute-start(bf16[768,768]{1,0:T(8,128)(2,1)} %get-tuple-element.158), channel_id=1, source_target_pairs={{0,2},{1,3},{2,0},{3,1},{4,6},{5,7},{6,4},{7,5},{8,10},{9,11},{10,... | collective-permute-start | bytes 3538952 | tf_op jit(solution)/shard_map/ppermute | solution.py:37
  119.4 7.7 %collective-permute-start.19 = (bf16[3,768,192]{1,2,0:T(8,128)(2,1)S(1)}, bf16[3,768,192]{1,2,0:T(8,128)(2,1)S(1)}, u32[]{:S(2)}, u32[]{:S(2)}) collective-permute-start(bf16[3,768,192]{1,2,0:T(8,128)(2,1)S(1)} %collective-permute-done.18), channel_id=1, source_target_pairs={{0,1},{1,0},{2,3},{3,2},{4,5},{5,4},{6,7},{7,6},{8,9},{9,8},{10,11... | collective-permute-start | bytes 2654216 | tf_op jit(solution)/shard_map/ppermute | solution.py:37
  124.4 81.8 %copy-start.46 = (f32[512]{0:T(512)}, f32[512]{0:T(512)S(1)}, u32[]{:S(2)}) copy-start(f32[512]{0:T(512)S(1)} %broadcast_multiply_fusion.10) | copy-start | bytes 6148
  124.7 81.5 %copy-start.52 = (f32[512]{0:T(512)}, f32[512]{0:T(512)S(1)}, u32[]{:S(2)}) copy-start(f32[512]{0:T(512)S(1)} %add_rsqrt_fusion.2) | copy-start | bytes 6148
  125.0 61.9 %copy-start.18 = (bf16[512,768]{1,0:T(8,128)(2,1)}, bf16[512,768]{1,0:T(8,128)(2,1)S(1)}, u32[]{:S(2)}) copy-start(bf16[512,768]{1,0:T(8,128)(2,1)S(1)} %fusion.42) | copy-start | bytes 2359300
  125.1 28.5 %collective-permute-start.21 = (bf16[256,768]{1,0:T(8,128)(2,1)S(1)}, bf16[256,768]{1,0:T(8,128)(2,1)S(1)}, u32[]{:S(2)}, u32[]{:S(2)}) collective-permute-start(bf16[256,768]{1,0:T(8,128)(2,1)S(1)} %slice.456), channel_id=1, source_target_pairs={{1,0},{2,1},{3,2},{4,3},{5,4},{6,5},{7,6},{8,7},{9,8},{10,9},{11,1... | collective-permute-start | bytes 1179656 | tf_op jit(solution)/shard_map/ppermute | solution.py:42
  127.1 55.5 %collective-permute-start.20 = (bf16[272,768]{1,0:T(8,128)(2,1)S(1)}, bf16[272,768]{1,0:T(8,128)(2,1)S(1)}, u32[]{:S(2)}, u32[]{:S(2)}) collective-permute-start(bf16[272,768]{1,0:T(8,128)(2,1)S(1)} %slice.455), channel_id=1, source_target_pairs={{0,1},{1,2},{2,3},{3,4},{4,5},{5,6},{6,7},{7,8},{8,9},{9,10},{10,1... | collective-permute-start | bytes 1253384 | tf_op jit(solution)/shard_map/ppermute | solution.py:42
  133.1 151.4 %copy-start.5 = (bf16[3,768,768]{1,2,0:T(8,128)(2,1)}, bf16[3,768,768]{1,2,0:T(8,128)(2,1)S(1)}, u32[]{:S(2)}) copy-start(bf16[3,768,768]{1,2,0:T(8,128)(2,1)S(1)} %pad_maximum_fusion.7) | copy-start | bytes 10616836
  133.1 51.1 %copy-start.73 = (f32[768]{0:T(1024)S(1)}, f32[768]{0:T(1024)}, u32[]{:S(2)}) copy-start(f32[768]{0:T(1024)} %get-tuple-element.119) | copy-start | bytes 9220
  152.1 56.7 %collective-permute-start.25 = (bf16[768,768]{1,0:T(8,128)(2,1)}, bf16[768,768]{1,0:T(8,128)(2,1)}, u32[]{:S(2)}, u32[]{:S(2)}) collective-permute-start(bf16[768,768]{1,0:T(8,128)(2,1)} %get-tuple-element.161), channel_id=1, source_target_pairs={{0,1},{1,0},{2,3},{3,2},{4,5},{5,4},{6,7},{7,6},{8,9},{9,8},{10,11... | collective-permute-start | bytes 3538952 | tf_op jit(solution)/shard_map/ppermute | solution.py:37
  153.6 51.9 %collective-permute-start.22 = (bf16[192,768]{1,0:T(8,128)(2,1)S(1)}, bf16[192,768]{1,0:T(8,128)(2,1)S(1)}, u32[]{:S(2)}, u32[]{:S(2)}) collective-permute-start(bf16[192,768]{1,0:T(8,128)(2,1)S(1)} %copy-done.39), channel_id=1, source_target_pairs={{0,1},{1,0},{2,3},{3,2},{4,5},{5,4},{6,7},{7,6},{8,9},{9,8},{10,11... | collective-permute-start | bytes 884744 | tf_op jit(solution)/shard_map/ppermute | solution.py:37
  153.6 33.3 %copy-start.93 = (bf16[256,768]{1,0:T(8,128)(2,1)}, bf16[256,768]{1,0:T(8,128)(2,1)S(1)}, u32[]{:S(2)}) copy-start(bf16[256,768]{1,0:T(8,128)(2,1)S(1)} %collective-permute-done.21) | copy-start | bytes 1179652
  153.6 52.5 %collective-permute-start.24 = (bf16[192,768]{1,0:T(8,128)(2,1)}, bf16[192,768]{1,0:T(8,128)(2,1)S(1)}, u32[]{:S(2)}, u32[]{:S(2)}) collective-permute-start(bf16[192,768]{1,0:T(8,128)(2,1)} %collective-permute-done.23), channel_id=1, source_target_pairs={{0,1},{1,0},{2,3},{3,2},{4,5},{5,4},{6,7},{7,6},{8,9},{9,8},{10,11... | collective-permute-start | bytes 884744 | tf_op jit(solution)/shard_map/ppermute | solution.py:37
  182.5 26.3 %collective-permute-start.27 = (bf16[768,768]{1,0:T(8,128)(2,1)}, bf16[768,768]{1,0:T(8,128)(2,1)}, u32[]{:S(2)}, u32[]{:S(2)}) collective-permute-start(bf16[768,768]{1,0:T(8,128)(2,1)} %collective-permute-done.26), channel_id=1, source_target_pairs={{0,1},{1,0},{2,3},{3,2},{4,5},{5,4},{6,7},{7,6},{8,9},{9,8},{10,11... | collective-permute-start | bytes 3538952 | tf_op jit(solution)/shard_map/ppermute | solution.py:37
  205.6 17.7 %collective-permute-start.28 = (bf16[768,768]{1,0:T(8,128)(2,1)}, bf16[768,768]{1,0:T(8,128)(2,1)S(1)}, u32[]{:S(2)}, u32[]{:S(2)}) collective-permute-start(bf16[768,768]{1,0:T(8,128)(2,1)} %get-tuple-element.158), channel_id=1, source_target_pairs={{0,1},{1,0},{2,3},{3,2},{4,5},{5,4},{6,7},{7,6},{8,9},{9,8},{10,11... | collective-permute-start | bytes 3538952 | tf_op jit(solution)/shard_map/ppermute | solution.py:37
  205.7 17.6 %collective-permute-start.30 = (bf16[768,768]{1,0:T(8,128)(2,1)}, bf16[768,768]{1,0:T(8,128)(2,1)S(1)}, u32[]{:S(2)}, u32[]{:S(2)}) collective-permute-start(bf16[768,768]{1,0:T(8,128)(2,1)} %collective-permute-done.29), channel_id=1, source_target_pairs={{0,1},{1,0},{2,3},{3,2},{4,5},{5,4},{6,7},{7,6},{8,9},{9,8},{10,11... | collective-permute-start | bytes 3538952 | tf_op jit(solution)/shard_map/ppermute | solution.py:37
  208.5 49.7 %copy-start.9 = (f32[512,768]{1,0:T(8,128)}, f32[512,768]{1,0:T(8,128)S(1)}, u32[]{:S(2)}) copy-start(f32[512,768]{1,0:T(8,128)S(1)} %get-tuple-element.192) | copy-start | bytes 4718596
  299.6 25.6 %collective-permute-start.32 = (bf16[256,768]{1,0:T(8,128)(2,1)S(1)}, bf16[256,768]{1,0:T(8,128)(2,1)}, u32[]{:S(2)}, u32[]{:S(2)}) collective-permute-start(bf16[256,768]{1,0:T(8,128)(2,1)S(1)} %slice.463), channel_id=1, source_target_pairs={{0,1},{1,2},{2,3},{3,4},{4,5},{5,6},{6,7},{7,8},{8,9},{9,10},{10,1... | collective-permute-start | bytes 1179656 | tf_op jit(solution)/shard_map/ppermute | solution.py:42
  302.6 22.6 %collective-permute-start.31 = (bf16[272,768]{1,0:T(8,128)(2,1)}, bf16[272,768]{1,0:T(8,128)(2,1)}, u32[]{:S(2)}, u32[]{:S(2)}) collective-permute-start(bf16[272,768]{1,0:T(8,128)(2,1)} %slice.462), channel_id=1, source_target_pairs={{1,0},{2,1},{3,2},{4,3},{5,4},{6,5},{7,6},{8,7},{9,8},{10,9},{11,1... | collective-permute-start | bytes 1253384 | tf_op jit(solution)/shard_map/ppermute | solution.py:42
  329.2 22.3 %copy-start.21 = (f32[512,768]{1,0:T(8,128)}, f32[512,768]{1,0:T(8,128)S(1)}, u32[]{:S(2)}) copy-start(f32[512,768]{1,0:T(8,128)S(1)} %get-tuple-element.142) | copy-start | bytes 4718596
  358.0 31.1 %copy-start.1 = (f32[512,768]{1,0:T(8,128)}, f32[512,768]{1,0:T(8,128)S(1)}, u32[]{:S(2)}) copy-start(f32[512,768]{1,0:T(8,128)S(1)} %get-tuple-element.144) | copy-start | bytes 4718596
  683.0 31.6 %collective-permute-start.34 = (bf16[256,768]{1,0:T(8,128)(2,1)}, bf16[256,768]{1,0:T(8,128)(2,1)}, u32[]{:S(2)}, u32[]{:S(2)}) collective-permute-start(bf16[256,768]{1,0:T(8,128)(2,1)} %slice.466), channel_id=1, source_target_pairs={{0,1},{1,2},{2,3},{3,4},{4,5},{5,6},{6,7},{7,8},{8,9},{9,10},{10,1... | collective-permute-start | bytes 1179656 | tf_op jit(solution)/shard_map/ppermute | solution.py:42
  686.6 28.1 %collective-permute-start.33 = (bf16[272,768]{1,0:T(8,128)(2,1)}, bf16[272,768]{1,0:T(8,128)(2,1)}, u32[]{:S(2)}, u32[]{:S(2)}) collective-permute-start(bf16[272,768]{1,0:T(8,128)(2,1)} %slice.465), channel_id=1, source_target_pairs={{1,0},{2,1},{3,2},{4,3},{5,4},{6,5},{7,6},{8,7},{9,8},{10,9},{11,1... | collective-permute-start | bytes 1253384 | tf_op jit(solution)/shard_map/ppermute | solution.py:42
  (100 other events, 775.9 us)

commit v3 on v1

--- a/solution.py
+++ b/solution.py
@@ -1,3 +1,5 @@
+import functools
+
 import jax
 import jax.numpy as jnp
 from jax import lax
@@ -58,16 +60,6 @@
     inverse = lax.rsqrt(spread + NORM_EPSILON)
     unit = centered * inverse
     return unit * gain + offset, unit, inverse
-
-
-def norm_backward(grad, unit, inverse, gain):
-    scaled = grad * gain
-    result = (
-        scaled
-        - jnp.mean(scaled, axis=-1, keepdims=True)
-        - unit * jnp.mean(scaled * unit, axis=-1, keepdims=True)
-    ) * inverse
-    return result, jnp.sum(grad * unit, axis=0), jnp.sum(grad, axis=0)
 
 
 def with_halo(rows):
@@ -184,11 +176,11 @@
             lse_ref[tile, pair : pair + 1, :] = most + jnp.log(total)
 
 
-def attend_backward_kernel(
+def attend_backward_body(
     q_ref, k_ref, v_ref, pooled_k_ref, pooled_v_ref, grad_ref, lse_ref,
     first_ref, past_ref, keep_ref, conv_ref,
     grad_q_ref, grad_k_ref, grad_v_ref, small_ref,
-    wide_k, wide_v, far_k, far_v, wide_f32,
+    wide_k, wide_v, far_k, far_v, wide_f32, slot_of,
 ):
     pairs = q_ref.shape[1] // PAIR
     wide_k[...] = jnp.zeros_like(wide_k)
@@ -224,6 +216,7 @@
             grad_query = unstack(product_left_t(key, grad_scores)).T * (HEAD_DIM**-0.5)
             grad_q_ref[rows, lanes] = grad_query.astype(BF16)
             small_ref[0:1, lanes] += jnp.sum(grad_query, axis=0, keepdims=True)
+        slot_of(tile)
 
     count = far_k.shape[0]
     begin = LEFT - 4 * POOL_REACH - 2
@@ -276,31 +269,6 @@
     )(queries, keys, values, first, past, keep, conv, conv_bias)
 
 
-def attend_backward(queries, keys, values, pooled_k, pooled_v, grad, lse, first, past, keep, conv):
-    total, width = queries.shape
-    shape = jax.ShapeDtypeStruct
-    return pl.pallas_call(
-        attend_backward_kernel,
-        out_shape=(
-            shape((total, width), BF16),
-            shape(keys.shape, BF16),
-            shape(keys.shape, BF16),
-            shape((16, width), F32),
-        ),
-        in_specs=in_vmem(11),
-        out_specs=tuple(in_vmem(4)),
-        scratch_shapes=[
-            pltpu.VMEM((width // PAIR, keys.shape[0], PAIR), F32),
-            pltpu.VMEM((width // PAIR, keys.shape[0], PAIR), F32),
-            pltpu.VMEM(pooled_k.shape, F32),
-            pltpu.VMEM(pooled_k.shape, F32),
-            pltpu.VMEM((keys.shape[0], PAIR), F32),
-        ],
-        compiler_params=pltpu.CompilerParams(vmem_limit_bytes=VMEM_LIMIT),
-        name="attend_backward",
-    )(queries, keys, values, pooled_k, pooled_v, grad, lse, first, past, keep, conv)
-
-
 def gelu_parts(pre):
     size = jnp.abs(pre) * (0.5**0.5)
     t = 1.0 / (1.0 + 0.5 * size)
@@ -335,135 +303,512 @@
     act, slope = act.astype(BF16), slope.astype(BF16)
     middle = normed + (product(act, down) + biases[2])
     result, unit_two, inverse_two = norm_forward(middle, gains[1], biases[3])
-    saved = (
-        entry_wide,
-        queries,
-        keys,
-        values,
-        pooled_k,
-        pooled_v,
-        mixed,
-        lse,
-        unit_one,
-        inverse_one,
-        normed_low,
-        act,
-        slope,
-        unit_two,
-        inverse_two,
+    saved = dict(
+        act=act, slope=slope, normed=normed_low, unit_one=unit_one, unit_two=unit_two, mixed=mixed,
+        q=queries, k=keys, v=values, pooled_k=pooled_k, pooled_v=pooled_v, entry=entry_wide,
+        down=down, up=up, out=out, qkv=qkv, inverse_one=inverse_one, inverse_two=inverse_two, lse=lse,
     )
     return result, saved
 
 
-def split_rows(values):
-    return jnp.split(values, 4, axis=0)
-
-
-def reduce_parts(parts):
-    sent = jnp.stack([parts[1], parts[3]]).astype(BF16)
-    received = swap(sent, "mp", 1).astype(F32)
-    own = parts[0] + received[0]
-    across = parts[2] + received[1]
-    own = own + swap(across.astype(BF16), "mp", 2).astype(F32)
-    place = lax.axis_index("seq")
-    count = lax.axis_size("seq")
-    bit = 1
-    while bit < count:
-        half = own.shape[0] // 2
-        side = (place // bit) % 2
-        kept = lax.dynamic_slice_in_dim(own, side * half, half, 0)
-        given = lax.dynamic_slice_in_dim(own, (1 - side) * half, half, 0).astype(BF16)
-        own = kept + swap(given, "seq", bit).astype(F32)
-        bit *= 2
-    whole = own.astype(BF16)
-    while bit > 1:
-        bit //= 2
-        side = (place // bit) % 2
-        other = swap(whole, "seq", bit)
-        whole = jnp.where(
-            side == 0,
-            jnp.concatenate([whole, other], axis=0),
-            jnp.concatenate([other, whole], axis=0),
-        )
-    return whole
-
-
-def layer_backward(grad_out, masks, weights, saved):
-    first, past, keep = masks
-    qkv, qv, conv, conv_bias, out, up, up_bias, down, gains, biases = weights
-    (
-        entry_wide,
-        queries,
-        keys,
-        values,
-        pooled_k,
-        pooled_v,
-        mixed,
-        lse,
-        unit_one,
-        inverse_one,
-        normed_low,
-        act,
-        slope,
-        unit_two,
-        inverse_two,
-    ) = saved
-    total, width = queries.shape
-    grad_middle, gain_two, shift_two = norm_backward(grad_out, unit_two, inverse_two, gains[1])
-    bias_down = jnp.sum(grad_middle, axis=0)
-    grad_middle_low = grad_middle.astype(BF16)
-    grad_w_down = product_left_t(act, grad_middle_low)
-    grad_pre = product_right_t(grad_middle_low, down) * slope.astype(F32)
-    grad_b_up = jnp.sum(grad_pre, axis=0)
-    grad_pre_low = grad_pre.astype(BF16)
-    grad_w_up_t = product_left_t(grad_pre_low, normed_low)
-    feed_parts = [
-        jnp.concatenate(pair, axis=0)
-        for pair in zip(split_rows(grad_w_down), split_rows(grad_w_up_t))
+CHUNK = 256
+LAG = 2
+MESH = pl.DeviceIdType.MESH
+LAYER_ROWS = 2304
+SMALL_ROWS = 256
+NORM_ROWS = 64
+
+
+def seat_of(seq=None, mp=None):
+    return {
+        "seq": lax.axis_index("seq") if seq is None else seq,
+        "mp": lax.axis_index("mp") if mp is None else mp,
+    }
+
+
+class Reducer:
+    def __init__(self, group, count, parts, out, bufs, sems):
+        place, seat = lax.axis_index("seq"), lax.axis_index("mp")
+        self.group, self.count, self.parts, self.out = group, count, parts, out
+        self.low, self.high = place % 2, place // 2
+        self.core = seat_of(mp=seat + 1 - 2 * (seat % 2))
+        self.across = seat_of(mp=(seat + 2) % 4)
+        self.beside = seat_of(seq=place + 1 - 2 * self.low)
+        self.others = [
+            seat_of(seq=((self.high + step) % group) * 2 + self.low) for step in range(1, group)
+        ]
+        (self.own_v, self.core_v, self.across_v, self.cross_v, self.first_v, self.give_v,
+         self.half_v, self.keep_v, self.piece_v, self.slab_v, self.sum_v, self.done_v) = bufs
+        (self.local_s, self.core_s, self.core_r, self.x_s, self.x_r, self.y_s, self.y_r,
+         self.z_s, self.z_r, self.g_s, self.g_r, self.f_s, self.f_r, self.f_l) = sems
+        self.rows = CHUNK // group
+        self.half = parts.shape[-1] // 2
+        stages = [(self.step_zero, 0), (self.step_core, 1)]
+        for k, stage in enumerate(
+            (self.step_x, self.step_y, self.step_z, self.step_gather, self.step_end)
+        ):
+            stages.append((stage, 1 + LAG * (k + 1)))
+        self.stages = stages
+        self.last = stages[-1][1]
+
+    def remote(self, source, target, send, recv, device):
+        return pltpu.make_async_remote_copy(
+            src_ref=source, dst_ref=target, send_sem=send, recv_sem=recv,
+            device_id=device, device_id_type=MESH,
+        )
+
+    def chunk_rows(self, c):
+        return pl.ds(pl.multiple_of(c * CHUNK, CHUNK), CHUNK)
+
+    def local_copy(self, c):
+        return pltpu.make_async_copy(
+            self.parts.at[pl.ds(0, 2), self.chunk_rows(c)], self.own_v.at[c % 2], self.local_s.at[c % 2]
+        )
+
+    def core_copy(self, c):
+        return self.remote(
+            self.parts.at[pl.ds(2, 2), self.chunk_rows(c)], self.core_v.at[c % 4],
+            self.core_s.at[c], self.core_r.at[c], self.core,
+        )
+
+    def x_copy(self, c):
+        return self.remote(
+            self.across_v.at[c % 3], self.cross_v.at[c % 6], self.x_s.at[c], self.x_r.at[c], self.across
+        )
+
+    def y_copy(self, c):
+        return self.remote(
+            self.give_v.at[c % 3], self.half_v.at[c % 6], self.y_s.at[c], self.y_r.at[c], self.beside
+        )
+
+    def z_copy(self, c, step):
+        to = (self.high + step) % self.group
+        return self.remote(
+            self.slab_v.at[c % 3, pl.ds(pl.multiple_of(to * self.rows, self.rows), self.rows)],
+            self.piece_v.at[c % 6, step - 1],
+            self.z_s.at[c, step - 1], self.z_r.at[c, step - 1], self.others[step - 1],
+        )
+
+    def own_rows(self):
+        return pl.ds(pl.multiple_of(self.high * self.rows, self.rows), self.rows)
+
+    def g_copy(self, c, step):
+        mine = self.done_v.at[c % 8, self.own_rows()]
+        return self.remote(
+            mine, mine, self.g_s.at[c, step - 1], self.g_r.at[c, step - 1], self.others[step - 1]
+        )
+
+    def target(self, c):
+        lanes = pl.ds(pl.multiple_of(self.low * self.half, 128), self.half)
+        return self.out.at[self.chunk_rows(c), lanes]
+
+    def f_copy(self, c):
+        return self.remote(
+            self.done_v.at[c % 8], self.target(c), self.f_s.at[c], self.f_r.at[c], self.beside
+        )
+
+    def f_own(self, c):
+        return pltpu.make_async_copy(self.done_v.at[c % 8], self.target(c), self.f_l.at[c])
+
+    def step_zero(self, c):
+        self.local_copy(c).start()
+        self.core_copy(c).start()
+
+    def step_core(self, c):
+        self.local_copy(c).wait()
+        self.core_copy(c).wait()
+        own, came = self.own_v.at[c % 2], self.core_v.at[c % 4]
+        self.first_v[c % 3] = own[0].astype(F32) + came[0].astype(F32)
+        self.across_v[c % 3] = (own[1].astype(F32) + came[1].astype(F32)).astype(BF16)
+        self.x_copy(c).start()
+
+    def step_x(self, c):
+        self.x_copy(c).wait()
+        total = self.first_v[c % 3] + self.cross_v[c % 6].astype(F32)
+        left, right = total[:, : self.half], total[:, self.half :]
+        self.keep_v[c % 3] = jnp.where(self.low == 0, left, right)
+        self.give_v[c % 3] = jnp.where(self.low == 0, right, left).astype(BF16)
+        self.y_copy(c).start()
+
+    def step_y(self, c):
+        self.y_copy(c).wait()
+        total = self.keep_v[c % 3] + self.half_v[c % 6].astype(F32)
+        self.sum_v[c % 3] = total
+        self.slab_v[c % 3] = total.astype(BF16)
+        for step in range(1, self.group):
+            self.z_copy(c, step).start()
+
+    def step_z(self, c):
+        total = self.sum_v[c % 3, self.own_rows(), :]
+        for step in range(1, self.group):
+            self.z_copy(c, step).wait()
+            total = total + self.piece_v[c % 6, step - 1].astype(F32)
+        self.done_v[c % 8, self.own_rows(), :] = total.astype(BF16)
+        for step in range(1, self.group):
+            self.g_copy(c, step).start()
+
+    def step_gather(self, c):
+        for step in range(1, self.group):
+            self.g_copy(c, step).wait()
+        self.f_copy(c).start()
+        self.f_own(c).start()
+
+    def step_end(self, c):
+        self.f_own(c).wait()
+        self.f_copy(c).wait()
+
+    def slot(self, at):
+        for stage, delay in self.stages:
+            c = at - delay
+            if isinstance(c, int):
+                if 0 <= c < self.count:
+                    stage(c)
+            else:
+                pl.when((c >= 0) & (c < self.count))(functools.partial(stage, c))
+
+
+def reducer_scratch(count, group, width):
+    vmem, dma = pltpu.VMEM, pltpu.SemaphoreType.DMA
+    half, piece, rows = width // 2, CHUNK // group, CHUNK
+    bufs = [
+        vmem((2, 2, rows, width), BF16),
+        vmem((4, 2, rows, width), BF16),
+        vmem((3, rows, width), BF16),
+        vmem((6, rows, width), BF16),
+        vmem((3, rows, width), F32),
+        vmem((3, rows, half), BF16),
+        vmem((6, rows, half), BF16),
+        vmem((3, rows, half), F32),
+        vmem((6, group - 1, piece, half), BF16),
+        vmem((3, rows, half), BF16),
+        vmem((3, rows, half), F32),
+        vmem((8, rows, half), BF16),
     ]
-    feed = reduce_parts(feed_parts)
-    grad_normed = product_right_t(grad_pre_low, up) + grad_middle
-    grad_resid, gain_one, shift_one = norm_backward(grad_normed, unit_one, inverse_one, gains[0])
-    bias_out = jnp.sum(grad_resid, axis=0)
-    grad_resid_low = grad_resid.astype(BF16)
-    grad_w_out = product_left_t(mixed, grad_resid_low)
-    grad_mixed = product_right_t(grad_resid_low, out).astype(BF16)
-    grad_q_low, grad_k_low, grad_v_low, small = attend_backward(
-        queries, keys, values, pooled_k, pooled_v, grad_mixed, lse, first, past, keep, conv
-    )
-    entry = entry_wide[LEFT : LEFT + total]
-    w_q = product_left_t(grad_q_low, entry)
-    w_k = product_left_t(grad_k_low, entry_wide)
-    w_v = product_left_t(grad_v_low, entry_wide)
-    rest_parts = [
-        jnp.concatenate(pieces, axis=0)
-        for pieces in zip(*(split_rows(piece) for piece in (grad_w_out, w_q, w_k, w_v)))
-    ]
-    rest = reduce_parts(rest_parts)
-    wide_grad = product_right_t(grad_k_low, qkv[1]) + product_right_t(grad_v_low, qkv[2])
-    from_right = shift(wide_grad[LEFT - LEFT_SENT : LEFT].astype(BF16), -1).astype(F32)
-    from_left = shift(wide_grad[LEFT + total :].astype(BF16), 1).astype(F32)
-    grad_hidden = (
-        product_right_t(grad_q_low, qkv[0])
-        + wide_grad[LEFT : LEFT + total]
-        + grad_resid
-        + jnp.pad(from_right, ((total - LEFT_SENT, 0), (0, 0)))
-        + jnp.pad(from_left, ((0, total - RIGHT), (0, 0)))
-    )
-    grad_b_up_rows = grad_b_up.reshape(4, -1, width // 4).transpose(1, 0, 2).reshape(-1, width)
-    small_split = jnp.concatenate([small[:14], grad_b_up_rows], axis=0)
-    small_whole = jnp.stack([gain_one, gain_two, bias_out, shift_one, bias_down, shift_two])
-    return grad_hidden, feed, rest, small_split, small_whole
-
-
-def to_absolute(rows):
-    quarter = rows.shape[1] // 4
-    parts = [rows[:, k * quarter : (k + 1) * quarter] for k in range(4)]
-    place = lax.axis_index("mp")
-    odd, high = place % 2 == 1, place // 2 == 1
-    parts = [jnp.where(odd, parts[k ^ 1], parts[k]) for k in range(4)]
-    parts = [jnp.where(high, parts[k ^ 2], parts[k]) for k in range(4)]
-    return jnp.concatenate(parts, axis=1)
+    sems = [dma((2,))] + [dma((count,))] * 6 + [dma((count, group - 1))] * 4 + [dma((count,))] * 3
+    return bufs, sems
+
+
+LAYER_NAMES = (
+    "act", "slope", "normed", "unit_one", "unit_two", "mixed", "q", "k", "v", "pooled_k",
+    "pooled_v", "entry", "down", "up", "out", "qkv",
+)
+LOCAL_NAMES = ("inverse_one", "inverse_two", "lse")
+
+
+def backward_kernel(group, count, *refs):
+    refs = list(refs)
+    take = lambda n: [refs.pop(0) for _ in range(n)]
+    cot_ref, gains_ref, conv_ref, first_ref, past_ref, keep_ref = take(6)
+    layers = []
+    for _ in range(LAYERS):
+        names = LAYER_NAMES + LOCAL_NAMES
+        layers.append(dict(zip(names, take(len(names)))))
+    sums_ref, grad_in_ref, parts_ref = take(3)
+    bufs, sems = take(12), take(14)
+    (g_ref, gm_ref, gr_low, gmix_ref, send_left, send_right, from_right, from_left,
+     split_ref, up_ref, whole_ref, load_s, halo_s, store_s, out_s) = take(15)
+    total, width = g_ref.shape
+    place, seat = lax.axis_index("seq"), lax.axis_index("mp")
+    seqs = lax.axis_size("seq")
+    red = Reducer(group, count, parts_ref, sums_ref, bufs, sems)
+    ahead = seat_of(seq=(place + (seat + 1) // 4) % seqs, mp=(seat + 1) % 4)
+    behind = seat_of(seq=(place + seqs - (3 - seat + 1) // 4) % seqs, mp=(seat + 3) % 4)
+    barrier = pltpu.get_barrier_semaphore()
+    devices = [red.core, red.across, red.beside, ahead, behind] + red.others
+    for device in devices:
+        pl.semaphore_signal(barrier, inc=1, device_id=device, device_id_type=MESH)
+    pl.semaphore_wait(barrier, len(devices))
+
+    split_ref[...] = jnp.zeros_like(split_ref)
+    up_ref[...] = jnp.zeros_like(up_ref)
+    whole_ref[...] = jnp.zeros_like(whole_ref)
+    quarter = width // 4
+    feed = 4 * width
+
+    def load(source, target, index):
+        copy = pltpu.make_async_copy(source, target, load_s.at[index])
+        copy.start()
+        return copy
+
+    def place_of(part):
+        return (part % 2) * 2 + part // 2
+
+    def norm_back(layer, grad, unit, inverse, gain, result, low_ref, rows_at):
+        gain_row, shift_row, bias_row = rows_at
+
+        @pl.loop(0, total // NORM_ROWS)
+        def _(block):
+            rows = pl.ds(pl.multiple_of(block * NORM_ROWS, NORM_ROWS), NORM_ROWS)
+            g, n = grad[rows, :], unit[rows, :]
+            a = g * gain
+            mean = jnp.sum(a, axis=1, keepdims=True) * (1.0 / width)
+            tilt = jnp.sum(a * n, axis=1, keepdims=True) * (1.0 / width)
+            back = (a - mean - n * tilt) * inverse[rows, :]
+            result[rows, :] = back
+            low_ref[rows, :] = back.astype(BF16)
+            for at, value in ((gain_row, g * n), (shift_row, g), (bias_row, back)):
+                whole_ref[layer, at : at + 1, :] += jnp.sum(value, axis=0, keepdims=True)
+
+    def feed_scope(layer, base, ticks, down, up, act, slope, normed, unit_one, unit_two, out, mixed,
+                   gm_low, gn_ref, stage, wide_out):
+        ref = layers[layer]
+        pairs = ((ref["unit_two"], unit_two), (ref["down"], down), (ref["slope"], slope),
+                 (ref["act"], act), (ref["normed"], normed), (ref["up"], up),
+                 (ref["unit_one"], unit_one), (ref["out"], out), (ref["mixed"], mixed))
+        copies = [load(a, b, i) for i, (a, b) in enumerate(pairs)]
+        copies[0].wait()
+        norm_back(layer, g_ref, unit_two, ref["inverse_two"], gains_ref[layer, 1:2, :], gm_ref,
+                  gm_low, (1, 5, 4))
+        gn_ref[...] = gm_ref[...]
+        for copy in copies[1:6]:
+            copy.wait()
+        ticks()
+        stores = []
+        for j in range(3):
+            for copy in stores:
+                copy.wait()
+
+            @pl.loop(0, 4)
+            def _(part):
+                at = pl.multiple_of(part * width + j * CHUNK, CHUNK)
+                cols = pl.ds(at, CHUNK)
+                pos = place_of(part)
+                ga = product_right_t(gm_low[...], down[cols, :])
+                gp = ga * slope[:, cols].astype(F32)
+                up_ref[layer, pl.ds(part, 1), j * CHUNK : (j + 1) * CHUNK] = jnp.sum(
+                    gp, axis=0, keepdims=True
+                )
+                gp_low = gp.astype(BF16)
+                stage[0, pos] = product_left_t(act[:, cols], gm_low[...]).astype(BF16)
+                stage[1, pos] = product_left_t(gp_low, normed[...]).astype(BF16)
+                gn_ref[...] += product_right_t(gp_low, up[:, cols])
+
+            stores = []
+            for kind in range(2):
+                at = base + kind * width + j * CHUNK
+                copy = pltpu.make_async_copy(
+                    stage.at[kind], parts_ref.at[:, pl.ds(at, CHUNK)], store_s.at[kind]
+                )
+                copy.start()
+                stores.append(copy)
+            ticks()
+        for copy in copies[6:]:
+            copy.wait()
+        norm_back(layer, gn_ref, unit_one, ref["inverse_one"], gains_ref[layer, 0:1, :], gm_ref,
+                  gr_low, (0, 3, 2))
+        gmix_ref[...] = product_right_t(gr_low[...], out[...]).astype(BF16)
+        wide_out[...] = product_left_t(mixed[...], gr_low[...]).astype(BF16)
+        for copy in stores:
+            copy.wait()
+        store_parts(wide_out, base + 2 * width, 0)
+        ticks()
+
+    def part_copies(source, at, bank):
+        return [
+            pltpu.make_async_copy(
+                source.at[pl.ds(part * quarter, quarter)],
+                parts_ref.at[place_of(part), pl.ds(at, quarter)],
+                out_s.at[bank, part],
+            )
+            for part in range(4)
+        ]
+
+    def store_parts(source, at, bank):
+        copies = part_copies(source, at, bank)
+        for copy in copies:
+            copy.start()
+        for copy in copies:
+            copy.wait()
+
+    def attend_scope(layer, slot_of, grad_q, grad_k, grad_v, q, k, v, pooled_k, pooled_v,
+                     wide_k, wide_v, far_k, far_v, wide_f32):
+        ref = layers[layer]
+        names = ("q", "k", "v", "pooled_k", "pooled_v")
+        copies = [load(ref[n], b, i) for i, (n, b) in enumerate(zip(names, (q, k, v, pooled_k, pooled_v)))]
+        for copy in copies:
+            copy.wait()
+        attend_backward_body(
+            q, k, v, pooled_k, pooled_v, gmix_ref, ref["lse"], first_ref, past_ref, keep_ref,
+            conv_ref.at[layer], grad_q, grad_k, grad_v, split_ref.at[layer],
+            wide_k, wide_v, far_k, far_v, wide_f32, slot_of,
+        )
+
+    def project_scope(layer, base, last, grad_q, grad_k, grad_v, qkv, entry, wide, full):
+        ref = layers[layer]
+        copies = [load(ref["qkv"], qkv, 0), load(ref["entry"], entry, 1)]
+        for copy in copies:
+            copy.wait()
+        wide[...] = product_right_t(grad_k[...], qkv[1])
+        wide[...] += product_right_t(grad_v[...], qkv[2])
+        send_left[...] = wide[LEFT - LEFT_SENT : LEFT, :].astype(BF16)
+        send_right[...] = wide[LEFT + total :, :].astype(BF16)
+        halo = [
+            red.remote(send_left, from_right, halo_s.at[layer, 0], halo_s.at[layer, 1], behind),
+            red.remote(send_right, from_left, halo_s.at[layer, 2], halo_s.at[layer, 3], ahead),
+        ]
+        for copy in halo:
+            copy.start()
+        own = slice(LEFT, LEFT + total)
+        gm_ref[...] += wide[own, :]
+        gm_ref[...] += product_right_t(grad_q[...], qkv[0])
+        banks = []
+        for which, (grad, rows) in enumerate(((grad_q, own), (grad_k, slice(None)), (grad_v, slice(None)))):
+            bank = which % 2
+            if which >= 2:
+                for copy in banks[which - 2]:
+                    copy.wait()
+            full[bank] = product_left_t(grad[...], entry[rows, :]).astype(BF16)
+            copies = part_copies(full.at[bank], base + 2 * width + (which + 1) * quarter, bank)
+            for copy in copies:
+                copy.start()
+            banks.append(copies)
+        for copies in banks[1:]:
+            for copy in copies:
+                copy.wait()
+        for copy in halo:
+            copy.wait()
+        index = place * 4 + seat
+        right = jnp.where(index == 4 * seqs - 1, 0.0, 1.0)
+        left = jnp.where(index == 0, 0.0, 1.0)
+        gm_ref[total - LEFT_SENT :, :] += from_right[...].astype(F32) * right
+        gm_ref[:RIGHT, :] += from_left[...].astype(F32) * left
+
+    slots = [0]
+    state = {"next": 0}
+
+    def tick(limit):
+        def run():
+            if state["next"] < limit:
+                red.slot(state["next"])
+                state["next"] += 1
+        return run
+
+    def loop_ticks(number):
+        begin = state["next"]
+        state["next"] += number
+        return lambda step: red.slot(begin + step)
+
+    start = load(cot_ref, gr_low, 0)
+    start.wait()
+    g_ref[...] = gr_low[...].astype(F32)
+    vmem = pltpu.VMEM
+    block = (total, width)
+    wide_rows = total + LEFT + RIGHT
+    far_rows = total // 4 + 2 * POOL_REACH
+    pairs = width // PAIR
+    for turn, layer in enumerate(reversed(range(LAYERS))):
+        base = turn * LAYER_ROWS
+        state["calls"] = 0
+
+        def ticks():
+            state["calls"] += 1
+            if turn > 0 or state["calls"] >= 4:
+                tick(count)()
+
+        pl.run_scoped(
+            functools.partial(feed_scope, layer, base, ticks),
+            vmem((feed, width), BF16), vmem((width, feed), BF16), vmem((total, feed), BF16),
+            vmem((total, feed), BF16), vmem(block, BF16), vmem(block, F32), vmem(block, F32),
+            vmem((width, width), BF16), vmem(block, BF16), vmem(block, BF16), vmem(block, F32),
+            vmem((2, 4, CHUNK, width), BF16), vmem((width, width), BF16),
+        )
+
+        def attention(grad_q, grad_k, grad_v):
+            pl.run_scoped(
+                functools.partial(attend_scope, layer, loop_ticks(total // TILE), grad_q, grad_k, grad_v),
+                vmem(block, BF16), vmem((wide_rows, width), BF16), vmem((wide_rows, width), BF16),
+                vmem((far_rows, width), BF16), vmem((far_rows, width), BF16),
+                vmem((pairs, wide_rows, PAIR), F32), vmem((pairs, wide_rows, PAIR), F32),
+                vmem((far_rows, width), F32), vmem((far_rows, width), F32),
+                vmem((wide_rows, PAIR), F32),
+            )
+            pl.run_scoped(
+                functools.partial(project_scope, layer, base, turn == LAYERS - 1, grad_q, grad_k, grad_v),
+                vmem((3, width, width), BF16), vmem((wide_rows, width), BF16),
+                vmem((wide_rows, width), F32), vmem((2, width, width), BF16),
+            )
+
+        pl.run_scoped(
+            attention, vmem(block, BF16), vmem((wide_rows, width), BF16), vmem((wide_rows, width), BF16)
+        )
+        g_ref[...] = gm_ref[...]
+
+    final = pltpu.make_async_copy(g_ref, grad_in_ref, load_s.at[0])
+    final.start()
+
+    def small_scope(stage):
+        stage[...] = jnp.zeros_like(stage)
+        for layer in range(LAYERS):
+            at = 32 * layer
+            for part in range(4):
+                pos = place_of(part)
+                rolled = split_ref[layer]
+                if part:
+                    rolled = pltpu.roll(rolled, width - part * quarter, 1)
+                stage[pos, at : at + 16, :] = rolled.astype(BF16)
+                rest = jnp.concatenate([whole_ref[layer], up_ref[layer, part : part + 1, :]] + [jnp.zeros((7, width), F32)], axis=0)
+                stage[pos, at + 16 : at + 32, :] = rest.astype(BF16)
+        copy = pltpu.make_async_copy(
+            stage, parts_ref.at[:, pl.ds(LAYERS * LAYER_ROWS, SMALL_ROWS)], store_s.at[0]
+        )
+        copy.start()
+        copy.wait()
+
+    pl.run_scoped(small_scope, vmem((4, SMALL_ROWS, width), BF16))
+
+    @pl.loop(state["next"], count + red.last)
+    def _(at):
+        red.slot(at)
+
+    final.wait()
+
+
+def backward(cot, gains, conv, first, past, keep, saved):
+    total, width = cot.shape
+    group = lax.axis_size("seq") // 2
+    rows = LAYERS * LAYER_ROWS + SMALL_ROWS
+    count = rows // CHUNK
+    vmem, dma = pltpu.VMEM, pltpu.SemaphoreType.DMA
+    anywhere = pl.BlockSpec(memory_space=pl.ANY)
+    local = pl.BlockSpec(memory_space=pltpu.VMEM)
+    args = [cot, gains, conv, first, past, keep]
+    specs = [anywhere] + [local] * 5
+    for layer in saved:
+        args += [layer[name] for name in LAYER_NAMES + LOCAL_NAMES]
+        specs += [anywhere] * len(LAYER_NAMES) + [local] * len(LOCAL_NAMES)
+    bufs, sems = reducer_scratch(count, group, width)
+    shape = jax.ShapeDtypeStruct
+    return pl.pallas_call(
+        functools.partial(backward_kernel, group, count),
+        out_shape=(
+            shape((rows, width), BF16),
+            shape((total, width), F32),
+            shape((4, rows, width), BF16),
+        ),
+        in_specs=specs,
+        out_specs=(anywhere,) * 3,
+        scratch_shapes=bufs + sems + [
+            vmem((total, width), F32),
+            vmem((total, width), F32),
+            vmem((total, width), BF16),
+            vmem((total, width), BF16),
+            vmem((LEFT_SENT, width), BF16),
+            vmem((RIGHT, width), BF16),
+            vmem((LEFT_SENT, width), BF16),
+            vmem((RIGHT, width), BF16),
+            vmem((LAYERS, 16, width), F32),
+            vmem((LAYERS, 8, width), F32),
+            vmem((LAYERS, 8, width), F32),
+            dma((9,)),
+            dma((LAYERS, 4)),
+            dma((2,)),
+            dma((2, 4)),
+        ],
+        compiler_params=pltpu.CompilerParams(
+            collective_id=0, has_side_effects=True, vmem_limit_bytes=60 * 1024 * 1024
+        ),
+        name="backward",
+    )(*args)
 
 
 def shards(
@@ -528,33 +873,32 @@
             shared_biases[index],
         )
         hidden, saved = layer_forward(hidden, masks, weights)
-        stack.append((weights, saved))
-    gradient = cotangent.astype(F32)
-    collected = [None] * LAYERS
-    for index in reversed(range(LAYERS)):
-        weights, saved = stack[index]
-        gradient, feed, rest, split, whole = layer_backward(gradient, masks, weights, saved)
-        collected[index] = (feed, rest, split, whole)
-    feed = jnp.stack([part[0] for part in collected]).astype(F32)
-    rest = jnp.stack([part[1] for part in collected]).astype(F32)
-    small_split = jnp.stack([to_absolute(part[2]) for part in collected])
-    small_whole = jnp.stack([part[3] for part in collected])
-    small_total = lax.psum(jnp.concatenate([small_split, small_whole], axis=1), BOTH)
-    own_small = lax.dynamic_slice_in_dim(small_total[:, :18], place * quarter, quarter, 2)
+        stack.append(saved)
+    sums, gradient, _ = backward(
+        cotangent, norm_gains, conv_all, near_bounds[0], near_bounds[1], keep, stack
+    )
+    sums = sums.astype(F32)
+    per_layer = sums[: LAYERS * LAYER_ROWS].reshape(LAYERS, LAYER_ROWS, width)
+    per_layer = jnp.stack([per_layer[1], per_layer[0]])
+    small = sums[LAYERS * LAYER_ROWS :][: 32 * LAYERS].reshape(LAYERS, 32, width)
     units = down_weight.shape[1]
+    grad_down = per_layer[:, :units]
+    grad_up = per_layer[:, units : 2 * units].transpose(0, 2, 1)
+    rest = per_layer[:, 2 * units :].reshape(LAYERS, 4, quarter, width)
+    split = small[:, :14, :quarter]
     return (
         hidden,
         gradient,
-        rest[:, quarter:].reshape(2, 3, quarter, width).transpose(0, 1, 3, 2),
-        own_small[:, :2],
-        own_small[:, 2:12].reshape(2, 2, 5, quarter),
-        own_small[:, 12:14],
-        rest[:, :quarter],
-        feed[:, units:].transpose(0, 2, 1),
-        own_small[:, 14:18].reshape(2, -1),
-        feed[:, :units],
-        small_total[:, 18:20],
-        small_total[:, 20:24],
+        rest[:, 1:].transpose(0, 1, 3, 2),
+        split[:, :2],
+        split[:, 2:12].reshape(LAYERS, 2, 5, quarter),
+        split[:, 12:14],
+        rest[:, 0],
+        grad_up,
+        small[:, 24],
+        grad_down,
+        small[:, 16:18],
+        small[:, 18:22],
     )
 
 

time: 842 us -> 602 us (0.71)
  waiting for transfers between devices: 288 us -> 38.7 us
  Pallas kernels: 71.7 us -> 309 us
  matrix products: 169 us -> 61.3 us
  starting transfers between devices: 116 us -> 51.3 us
  local copies, waits for them, and re-layouts: 101 us -> 69.2 us
  between operations: 16.5 us -> 1.72 us
  other arithmetic: 76 us -> 64.6 us
    pallas_call x2 -> x1, Pallas kernels: 39.7 us -> 277 us  [backward(): pl.pallas_call(functools.partial(backward_kernel, group, count), out_shap...]
    ppermute x59 -> x27, waiting for transfers between devices: 218 us -> 38.6 us  [swap(): return lax.ppermute(values, axis, [(i, i ^ bit) for i in range(count)])]
    dot_general x24 -> x0, matrix products: 114 us -> none  [the longest x12 72.4 us: product_right_t(): lax.dot_general(left, right, (((1,), (1,)), ((), ())), preferred_element_...]
    psum x1 -> x0, waiting for transfers between devices: 69.6 us -> none  [shards(): lax.psum(jnp.concatenate([small_split, small_whole], axis=1), BOTH)]
    ppermute x59 -> x27, starting transfers between devices: 87.9 us -> 34.9 us  [swap(): return lax.ppermute(values, axis, [(i, i ^ bit) for i in range(count)])]
    split x24 -> x0, local copies, waits for them, and re-layouts: 30.8 us -> none  [split_rows(): return jnp.split(values, 4, axis=0)]
    concatenate x1 -> x7, other arithmetic: 1.43 us -> 29.1 us  [the longest x2 11.7 us: shards(): down = jnp.concatenate(gather_parts(down_weight[index]), axis=0)]
    add x12 -> x1, other arithmetic: 19.9 us -> 1.99 us  [norm_forward(): return (unit * gain + offset, unit, inverse)]
  transfers between devices with their start and end apart: 68 -> 31, of which waited for: 19 -> 5; matrix products, arithmetic and copies ran while one was open for 31% -> 18% of each run, Pallas kernels for 6% -> 3%
where the time goes in v3:
time: 602 us; the launch traced here: 595 us
  Pallas kernels  309 us (51%)
  local copies, waits for them, and re-layouts  69.2 us (11%)
  other arithmetic  64.6 us (11%)
  matrix products  61.3 us (10%)
  starting transfers between devices  51.3 us (9%)
  waiting for transfers between devices  38.7 us (6%)
    pallas_call x1, Pallas kernels, backward(): pl.pallas_call(functools.partial(backward_kernel, group, count), out_shap...  277 us
    dot_general x12, matrix products, product(): return jnp.dot(left, right, preferred_element_type=F32)  61.3 us
    ppermute x27, waiting for transfers between devices, swap(): return lax.ppermute(values, axis, [(i, i ^ bit) for i in range(count)])  38.6 us
    ppermute x27, starting transfers between devices, swap(): return lax.ppermute(values, axis, [(i, i ^ bit) for i in range(count)])  34.9 us
    pallas_call x2, Pallas kernels, attend_forward(): pl.pallas_call(attend_forward_kernel, out_shape=(shape((total, width), BF...  32 us
    ppermute x4, starting transfers between devices, shift(): lax.ppermute(values, BOTH, [(i, i + step) for i in range(count) if 0 <= i...  16.4 us
    unnamed x119, local copies, waits for them, and re-layouts  13.6 us
  transfers between devices with their start and end apart: 31, of which 5 were waited for; matrix products, arithmetic and copies ran while one was open for 18% of the time, Pallas kernels for 3%

profile of v3, /device:TPU:15, one launch (start us, length us, event | category | flops | bytes accessed | tf_op | source)
XLA Modules:
  0.0 595.4 jit_solution(7920069041590944419)
XLA Ops:
  7.5 3.0 fusion.28
  11.9 3.3 slice_bitcast_fusion.27
  15.3 1.6 slice_bitcast_fusion.26
  29.7 10.2 %collective-permute-done.23 = bf16[192,768]{1,0:T(8,128)(2,1)S(1)} collective-permute-done((bf16[192,768]{1,0:T(8,128)(2,1)S(1)}, bf16[192,768]{1,0:T(8,128)(2,1)S(1)}, u32[]{:S(2)}, u32[]{:S(2)}) %collective-permute-start.23) | collective-permute-done | bytes 294944 | tf_op jit(solution)/shard_map/ppermute | solution.py:37
  43.4 1.9 collective-permute-done.24
  51.2 2.3 pad_maximum_fusion.9.refs_20_
  53.5 2.2 pad_maximum_fusion.10.refs_39_
  59.2 1.4 collective-permute-done.18
  60.7 4.8 collective-permute-start.7
  65.5 2.3 copy.92
  67.8 4.2 collective-permute-start.6
  73.5 2.3 copy.84
  75.8 4.0 pad_maximum_fusion.5.refs_21_
  79.8 2.0 fusion.24.q_ref.refs_12_
  81.8 19.0 %collective-permute-start.14 = (bf16[768,768]{1,0:T(8,128)(2,1)}, bf16[768,768]{1,0:T(8,128)(2,1)}, u32[]{:S(2)}, u32[]{:S(2)}) collective-permute-start(bf16[768,768]{1,0:T(8,128)(2,1)} %get-tuple-element.128), channel_id=1, source_target_pairs={{0,1},{1,0},{2,3},{3,2},{4,5},{5,4},{6,7},{7,6},{8,9},{9,8},{10,11... | collective-permute-start | bytes 3538952 | tf_op jit(solution)/shard_map/ppermute | solution.py:37
  101.3 3.9 convolution_convert_fusion.1.k_ref.refs_13_
  105.2 3.8 add_convert_fusion.1.v_ref.refs_14_
  109.0 16.0 %attend_forward.2 = (bf16[512,768]{1,0:T(8,128)(2,1)}, f32[4,6,256]{2,1,0:T(8,128)}, bf16[256,768]{1,0:T(8,128)(2,1)}, bf16[256,768]{1,0:T(8,128)(2,1)}) custom-call(bf16[512,768]{1,0:T(8,128)(2,1)} %fusion.24.q_ref.refs_12_, bf16[1088,768]{1,0:T(8,128)(2,1)} %convolution_convert_fusion.1.k_ref.refs_13_, bf16[1088,768]{1,0:T(8,128)(2,1)} %add_convert_fusion.1.v_ref.refs_14_, ...), custom_call_target="tpu_custom_call" | custom-call | tf_op jit(solution)/shard_map/attend_forward/pallas_call | solution.py:256
  125.0 2.3 fusion.32
  129.6 1.6 collective-permute-start.26
  131.2 2.3 copy.93
  133.5 4.5 pad_maximum_fusion.6.refs_40_
  139.4 3.8 pad_maximum_fusion.1.refs_19_
  143.2 12.2 %fusion.4 = (bf16[512,3072]{1,0:T(8,128)(2,1)}, bf16[512,3072]{1,0:T(8,128)(2,1)S(1)}) fusion(f32[3072]{0:T(1024)S(1)} %bitcast.107, bf16[512,768]{1,0:T(8,128)(2,1)S(1)} %get-tuple-element.116.refs_8_, bf16[768,3072]{1,0:T(8,128)(2,1)S(1)} %pad_maximum_fusion.1.refs_19_), kind=kOutput, calls=%fused_computation.14 | convolution fusion | flops 2477260800 | bytes 11808768 | tf_op jit(solution)/shard_map/dot_general | solution.py:24
  157.5 1.5 collective-permute-start.27
  159.0 23.8 %collective-permute-done.29 = bf16[768,768]{1,0:T(8,128)(2,1)} collective-permute-done((bf16[768,768]{1,0:T(8,128)(2,1)}, bf16[768,768]{1,0:T(8,128)(2,1)}, u32[]{:S(2)}, u32[]{:S(2)}) %collective-permute-start.29) | collective-permute-done | bytes 1179680 | tf_op jit(solution)/shard_map/ppermute | solution.py:37
  183.7 5.5 fusion.33
  189.6 1.5 fusion.18
  192.9 1.9 collective-permute-start.21
  195.6 2.9 add_convert_fusion.2.q_ref.refs_31_
  198.6 4.9 pad_maximum_fusion.2.refs_18_
  203.5 5.4 collective-permute-start.20
  208.9 3.2 pad_maximum_fusion.3.refs_38_
  212.1 6.8 %pad_maximum_fusion.4.refs_37_ = bf16[3072,768]{1,0:T(8,128)(2,1)} fusion(bf16[768,768]{1,0:T(8,128)(2,1)} %collective-permute-done.30, bf16[768,768]{1,0:T(8,128)(2,1)} %collective-permute-done.29, bf16[768,768]{1,0:T(8,128)(2,1)} %collective-permute-done.28, bf16[768,768]{1,0:T(8,128)(2,1)} %get-tuple-element.127), kind=kLoop, calls=%fused_computation.37 | loop fusion | flops 18874368 | bytes 9437184 | tf_op jit(solution)/shard_map/concatenate | solution.py:852
  219.0 3.9 convolution_convert_fusion.k_ref.refs_32_
  222.9 3.7 add_convert_fusion.v_ref.refs_33_
  226.6 16.1 %attend_forward.3 = (bf16[512,768]{1,0:T(8,128)(2,1)}, f32[4,6,256]{2,1,0:T(8,128)}, bf16[256,768]{1,0:T(8,128)(2,1)}, bf16[256,768]{1,0:T(8,128)(2,1)}) custom-call(bf16[512,768]{1,0:T(8,128)(2,1)} %add_convert_fusion.2.q_ref.refs_31_, bf16[1088,768]{1,0:T(8,128)(2,1)} %convolution_convert_fusion.k_ref.refs_32_, ...), custom_call_target="tpu_custom_call" | custom-call | tf_op jit(solution)/shard_map/attend_forward/pallas_call | solution.py:256
  242.8 2.1 fusion.34
  245.6 12.2 %fusion.9 = (bf16[512,3072]{1,0:T(8,128)(2,1)}, bf16[512,3072]{1,0:T(8,128)(2,1)S(1)}) fusion(f32[3072]{0:T(1024)S(1)} %bitcast.106, bf16[512,768]{1,0:T(8,128)(2,1)S(1)} %get-tuple-element.112.refs_27_, bf16[768,3072]{1,0:T(8,128)(2,1)S(1)} %pad_maximum_fusion.3.refs_38_), kind=kOutput, calls=%fused_computation.19 | convolution fusion | flops 2477260800 | bytes 11808768 | tf_op jit(solution)/shard_map/dot_general | solution.py:24
  257.9 6.7 %fusion.35 = (f32[512]{0:T(512)S(1)}, f32[512,768]{1,0:T(8,128)S(1)}) fusion(f32[768]{0:T(1024)S(1)} %copy-done.52, bf16[512,3072]{1,0:T(8,128)(2,1)S(1)} %get-tuple-element.124.refs_25_, bf16[768,768]{1,0:T(8,128)(2,1)} %collective-permute-done.30, bf16[768,768]{1,0:T(8,128)(2,1)} %collective-permute-done.29, ...), kind=kOutput, calls=%fused_computation.144 | convolution fusion | flops 2436759040 | bytes 11021312 | tf_op jit(solution)/shard_map/dot_general | solution.py:24
  266.7 2.0 multiply_add_fusion.2
  268.7 5.9 pad_maximum_fusion.8
  274.6 276.6 %backward.1 = (bf16[4864,768]{1,0:T(8,128)(2,1)}, f32[512,768]{1,0:T(8,128)}, bf16[4,4864,768]{2,1,0:T(8,128)(2,1)}) custom-call(bf16[512,768]{1,0:T(8,128)(2,1)} %refs_0_.1, f32[2,2,768]{2,1,0:T(2,128)} %refs_1_.1, f32[2,2,5,768]{3,2,1,0:T(8,128)} %reshape.224.refs_2_, s32[4,1,128]{2,1,0:T(1,128)} %get-tuple-element.152.first_ref.refs_3_, ...), custom_call_target="tpu_custom_call" | custom-call | tf_op jit(solution)/shard_map/backward/pallas_call | solution.py:781
  551.2 9.6 %convert_element_type.66 = f32[4864,768]{1,0:T(8,128)} convert(bf16[4864,768]{1,0:T(8,128)(2,1)} %get-tuple-element.31) | non-fusion elementwise | flops 3735552 | bytes 22413312 | tf_op jit(solution)/shard_map/convert_element_type | solution.py:880
  562.3 10.9 %slice_bitcast_fusion = (f32[1,2304,768]{2,1,0:T(8,128)}, f32[1,2304,768]{2,1,0:T(8,128)}) fusion(f32[4864,768]{1,0:T(8,128)} %convert_element_type.66), kind=kLoop, calls=%fused_computation.8 | loop fusion | bytes 28311552 | tf_op jit(solution)/shard_map/slice | solution.py:882
  573.3 9.0 %pad_maximum_fusion = (f32[2,768,768]{2,1,0:T(8,128)}, f32[2,768,768]{2,1,0:T(8,128)S(1)}, f32[2,768,768]{1,2,0:T(8,128)}) fusion(f32[1,2304,768]{2,1,0:T(8,128)} %get-tuple-element.118, f32[1,2304,768]{2,1,0:T(8,128)} %get-tuple-element.119), kind=kLoop, calls=%fused_computation.33 | loop fusion | flops 3538944 | bytes 28311552 | tf_op jit(solution)/shard_map/stack | solution.py:882
  582.3 2.0 slice_bitcast_fusion.2
  587.2 6.2 %copy.101 = f32[2,768,768]{2,1,0:T(8,128)} copy(f32[2,768,768]{1,2,0:T(8,128)} %get-tuple-element.122) | data formatting | bytes 9437184
  (244 shorter events, 54.3 us)
Async XLA Ops:
  3.6 17.6 %collective-permute-start.4 = (f32[36,192]{1,0:T(8,128)S(1)}, f32[36,192]{1,0:T(8,128)S(1)}, u32[]{:S(2)}, u32[]{:S(2)}) collective-permute-start(f32[36,192]{1,0:T(8,128)S(1)} %pad_maximum_fusion.12), channel_id=1, source_target_pairs={{0,2},{1,3},{2,0},{3,1},{4,6},{5,7},{6,4},{7,5},{8,10},{9,11},{10,... | collective-permute-start | bytes 82952 | tf_op jit(solution)/shard_map/ppermute | solution.py:37
  3.9 22.8 %collective-permute-start.3 = (f32[36,192]{1,0:T(8,128)S(1)}, f32[36,192]{1,0:T(8,128)S(1)}, u32[]{:S(2)}, u32[]{:S(2)}) collective-permute-start(f32[36,192]{1,0:T(8,128)S(1)} %pad_maximum_fusion.12), channel_id=1, source_target_pairs={{0,1},{1,0},{2,3},{3,2},{4,5},{5,4},{6,7},{7,6},{8,9},{9,8},{10,11... | collective-permute-start | bytes 82952 | tf_op jit(solution)/shard_map/ppermute | solution.py:37
  5.9 45.2 %copy-start.25 = (bf16[192,768]{1,0:T(8,128)(2,1)}, bf16[192,768]{1,0:T(8,128)(2,1)S(1)}, u32[]{:S(2)}) copy-start(bf16[192,768]{1,0:T(8,128)(2,1)S(1)} %get-tuple-element.136) | copy-start | bytes 884740
  6.0 47.5 %copy-start.23 = (bf16[192,768]{1,0:T(8,128)(2,1)}, bf16[192,768]{1,0:T(8,128)(2,1)S(1)}, u32[]{:S(2)}) copy-start(bf16[192,768]{1,0:T(8,128)(2,1)S(1)} %get-tuple-element.135) | copy-start | bytes 884740
  6.0 22.2 %collective-permute-start.9 = (bf16[192,768]{1,0:T(8,128)(2,1)S(1)}, bf16[192,768]{1,0:T(8,128)(2,1)}, u32[]{:S(2)}, u32[]{:S(2)}) collective-permute-start(bf16[192,768]{1,0:T(8,128)(2,1)S(1)} %get-tuple-element.136), channel_id=1, source_target_pairs={{0,2},{1,3},{2,0},{3,1},{4,6},{5,7},{6,4},{7,5},{8,10},{9,11},{10,... | collective-permute-start | bytes 884744 | tf_op jit(solution)/shard_map/ppermute | solution.py:37
  7.2 22.1 %collective-permute-start.8 = (bf16[192,768]{1,0:T(8,128)(2,1)S(1)}, bf16[192,768]{1,0:T(8,128)(2,1)}, u32[]{:S(2)}, u32[]{:S(2)}) collective-permute-start(bf16[192,768]{1,0:T(8,128)(2,1)S(1)} %get-tuple-element.136), channel_id=1, source_target_pairs={{0,1},{1,0},{2,3},{3,2},{4,5},{5,4},{6,7},{7,6},{8,9},{9,8},{10,11... | collective-permute-start | bytes 884744 | tf_op jit(solution)/shard_map/ppermute | solution.py:37
  10.5 31.8 %collective-permute-start.1 = (bf16[3,768,192]{1,2,0:T(8,128)(2,1)}, bf16[3,768,192]{1,2,0:T(8,128)(2,1)S(1)}, u32[]{:S(2)}, u32[]{:S(2)}) collective-permute-start(bf16[3,768,192]{1,2,0:T(8,128)(2,1)} %get-tuple-element.132), channel_id=1, source_target_pairs={{0,2},{1,3},{2,0},{3,1},{4,6},{5,7},{6,4},{7,5},{8,10},{9,11},{10,... | collective-permute-start | bytes 2654216 | tf_op jit(solution)/shard_map/ppermute | solution.py:37
  16.9 25.9 %copy-start.35 = (f32[2,768]{1,0:T(2,128)S(1)}, f32[2,768]{1,0:T(2,128)}, u32[]{:S(2)}) copy-start(f32[2,768]{1,0:T(2,128)} %param.21) | copy-start | bytes 18436
  21.1 6.7 %collective-permute-start.5 = (f32[36,192]{1,0:T(8,128)S(1)}, f32[36,192]{1,0:T(8,128)S(1)}, u32[]{:S(2)}, u32[]{:S(2)}) collective-permute-start(f32[36,192]{1,0:T(8,128)S(1)} %collective-permute-done.4), channel_id=1, source_target_pairs={{0,1},{1,0},{2,3},{3,2},{4,5},{5,4},{6,7},{7,6},{8,9},{9,8},{10,11... | collective-permute-start | bytes 82952 | tf_op jit(solution)/shard_map/ppermute | solution.py:37
  26.7 13.3 %collective-permute-start.23 = (bf16[192,768]{1,0:T(8,128)(2,1)S(1)}, bf16[192,768]{1,0:T(8,128)(2,1)S(1)}, u32[]{:S(2)}, u32[]{:S(2)}) collective-permute-start(bf16[192,768]{1,0:T(8,128)(2,1)S(1)} %get-tuple-element.135), channel_id=1, source_target_pairs={{0,2},{1,3},{2,0},{3,1},{4,6},{5,7},{6,4},{7,5},{8,10},{9,11},{10,... | collective-permute-start | bytes 884744 | tf_op jit(solution)/shard_map/ppermute | solution.py:37
  27.9 13.3 %collective-permute-start.22 = (bf16[192,768]{1,0:T(8,128)(2,1)S(1)}, bf16[192,768]{1,0:T(8,128)(2,1)}, u32[]{:S(2)}, u32[]{:S(2)}) collective-permute-start(bf16[192,768]{1,0:T(8,128)(2,1)S(1)} %get-tuple-element.135), channel_id=1, source_target_pairs={{0,1},{1,0},{2,3},{3,2},{4,5},{5,4},{6,7},{7,6},{8,9},{9,8},{10,11... | collective-permute-start | bytes 884744 | tf_op jit(solution)/shard_map/ppermute | solution.py:37
  28.2 14.1 %collective-permute-start.10 = (bf16[192,768]{1,0:T(8,128)(2,1)}, bf16[192,768]{1,0:T(8,128)(2,1)}, u32[]{:S(2)}, u32[]{:S(2)}) collective-permute-start(bf16[192,768]{1,0:T(8,128)(2,1)} %collective-permute-done.9), channel_id=1, source_target_pairs={{0,1},{1,0},{2,3},{3,2},{4,5},{5,4},{6,7},{7,6},{8,9},{9,8},{10,11... | collective-permute-start | bytes 884744 | tf_op jit(solution)/shard_map/ppermute | solution.py:37
  29.3 27.8 %collective-permute-start = (bf16[3,768,192]{1,2,0:T(8,128)(2,1)}, bf16[3,768,192]{1,2,0:T(8,128)(2,1)S(1)}, u32[]{:S(2)}, u32[]{:S(2)}) collective-permute-start(bf16[3,768,192]{1,2,0:T(8,128)(2,1)} %get-tuple-element.132), channel_id=1, source_target_pairs={{0,1},{1,0},{2,3},{3,2},{4,5},{5,4},{6,7},{7,6},{8,9},{9,8},{10,11... | collective-permute-start | bytes 2654216 | tf_op jit(solution)/shard_map/ppermute | solution.py:37
  40.0 20.7 %collective-permute-start.18 = (bf16[3,768,192]{1,2,0:T(8,128)(2,1)}, bf16[3,768,192]{1,2,0:T(8,128)(2,1)}, u32[]{:S(2)}, u32[]{:S(2)}) collective-permute-start(bf16[3,768,192]{1,2,0:T(8,128)(2,1)} %get-tuple-element.133), channel_id=1, source_target_pairs={{0,2},{1,3},{2,0},{3,1},{4,6},{5,7},{6,4},{7,5},{8,10},{9,11},{10,... | collective-permute-start | bytes 2654216 | tf_op jit(solution)/shard_map/ppermute | solution.py:37
  41.2 26.7 %collective-permute-start.17 = (bf16[3,768,192]{1,2,0:T(8,128)(2,1)}, bf16[3,768,192]{1,2,0:T(8,128)(2,1)S(1)}, u32[]{:S(2)}, u32[]{:S(2)}) collective-permute-start(bf16[3,768,192]{1,2,0:T(8,128)(2,1)} %get-tuple-element.133), channel_id=1, source_target_pairs={{0,1},{1,0},{2,3},{3,2},{4,5},{5,4},{6,7},{7,6},{8,9},{9,8},{10,11... | collective-permute-start | bytes 2654216 | tf_op jit(solution)/shard_map/ppermute | solution.py:37
  42.2 3.1 collective-permute-start.24
  42.3 31.1 %collective-permute-start.2 = (bf16[3,768,192]{1,2,0:T(8,128)(2,1)S(1)}, bf16[3,768,192]{1,2,0:T(8,128)(2,1)}, u32[]{:S(2)}, u32[]{:S(2)}) collective-permute-start(bf16[3,768,192]{1,2,0:T(8,128)(2,1)S(1)} %collective-permute-done.1), channel_id=1, source_target_pairs={{0,1},{1,0},{2,3},{3,2},{4,5},{5,4},{6,7},{7,6},{8,9},{9,8},{10,11... | collective-permute-start | bytes 2654216 | tf_op jit(solution)/shard_map/ppermute | solution.py:37
  45.3 55.5 %collective-permute-start.12 = (bf16[768,768]{1,0:T(8,128)(2,1)}, bf16[768,768]{1,0:T(8,128)(2,1)}, u32[]{:S(2)}, u32[]{:S(2)}) collective-permute-start(bf16[768,768]{1,0:T(8,128)(2,1)} %get-tuple-element.130), channel_id=1, source_target_pairs={{0,2},{1,3},{2,0},{3,1},{4,6},{5,7},{6,4},{7,5},{8,10},{9,11},{10,... | collective-permute-start | bytes 3538952 | tf_op jit(solution)/shard_map/ppermute | solution.py:37
  57.1 81.2 %collective-permute-start.11 = (bf16[768,768]{1,0:T(8,128)(2,1)}, bf16[768,768]{1,0:T(8,128)(2,1)}, u32[]{:S(2)}, u32[]{:S(2)}) collective-permute-start(bf16[768,768]{1,0:T(8,128)(2,1)} %get-tuple-element.130), channel_id=1, source_target_pairs={{0,1},{1,0},{2,3},{3,2},{4,5},{5,4},{6,7},{7,6},{8,9},{9,8},{10,11... | collective-permute-start | bytes 3538952 | tf_op jit(solution)/shard_map/ppermute | solution.py:37
  60.7 21.1 %collective-permute-start.7 = (bf16[256,768]{1,0:T(8,128)(2,1)}, bf16[256,768]{1,0:T(8,128)(2,1)}, u32[]{:S(2)}, u32[]{:S(2)}) collective-permute-start(bf16[256,768]{1,0:T(8,128)(2,1)} %slice.287), channel_id=1, source_target_pairs={{1,0},{2,1},{3,2},{4,3},{5,4},{6,5},{7,6},{8,7},{9,8},{10,9},{11,1... | collective-permute-start | bytes 1179656 | tf_op jit(solution)/shard_map/ppermute | solution.py:42
  67.8 33.0 %collective-permute-start.6 = (bf16[272,768]{1,0:T(8,128)(2,1)}, bf16[272,768]{1,0:T(8,128)(2,1)}, u32[]{:S(2)}, u32[]{:S(2)}) collective-permute-start(bf16[272,768]{1,0:T(8,128)(2,1)} %slice.286), channel_id=1, source_target_pairs={{0,1},{1,2},{2,3},{3,4},{4,5},{5,6},{6,7},{7,8},{8,9},{9,10},{10,1... | collective-permute-start | bytes 1253384 | tf_op jit(solution)/shard_map/ppermute | solution.py:42
  73.5 65.7 %collective-permute-start.15 = (bf16[768,768]{1,0:T(8,128)(2,1)}, bf16[768,768]{1,0:T(8,128)(2,1)}, u32[]{:S(2)}, u32[]{:S(2)}) collective-permute-start(bf16[768,768]{1,0:T(8,128)(2,1)} %get-tuple-element.128), channel_id=1, source_target_pairs={{0,2},{1,3},{2,0},{3,1},{4,6},{5,7},{6,4},{7,5},{8,10},{9,11},{10,... | collective-permute-start | bytes 3538952 | tf_op jit(solution)/shard_map/ppermute | solution.py:37
  79.7 25.4 %copy-start.2 = (bf16[3,768,768]{2,1,0:T(8,128)(2,1)}, bf16[3,768,768]{2,1,0:T(8,128)(2,1)S(1)}, u32[]{:S(2)}) copy-start(bf16[3,768,768]{2,1,0:T(8,128)(2,1)S(1)} %pad_maximum_fusion.5.refs_21_) | copy-start | bytes 10616836
  79.8 21.6 %copy-start.43 = (bf16[1088]{0:T(1024)(128)(2,1)S(1)}, bf16[1088]{0:T(1024)(128)(2,1)}, u32[]{:S(2)}) copy-start(bf16[1088]{0:T(1024)(128)(2,1)} %pad.52.clone) | copy-start | bytes 6532
  81.8 23.4 %copy-start.50 = (f32[768]{0:T(1024)S(1)}, f32[768]{0:T(1024)}, u32[]{:S(2)}) copy-start(f32[768]{0:T(1024)} %get-tuple-element.94) | copy-start | bytes 9220
  81.8 73.6 %collective-permute-start.14 = (bf16[768,768]{1,0:T(8,128)(2,1)}, bf16[768,768]{1,0:T(8,128)(2,1)}, u32[]{:S(2)}, u32[]{:S(2)}) collective-permute-start(bf16[768,768]{1,0:T(8,128)(2,1)} %get-tuple-element.128), channel_id=1, source_target_pairs={{0,1},{1,0},{2,3},{3,2},{4,5},{5,4},{6,7},{7,6},{8,9},{9,8},{10,11... | collective-permute-start | bytes 3538952 | tf_op jit(solution)/shard_map/ppermute | solution.py:37
  100.8 28.8 %collective-permute-start.19 = (bf16[3,768,192]{1,2,0:T(8,128)(2,1)}, bf16[3,768,192]{1,2,0:T(8,128)(2,1)}, u32[]{:S(2)}, u32[]{:S(2)}) collective-permute-start(bf16[3,768,192]{1,2,0:T(8,128)(2,1)} %collective-permute-done.18), channel_id=1, source_target_pairs={{0,1},{1,0},{2,3},{3,2},{4,5},{5,4},{6,7},{7,6},{8,9},{9,8},{10,11... | collective-permute-start | bytes 2654216 | tf_op jit(solution)/shard_map/ppermute | solution.py:37
  100.8 38.4 %collective-permute-start.13 = (bf16[768,768]{1,0:T(8,128)(2,1)}, bf16[768,768]{1,0:T(8,128)(2,1)}, u32[]{:S(2)}, u32[]{:S(2)}) collective-permute-start(bf16[768,768]{1,0:T(8,128)(2,1)} %collective-permute-done.12), channel_id=1, source_target_pairs={{0,1},{1,0},{2,3},{3,2},{4,5},{5,4},{6,7},{7,6},{8,9},{9,8},{10,11... | collective-permute-start | bytes 3538952 | tf_op jit(solution)/shard_map/ppermute | solution.py:37
  109.0 16.0 %copy-start.55 = (f32[768]{0:T(1024)S(1)}, f32[768]{0:T(1024)}, u32[]{:S(2)}) copy-start(f32[768]{0:T(1024)} %get-tuple-element.102) | copy-start | bytes 9220
  129.6 27.9 %collective-permute-start.26 = (bf16[768,768]{1,0:T(8,128)(2,1)}, bf16[768,768]{1,0:T(8,128)(2,1)}, u32[]{:S(2)}, u32[]{:S(2)}) collective-permute-start(bf16[768,768]{1,0:T(8,128)(2,1)} %get-tuple-element.129), channel_id=1, source_target_pairs={{0,2},{1,3},{2,0},{3,1},{4,6},{5,7},{6,4},{7,5},{8,10},{9,11},{10,... | collective-permute-start | bytes 3538952 | tf_op jit(solution)/shard_map/ppermute | solution.py:37
  138.0 84.9 %copy-start.3 = (bf16[3,768,768]{2,1,0:T(8,128)(2,1)}, bf16[3,768,768]{2,1,0:T(8,128)(2,1)S(1)}, u32[]{:S(2)}) copy-start(bf16[3,768,768]{2,1,0:T(8,128)(2,1)S(1)} %pad_maximum_fusion.6.refs_40_) | copy-start | bytes 10616836
  138.4 45.3 %copy-start.9 = (f32[512,768]{1,0:T(8,128)}, f32[512,768]{1,0:T(8,128)S(1)}, u32[]{:S(2)}) copy-start(f32[512,768]{1,0:T(8,128)S(1)} %get-tuple-element.117.refs_9_) | copy-start | bytes 4718596
  138.4 65.1 %collective-permute-start.25 = (bf16[768,768]{1,0:T(8,128)(2,1)}, bf16[768,768]{1,0:T(8,128)(2,1)}, u32[]{:S(2)}, u32[]{:S(2)}) collective-permute-start(bf16[768,768]{1,0:T(8,128)(2,1)} %get-tuple-element.129), channel_id=1, source_target_pairs={{0,1},{1,0},{2,3},{3,2},{4,5},{5,4},{6,7},{7,6},{8,9},{9,8},{10,11... | collective-permute-start | bytes 3538952 | tf_op jit(solution)/shard_map/ppermute | solution.py:37
  139.2 43.6 %collective-permute-start.29 = (bf16[768,768]{1,0:T(8,128)(2,1)}, bf16[768,768]{1,0:T(8,128)(2,1)}, u32[]{:S(2)}, u32[]{:S(2)}) collective-permute-start(bf16[768,768]{1,0:T(8,128)(2,1)} %get-tuple-element.127), channel_id=1, source_target_pairs={{0,2},{1,3},{2,0},{3,1},{4,6},{5,7},{6,4},{7,5},{8,10},{9,11},{10,... | collective-permute-start | bytes 3538952 | tf_op jit(solution)/shard_map/ppermute | solution.py:37
  139.2 44.5 %collective-permute-start.16 = (bf16[768,768]{1,0:T(8,128)(2,1)}, bf16[768,768]{1,0:T(8,128)(2,1)S(1)}, u32[]{:S(2)}, u32[]{:S(2)}) collective-permute-start(bf16[768,768]{1,0:T(8,128)(2,1)} %collective-permute-done.15), channel_id=1, source_target_pairs={{0,1},{1,0},{2,3},{3,2},{4,5},{5,4},{6,7},{7,6},{8,9},{9,8},{10,11... | collective-permute-start | bytes 3538952 | tf_op jit(solution)/shard_map/ppermute | solution.py:37
  143.2 40.5 %copy-start.54 = (f32[768]{0:T(1024)S(1)}, f32[768]{0:T(1024)}, u32[]{:S(2)}) copy-start(f32[768]{0:T(1024)} %get-tuple-element.100) | copy-start | bytes 9220
  155.4 33.8 %copy-start.17 = (bf16[512,3072]{1,0:T(8,128)(2,1)}, bf16[512,3072]{1,0:T(8,128)(2,1)S(1)}, u32[]{:S(2)}) copy-start(bf16[512,3072]{1,0:T(8,128)(2,1)S(1)} %get-tuple-element.126.refs_6_) | copy-start | bytes 9437188
  155.5 56.7 %collective-permute-start.28 = (bf16[768,768]{1,0:T(8,128)(2,1)}, bf16[768,768]{1,0:T(8,128)(2,1)}, u32[]{:S(2)}, u32[]{:S(2)}) collective-permute-start(bf16[768,768]{1,0:T(8,128)(2,1)} %get-tuple-element.127), channel_id=1, source_target_pairs={{0,1},{1,0},{2,3},{3,2},{4,5},{5,4},{6,7},{7,6},{8,9},{9,8},{10,11... | collective-permute-start | bytes 3538952 | tf_op jit(solution)/shard_map/ppermute | solution.py:37
  157.5 51.4 %collective-permute-start.27 = (bf16[768,768]{1,0:T(8,128)(2,1)}, bf16[768,768]{1,0:T(8,128)(2,1)}, u32[]{:S(2)}, u32[]{:S(2)}) collective-permute-start(bf16[768,768]{1,0:T(8,128)(2,1)} %collective-permute-done.26), channel_id=1, source_target_pairs={{0,1},{1,0},{2,3},{3,2},{4,5},{5,4},{6,7},{7,6},{8,9},{9,8},{10,11... | collective-permute-start | bytes 3538952 | tf_op jit(solution)/shard_map/ppermute | solution.py:37
  182.7 29.4 %collective-permute-start.30 = (bf16[768,768]{1,0:T(8,128)(2,1)}, bf16[768,768]{1,0:T(8,128)(2,1)}, u32[]{:S(2)}, u32[]{:S(2)}) collective-permute-start(bf16[768,768]{1,0:T(8,128)(2,1)} %collective-permute-done.29), channel_id=1, source_target_pairs={{0,1},{1,0},{2,3},{3,2},{4,5},{5,4},{6,7},{7,6},{8,9},{9,8},{10,11... | collective-permute-start | bytes 3538952 | tf_op jit(solution)/shard_map/ppermute | solution.py:37
  192.9 26.1 %collective-permute-start.21 = (bf16[256,768]{1,0:T(8,128)(2,1)}, bf16[256,768]{1,0:T(8,128)(2,1)}, u32[]{:S(2)}, u32[]{:S(2)}) collective-permute-start(bf16[256,768]{1,0:T(8,128)(2,1)} %slice.367), channel_id=1, source_target_pairs={{1,0},{2,1},{3,2},{4,3},{5,4},{6,5},{7,6},{8,7},{9,8},{10,9},{11,1... | collective-permute-start | bytes 1179656 | tf_op jit(solution)/shard_map/ppermute | solution.py:42
  203.5 15.5 %collective-permute-start.20 = (bf16[272,768]{1,0:T(8,128)(2,1)S(1)}, bf16[272,768]{1,0:T(8,128)(2,1)S(1)}, u32[]{:S(2)}, u32[]{:S(2)}) collective-permute-start(bf16[272,768]{1,0:T(8,128)(2,1)S(1)} %copy-done.29), channel_id=1, source_target_pairs={{0,1},{1,2},{2,3},{3,4},{4,5},{5,6},{6,7},{7,8},{8,9},{9,10},{10,1... | collective-permute-start | bytes 1253384 | tf_op jit(solution)/shard_map/ppermute | solution.py:42
  212.1 33.5 %copy-start.1 = (bf16[768,3072]{1,0:T(8,128)(2,1)}, bf16[768,3072]{1,0:T(8,128)(2,1)S(1)}, u32[]{:S(2)}) copy-start(bf16[768,3072]{1,0:T(8,128)(2,1)S(1)} %pad_maximum_fusion.3.refs_38_) | copy-start | bytes 14155780
  226.6 16.1 %copy-start.10 = (f32[512,768]{1,0:T(8,128)S(1)}, f32[512,768]{1,0:T(8,128)}, u32[]{:S(2)}) copy-start(f32[512,768]{1,0:T(8,128)} %get-tuple-element.115.refs_10_) | copy-start | bytes 4718596
  226.6 16.1 %copy-start.24 = (bf16[192,768]{1,0:T(8,128)(2,1)S(1)}, bf16[192,768]{1,0:T(8,128)(2,1)}, u32[]{:S(2)}) copy-start(bf16[192,768]{1,0:T(8,128)(2,1)} %copy-done.23) | copy-start | bytes 884740
  226.6 16.1 %copy-start.31 = (bf16[192,768]{1,0:T(8,128)(2,1)S(1)}, bf16[192,768]{1,0:T(8,128)(2,1)}, u32[]{:S(2)}) copy-start(bf16[192,768]{1,0:T(8,128)(2,1)} %copy-done.30) | copy-start | bytes 884740
  226.6 16.1 %copy-start.33 = (bf16[192,768]{1,0:T(8,128)(2,1)S(1)}, bf16[192,768]{1,0:T(8,128)(2,1)}, u32[]{:S(2)}) copy-start(bf16[192,768]{1,0:T(8,128)(2,1)} %copy-done.32) | copy-start | bytes 884740
  226.6 16.1 %copy-start.53 = (f32[768]{0:T(1024)S(1)}, f32[768]{0:T(1024)}, u32[]{:S(2)}) copy-start(f32[768]{0:T(1024)} %get-tuple-element.98) | copy-start | bytes 9220
  (39 other events, 213.3 us)

commit v4 on v3

--- a/solution.py
+++ b/solution.py
@@ -30,43 +30,6 @@
 
 def product_right_t(left, right):
     return lax.dot_general(left, right, (((1,), (1,)), ((), ())), preferred_element_type=F32)
-
-
-def swap(values, axis, bit):
-    count = lax.axis_size(axis)
-    return lax.ppermute(values, axis, [(i, i ^ bit) for i in range(count)])
-
-
-def shift(values, step):
-    count = lax.axis_size("seq") * lax.axis_size("mp")
-    return lax.ppermute(
-        values, BOTH, [(i, i + step) for i in range(count) if 0 <= i + step < count]
-    )
-
-
-def gather_parts(own):
-    across = swap(own, "mp", 2)
-    return [own, swap(own, "mp", 1), across, swap(across, "mp", 1)]
-
-
-def gather_small(own):
-    return gather_parts(own)
-
-
-def norm_forward(values, gain, offset):
-    average = jnp.mean(values, axis=-1, keepdims=True)
-    centered = values - average
-    spread = jnp.mean(centered * centered, axis=-1, keepdims=True)
-    inverse = lax.rsqrt(spread + NORM_EPSILON)
-    unit = centered * inverse
-    return unit * gain + offset, unit, inverse
-
-
-def with_halo(rows):
-    left = shift(rows[rows.shape[0] - LEFT_SENT :], 1)
-    right = shift(rows[:RIGHT], -1)
-    empty = jnp.zeros((LEFT - LEFT_SENT, rows.shape[1]), rows.dtype)
-    return jnp.concatenate([empty, left, rows, right], axis=0)
 
 
 def tap_mask(starts, finish, base_row):
@@ -135,45 +98,18 @@
     return jnp.concatenate([both[:HEAD_DIM, :TILE], both[HEAD_DIM:, TILE:]], axis=0)
 
 
-def pool_into(wide_ref, wide_f32, keep_ref, conv_ref, conv_bias_ref, which, pooled_ref):
+def pool_into(wide_ref, wide_f32, keep_ref, taps, shift_row, pooled_ref, pairs):
     count = pooled_ref.shape[0]
     begin = LEFT - 4 * POOL_REACH - 2
-    for pair in range(pooled_ref.shape[1] // PAIR):
+    for pair in pairs:
         lanes = slice(pair * PAIR, (pair + 1) * PAIR)
         wide_f32[...] = wide_ref[:, lanes].astype(F32)
-        total = jnp.broadcast_to(conv_bias_ref[which : which + 1, lanes], (count, PAIR))
+        total = jnp.broadcast_to(shift_row[:, lanes], (count, PAIR))
         for tap in range(5):
             rows = wide_f32[pl.ds(begin + tap, count, stride=4), :]
             kept = jnp.where(keep_ref[:, tap : tap + 1] > 0.0, rows, 0.0)
-            total = total + kept * conv_ref[which, tap : tap + 1, lanes]
+            total = total + kept * taps(tap)[:, lanes]
         pooled_ref[:, lanes] = total.astype(BF16)
-
-
-def attend_forward_kernel(
-    q_ref, k_ref, v_ref, first_ref, past_ref, keep_ref, conv_ref, conv_bias_ref,
-    mixed_ref, lse_ref, pooled_k_ref, pooled_v_ref, wide_f32,
-):
-    pool_into(k_ref, wide_f32, keep_ref, conv_ref, conv_bias_ref, 0, pooled_k_ref)
-    pool_into(v_ref, wide_f32, keep_ref, conv_ref, conv_bias_ref, 1, pooled_v_ref)
-    pairs = q_ref.shape[1] // PAIR
-
-    @pl.loop(0, q_ref.shape[0] // TILE)
-    def _(tile):
-        rows = pl.ds(pl.multiple_of(tile * TILE, TILE), TILE)
-        bias = tile_bias(tile, first_ref[tile], past_ref[tile])
-        bias = jnp.concatenate([bias, bias], axis=1)
-        for pair in range(pairs):
-            lanes = slice(pair * PAIR, (pair + 1) * PAIR)
-            query = stacked(q_ref[rows, lanes] * BF16(HEAD_DIM**-0.5))
-            key = keys_of(k_ref, pooled_k_ref, tile, lanes)
-            value = keys_of(v_ref, pooled_v_ref, tile, lanes)
-            scores = product_right_t(key, query) + bias
-            most = jnp.max(scores, axis=0, keepdims=True)
-            weight = jnp.exp(scores - most)
-            total = jnp.sum(weight, axis=0, keepdims=True)
-            both = product_left_t(value, weight.astype(BF16)) * (1.0 / total)
-            mixed_ref[rows, lanes] = unstack(both).T.astype(BF16)
-            lse_ref[tile, pair : pair + 1, :] = most + jnp.log(total)
 
 
 def attend_backward_body(
@@ -242,33 +178,6 @@
             result[:, lanes] = wide[pair].astype(BF16)
 
 
-def in_vmem(count):
-    return [pl.BlockSpec(memory_space=pltpu.VMEM)] * count
-
-
-VMEM_LIMIT = 56 * 1024 * 1024
-
-
-def attend_forward(queries, keys, values, first, past, keep, conv, conv_bias):
-    total, width = queries.shape
-    count = total // 4 + 2 * POOL_REACH
-    shape = jax.ShapeDtypeStruct
-    return pl.pallas_call(
-        attend_forward_kernel,
-        out_shape=(
-            shape((total, width), BF16),
-            shape((total // TILE, width // PAIR, 2 * TILE), F32),
-            shape((count, width), BF16),
-            shape((count, width), BF16),
-        ),
-        in_specs=in_vmem(8),
-        out_specs=tuple(in_vmem(4)),
-        scratch_shapes=[pltpu.VMEM((keys.shape[0], PAIR), F32)],
-        compiler_params=pltpu.CompilerParams(vmem_limit_bytes=VMEM_LIMIT),
-        name="attend_forward",
-    )(queries, keys, values, first, past, keep, conv, conv_bias)
-
-
 def gelu_parts(pre):
     size = jnp.abs(pre) * (0.5**0.5)
     t = 1.0 / (1.0 + 0.5 * size)
@@ -280,35 +189,6 @@
     cdf = jnp.where(pre < 0.0, tail, 1.0 - tail)
     density = jnp.exp(-0.5 * pre * pre) * (0.5 / jnp.pi) ** 0.5
     return pre * cdf, cdf + pre * density
-
-
-def layer_forward(hidden, masks, weights):
-    first, past, keep = masks
-    qkv, qv, conv, conv_bias, out, up, up_bias, down, gains, biases = weights
-    total = hidden.shape[0]
-    entry_wide = with_halo(hidden.astype(BF16))
-    entry = entry_wide[LEFT : LEFT + total]
-    queries = (product(entry, qkv[0]) + qv[0]).astype(BF16)
-    keys = product(entry_wide, qkv[1]).astype(BF16)
-    values = (product(entry_wide, qkv[2]) + qv[1]).astype(BF16)
-
-    mixed, lse, pooled_k, pooled_v = attend_forward(
-        queries, keys, values, first, past, keep, conv, conv_bias
-    )
-    resid = hidden + (product(mixed, out) + biases[0])
-    normed, unit_one, inverse_one = norm_forward(resid, gains[0], biases[1])
-    normed_low = normed.astype(BF16)
-    pre = product(normed_low, up) + up_bias
-    act, slope = gelu_parts(pre)
-    act, slope = act.astype(BF16), slope.astype(BF16)
-    middle = normed + (product(act, down) + biases[2])
-    result, unit_two, inverse_two = norm_forward(middle, gains[1], biases[3])
-    saved = dict(
-        act=act, slope=slope, normed=normed_low, unit_one=unit_one, unit_two=unit_two, mixed=mixed,
-        q=queries, k=keys, v=values, pooled_k=pooled_k, pooled_v=pooled_v, entry=entry_wide,
-        down=down, up=up, out=out, qkv=qkv, inverse_one=inverse_one, inverse_two=inverse_two, lse=lse,
-    )
-    return result, saved
 
 
 CHUNK = 256
@@ -400,7 +280,12 @@
 
     def target(self, c):
         lanes = pl.ds(pl.multiple_of(self.low * self.half, 128), self.half)
-        return self.out.at[self.chunk_rows(c), lanes]
+        layer_chunks = LAYER_ROWS // CHUNK
+        turned = (c + (LAYERS - 1) * layer_chunks) % (LAYERS * layer_chunks)
+        at = turned if isinstance(c, int) else jnp.where(c < LAYERS * layer_chunks, turned, c)
+        if isinstance(c, int) and c >= LAYERS * layer_chunks:
+            at = c
+        return self.out.at[self.chunk_rows(at), lanes]
 
     def f_copy(self, c):
         return self.remote(
@@ -550,7 +435,7 @@
                 whole_ref[layer, at : at + 1, :] += jnp.sum(value, axis=0, keepdims=True)
 
     def feed_scope(layer, base, ticks, down, up, act, slope, normed, unit_one, unit_two, out, mixed,
-                   gm_low, gn_ref, stage, wide_out):
+                   gm_low, gn_ref, stage_down, stage_up, wide_out, normed_t):
         ref = layers[layer]
         pairs = ((ref["unit_two"], unit_two), (ref["down"], down), (ref["slope"], slope),
                  (ref["act"], act), (ref["normed"], normed), (ref["up"], up),
@@ -562,6 +447,7 @@
         gn_ref[...] = gm_ref[...]
         for copy in copies[1:6]:
             copy.wait()
+        normed_t[...] = normed[...].T
         ticks()
         stores = []
         for j in range(3):
@@ -579,16 +465,16 @@
                     gp, axis=0, keepdims=True
                 )
                 gp_low = gp.astype(BF16)
-                stage[0, pos] = product_left_t(act[:, cols], gm_low[...]).astype(BF16)
-                stage[1, pos] = product_left_t(gp_low, normed[...]).astype(BF16)
+                stage_down[pos] = product_left_t(act[:, cols], gm_low[...]).astype(BF16)
+                stage_up[pos] = product(normed_t[...], gp_low).astype(BF16)
                 gn_ref[...] += product_right_t(gp_low, up[:, cols])
 
             stores = []
-            for kind in range(2):
-                at = base + kind * width + j * CHUNK
-                copy = pltpu.make_async_copy(
-                    stage.at[kind], parts_ref.at[:, pl.ds(at, CHUNK)], store_s.at[kind]
-                )
+            for kind, (source, target) in enumerate((
+                (stage_down, parts_ref.at[:, pl.ds(base + j * CHUNK, CHUNK)]),
+                (stage_up, parts_ref.at[:, pl.ds(base + width, width), pl.ds(j * CHUNK, CHUNK)]),
+            )):
+                copy = pltpu.make_async_copy(source, target, store_s.at[kind])
                 copy.start()
                 stores.append(copy)
             ticks()
@@ -638,8 +524,8 @@
         copies = [load(ref["qkv"], qkv, 0), load(ref["entry"], entry, 1)]
         for copy in copies:
             copy.wait()
-        wide[...] = product_right_t(grad_k[...], qkv[1])
-        wide[...] += product_right_t(grad_v[...], qkv[2])
+        wide[...] = product(grad_k[...], qkv[1])
+        wide[...] += product(grad_v[...], qkv[2])
         send_left[...] = wide[LEFT - LEFT_SENT : LEFT, :].astype(BF16)
         send_right[...] = wide[LEFT + total :, :].astype(BF16)
         halo = [
@@ -650,7 +536,7 @@
             copy.start()
         own = slice(LEFT, LEFT + total)
         gm_ref[...] += wide[own, :]
-        gm_ref[...] += product_right_t(grad_q[...], qkv[0])
+        gm_ref[...] += product(grad_q[...], qkv[0])
         banks = []
         for which, (grad, rows) in enumerate(((grad_q, own), (grad_k, slice(None)), (grad_v, slice(None)))):
             bank = which % 2
@@ -710,7 +596,8 @@
             vmem((feed, width), BF16), vmem((width, feed), BF16), vmem((total, feed), BF16),
             vmem((total, feed), BF16), vmem(block, BF16), vmem(block, F32), vmem(block, F32),
             vmem((width, width), BF16), vmem(block, BF16), vmem(block, BF16), vmem(block, F32),
-            vmem((2, 4, CHUNK, width), BF16), vmem((width, width), BF16),
+            vmem((4, CHUNK, width), BF16), vmem((4, width, CHUNK), BF16), vmem((width, width), BF16),
+            vmem((width, total), BF16),
         )
 
         def attention(grad_q, grad_k, grad_v):
@@ -811,6 +698,394 @@
     )(*args)
 
 
+def row_blocks(total, size, body):
+    @pl.loop(0, total // size)
+    def _(block):
+        body(pl.ds(pl.multiple_of(block * size, size), size))
+
+
+def attend_forward_body(
+    q_ref, k_ref, v_ref, first_ref, past_ref, keep_ref, taps, shifts,
+    mixed_ref, lse_ref, pooled_k_ref, pooled_v_ref, wide_f32, pairs,
+):
+    for which, (source, pooled) in enumerate(((k_ref, pooled_k_ref), (v_ref, pooled_v_ref))):
+        pool_into(source, wide_f32, keep_ref, taps[which], shifts[which], pooled, pairs)
+
+    @pl.loop(0, q_ref.shape[0] // TILE)
+    def _(tile):
+        rows = pl.ds(pl.multiple_of(tile * TILE, TILE), TILE)
+        bias = tile_bias(tile, first_ref[tile], past_ref[tile])
+        bias = jnp.concatenate([bias, bias], axis=1)
+        for pair in pairs:
+            lanes = slice(pair * PAIR, (pair + 1) * PAIR)
+            query = stacked(q_ref[rows, lanes] * BF16(HEAD_DIM**-0.5))
+            key = keys_of(k_ref, pooled_k_ref, tile, lanes)
+            value = keys_of(v_ref, pooled_v_ref, tile, lanes)
+            scores = product_right_t(key, query) + bias
+            most = jnp.max(scores, axis=0, keepdims=True)
+            weight = jnp.exp(scores - most)
+            total = jnp.sum(weight, axis=0, keepdims=True)
+            both = product_left_t(value, weight.astype(BF16)) * (1.0 / total)
+            mixed_ref[rows, lanes] = unstack(both).T.astype(BF16)
+            lse_ref[tile, pair : pair + 1, :] = most + jnp.log(total)
+
+
+SAVED_NAMES = LAYER_NAMES
+TENSORS = 4 * LAYERS
+
+
+def forward_kernel(*refs):
+    refs = list(refs)
+    take = lambda n: [refs.pop(0) for _ in range(n)]
+    (x_ref, qkv_ref, out_ref, up_ref, down_ref, small_ref, gains_ref, biases_ref, first_ref, past_ref,
+     keep_ref) = take(11)
+    hidden_ref, conv_ref = take(2)
+    results = [dict(zip(SAVED_NAMES + LOCAL_NAMES, take(len(SAVED_NAMES + LOCAL_NAMES)))) for _ in range(LAYERS)]
+    (qkv_v, out_v, up_v, down_v, entry_v, q_v, k_v, v_v, far_k, far_v, mixed_v, hidden_v, acc_v,
+     unit_one, unit_two, low_v, act_v, slope_v, pre_v, wide_f32, small_v, full_v,
+     own_s, x_s, x_r, y_s, y_r, c_s, c_r, d_s, d_r, halo_s, save_s, load_s) = take(34)
+    total, width = hidden_v.shape
+    quarter, half = width // 4, width // 2
+    place, seat, seqs = lax.axis_index("seq"), lax.axis_index("mp"), lax.axis_size("seq")
+    low = place % 2
+    core = seat_of(mp=seat + 1 - 2 * (seat % 2))
+    across = seat_of(mp=(seat + 2) % 4)
+    beside = seat_of(seq=place + 1 - 2 * low)
+    ahead = seat_of(seq=(place + (seat + 1) // 4) % seqs, mp=(seat + 1) % 4)
+    behind = seat_of(seq=(place + seqs - (4 - seat) // 4) % seqs, mp=(seat + 3) % 4)
+    barrier = pltpu.get_barrier_semaphore()
+    devices = [core, across, beside, ahead, behind]
+    for device in devices:
+        pl.semaphore_signal(barrier, inc=1, device_id=device, device_id_type=MESH)
+    entry_own = pl.ds(LEFT, total)
+    first_load = pltpu.make_async_copy(x_ref, entry_v.at[0, entry_own], load_s.at[0])
+    first_load.start()
+    small_load = pltpu.make_async_copy(small_ref, small_v.at[0], load_s.at[1])
+    small_load.start()
+    for layer in range(LAYERS):
+        entry_v[layer, : LEFT - LEFT_SENT, :] = jnp.zeros((LEFT - LEFT_SENT, width), BF16)
+    pl.semaphore_wait(barrier, len(devices))
+
+    def remote(source, target, send, recv, device):
+        return pltpu.make_async_remote_copy(
+            src_ref=source, dst_ref=target, send_sem=send, recv_sem=recv,
+            device_id=device, device_id_type=MESH,
+        )
+
+    def span(size, side):
+        if side is None:
+            return 0, size
+        return pl.multiple_of(side * (size // 2), size // 2), size // 2
+
+    def shard(tensor, side=None):
+        layer, kind = tensor // 4, tensor % 4
+        if kind == 0:
+            return qkv_ref.at[layer, :, pl.ds(*span(quarter, side))]
+        if kind == 1:
+            return out_ref.at[layer, pl.ds(*span(quarter, side))]
+        return (up_ref if kind == 2 else down_ref).at[layer, pl.ds(*span(width, side))]
+
+    def landed(tensor, part, side=None):
+        layer, kind = tensor // 4, tensor % 4
+        if kind == 2:
+            return up_v.at[layer, pl.ds(*span(width, side)), pl.ds(part * width, width)]
+        size = width if kind == 3 else quarter
+        at, count = span(size, side)
+        rows = pl.ds(part * size + at, count)
+        if kind == 0:
+            return qkv_v.at[layer, :, rows]
+        return (out_v if kind == 1 else down_v).at[layer, rows]
+
+    def own_copy(t):
+        return pltpu.make_async_copy(shard(t), landed(t, 0), own_s.at[t])
+
+    def x_copy(t):
+        return remote(shard(t, low), landed(t, 2, low), x_s.at[t], x_r.at[t], across)
+
+    def y_copy(t):
+        return remote(landed(t, 2, low), landed(t, 2, low), y_s.at[t], y_r.at[t], beside)
+
+    def c_copy(t):
+        return remote(shard(t), landed(t, 1), c_s.at[t], c_r.at[t], core)
+
+    def d_copy(t):
+        return remote(landed(t, 2), landed(t, 3), d_s.at[t], d_r.at[t], core)
+
+    def gather(step):
+        if step < TENSORS:
+            own_copy(step).start()
+            c_copy(step).start()
+            x_copy(step).start()
+        if 0 <= step - 2 < TENSORS:
+            x_copy(step - 2).wait_recv()
+            y_copy(step - 2).start()
+        if 0 <= step - 4 < TENSORS:
+            y_copy(step - 4).wait_recv()
+            d_copy(step - 4).start()
+
+    small_index = TENSORS
+    small_x = remote(small_ref, small_v.at[2], x_s.at[small_index], x_r.at[small_index], across)
+    small_c = remote(small_ref, small_v.at[1], c_s.at[small_index], c_r.at[small_index], core)
+    small_d = remote(small_v.at[2], small_v.at[3], d_s.at[small_index], d_r.at[small_index], core)
+
+    def halo(layer):
+        entry = entry_v.at[layer]
+        return (
+            remote(
+                entry.at[pl.ds(LEFT + total - LEFT_SENT, LEFT_SENT)],
+                entry.at[pl.ds(LEFT - LEFT_SENT, LEFT_SENT)],
+                halo_s.at[layer, 0], halo_s.at[layer, 1], ahead,
+            ),
+            remote(
+                entry.at[pl.ds(LEFT, RIGHT)], entry.at[pl.ds(LEFT + total, RIGHT)],
+                halo_s.at[layer, 2], halo_s.at[layer, 3], behind,
+            ),
+        )
+
+    saves = {}
+
+    def save(layer, name, source):
+        index = SAVED_NAMES.index(name)
+        copy = pltpu.make_async_copy(source, results[layer][name], save_s.at[layer, index])
+        copy.start()
+        saves[layer, name] = copy
+
+    def settle(layer, *names):
+        for name in names:
+            if (layer, name) in saves:
+                saves.pop((layer, name)).wait()
+
+    def norm(layer, which, extra, result, low_ref, unit, inverse):
+        gain = gains_ref[layer, which : which + 1, :]
+        offset = biases_ref[layer, 2 * which + 1 : 2 * which + 2, :]
+        shift_row = biases_ref[layer, 2 * which : 2 * which + 1, :]
+
+        def body(rows):
+            value = hidden_v[rows, :] + (extra[rows, :] + shift_row)
+            average = jnp.sum(value, axis=1, keepdims=True) * (1.0 / width)
+            centered = value - average
+            spread = jnp.sum(centered * centered, axis=1, keepdims=True) * (1.0 / width)
+            scale = lax.rsqrt(spread + NORM_EPSILON)
+            one = centered * scale
+            out = one * gain + offset
+            unit[rows, :] = one
+            inverse[rows, :] = scale
+            result[rows, :] = out
+            if low_ref is not None:
+                low_ref[rows, :] = out.astype(BF16)
+
+        row_blocks(total, NORM_ROWS, body)
+
+    first_load.wait()
+    for copy in halo(0):
+        copy.start()
+    small_x.start()
+    small_c.start()
+    gather(0)
+    gather(1)
+    row_blocks(total, NORM_ROWS, lambda rows: hidden_v.__setitem__(
+        (rows, slice(None)), entry_v[0, pl.ds(rows.start + LEFT, NORM_ROWS), :].astype(F32)))
+
+    for layer in range(LAYERS):
+        entry = entry_v.at[layer]
+        tensor = 4 * layer
+        steps = iter(((2, 3, 4, 5, 6, 7, 8, 9), (10, 11))[layer])
+
+        def advance():
+            step = next(steps, None)
+            if step is not None:
+                gather(step)
+
+        settle(layer - 1, "q", "k", "v", "pooled_k", "pooled_v", "mixed", "normed")
+
+        def project(which, target, side, rows):
+            lanes = slice(side * half, (side + 1) * half)
+            made = product_right_t(entry[rows, :], qkv_v[layer, which, lanes, :])
+            if which != 1:
+                row = 2 * layer + which // 2
+                made = made + full_v[row : row + 1, lanes]
+            target[:, lanes] = made.astype(BF16)
+
+        own_copy(tensor).wait()
+        c_copy(tensor).wait_recv()
+        if layer == 0:
+            small_load.wait()
+            small_c.wait_recv()
+            small_x.wait_recv()
+            small_d.start()
+            small_d.wait_recv()
+            rows = [small_v[0, :32, :]] + [
+                pltpu.roll(small_v[part, :32, :], part * quarter, 1) for part in range(1, 4)
+            ]
+            full_v[...] = rows[0] + rows[1] + rows[2] + rows[3]
+            for one in range(LAYERS):
+                for which in range(2):
+                    at = 4 + 10 * one + 5 * which
+                    conv_ref[one, which] = full_v[at : at + 5, :]
+        project(0, q_v, 0, entry_own)
+        advance()
+        for copy in halo(layer):
+            copy.wait_recv()
+        everything = slice(None)
+        project(1, k_v, 0, everything)
+        project(2, v_v, 0, everything)
+        save(layer, "entry", entry)
+        taps = [
+            lambda tap, at=4 + 10 * layer + 5 * which: full_v[at + tap : at + tap + 1, :]
+            for which in range(2)
+        ]
+        shifts = [full_v[24 + 2 * layer + which : 25 + 2 * layer + which, :] for which in range(2)]
+
+        def attend(pairs):
+            attend_forward_body(
+                q_v, k_v, v_v, first_ref, past_ref, keep_ref, taps, shifts,
+                mixed_v, results[layer]["lse"], far_k, far_v, wide_f32, pairs,
+            )
+
+        pairs = width // PAIR
+        attend(range(pairs // 2))
+        advance()
+        advance()
+        d_copy(tensor).wait_recv()
+        project(0, q_v, 1, entry_own)
+        project(1, k_v, 1, everything)
+        project(2, v_v, 1, everything)
+        for name, source in (("q", q_v), ("k", k_v), ("v", v_v)):
+            save(layer, name, source)
+        advance()
+        attend(range(pairs // 2, pairs))
+        save(layer, "pooled_k", far_k)
+        save(layer, "pooled_v", far_v)
+        save(layer, "mixed", mixed_v)
+        advance()
+        tensor += 1
+        own_copy(tensor).wait()
+        c_copy(tensor).wait_recv()
+        d_copy(tensor).wait_recv()
+        acc_v[...] = product(mixed_v[...], out_v[layer])
+        settle(layer - 1, "unit_one", "unit_two", "act", "slope")
+        norm(layer, 0, acc_v, hidden_v, low_v, unit_one, results[layer]["inverse_one"])
+        save(layer, "unit_one", unit_one)
+        save(layer, "normed", low_v)
+        advance()
+        for part in range(4):
+            if part == 0:
+                own_copy(tensor + 1).wait()
+                own_copy(tensor + 2).wait()
+            elif part == 1:
+                c_copy(tensor + 1).wait_recv()
+                c_copy(tensor + 2).wait_recv()
+            elif part == 3:
+                d_copy(tensor + 1).wait_recv()
+                d_copy(tensor + 2).wait_recv()
+
+            @pl.loop(0, 3)
+            def _(j):
+                at = pl.multiple_of(part * width + j * CHUNK, CHUNK)
+                cols = pl.ds(at, CHUNK)
+                lanes = pl.ds(pl.multiple_of(j * CHUNK, CHUNK), CHUNK)
+                pre_v[...] = product(low_v[...], up_v[layer, :, cols])
+                up_row = small_v[part, 32 + layer : 33 + layer, lanes]
+
+                def body(rows):
+                    act, slope = gelu_parts(pre_v[rows, :] + up_row)
+                    act_v[rows, cols] = act.astype(BF16)
+                    slope_v[rows, cols] = slope.astype(BF16)
+
+                row_blocks(total, NORM_ROWS, body)
+                made = product(act_v[:, cols], down_v[layer, cols, :])
+                if part == 0:
+                    @pl.when(j == 0)
+                    def _():
+                        acc_v[...] = made
+
+                    @pl.when(j > 0)
+                    def _():
+                        acc_v[...] += made
+                else:
+                    acc_v[...] += made
+
+            if part in (0, 2):
+                advance()
+        save(layer, "act", act_v)
+        save(layer, "slope", slope_v)
+        save(layer, "qkv", qkv_v.at[layer])
+        save(layer, "out", out_v.at[layer])
+        save(layer, "up", up_v.at[layer])
+        save(layer, "down", down_v.at[layer])
+        norm(layer, 1, acc_v, hidden_v, low_v if False else None, unit_two, results[layer]["inverse_two"])
+        save(layer, "unit_two", unit_two)
+        if layer + 1 < LAYERS:
+            later = entry_v.at[layer + 1]
+            row_blocks(total, NORM_ROWS, lambda rows: later.__setitem__(
+                (pl.ds(rows.start + LEFT, NORM_ROWS), slice(None)), hidden_v[rows, :].astype(BF16)))
+            for copy in halo(layer + 1):
+                copy.start()
+    last = pltpu.make_async_copy(hidden_v, hidden_ref, load_s.at[0])
+    last.start()
+    for key in list(saves):
+        settle(*key)
+    small_x.wait_send()
+    small_c.wait_send()
+    small_d.wait_send()
+    for t in range(TENSORS):
+        for copy in (x_copy(t), y_copy(t), c_copy(t), d_copy(t)):
+            copy.wait_send()
+    for layer in range(LAYERS):
+        for copy in halo(layer):
+            copy.wait_send()
+    last.wait()
+
+
+def forward(x, qkv_t, out, up, down, small, gains, biases, first, past, keep):
+    total, width = x.shape
+    vmem, dma, shape = pltpu.VMEM, pltpu.SemaphoreType.DMA, jax.ShapeDtypeStruct
+    anywhere = pl.BlockSpec(memory_space=pl.ANY)
+    local = pl.BlockSpec(memory_space=pltpu.VMEM)
+    feed, wide_rows, far_rows = 4 * width, total + LEFT + RIGHT, total // 4 + 2 * POOL_REACH
+    block, wide, far, square = (total, width), (wide_rows, width), (far_rows, width), (width, width)
+    saved = dict(
+        act=((total, feed), BF16), slope=((total, feed), BF16), normed=(block, BF16),
+        unit_one=(block, F32), unit_two=(block, F32), mixed=(block, BF16), q=(block, BF16),
+        k=(wide, BF16), v=(wide, BF16), pooled_k=(far, BF16), pooled_v=(far, BF16), entry=(wide, BF16),
+        down=((feed, width), BF16), up=((width, feed), BF16), out=(square, BF16),
+        qkv=((3, width, width), BF16), inverse_one=((total, 1), F32), inverse_two=((total, 1), F32),
+        lse=((total // TILE, width // PAIR, 2 * TILE), F32),
+    )
+    names = SAVED_NAMES + LOCAL_NAMES
+    shapes = [shape(block, F32), shape((LAYERS, 2, 5, width), F32)]
+    specs = [anywhere, local]
+    for _ in range(LAYERS):
+        shapes += [shape(*saved[name]) for name in names]
+        specs += [anywhere] * len(SAVED_NAMES) + [local] * len(LOCAL_NAMES)
+    tensors = dma((TENSORS + 1,))
+    outs = pl.pallas_call(
+        forward_kernel,
+        out_shape=tuple(shapes),
+        in_specs=[anywhere] * 6 + [local] * 5,
+        out_specs=tuple(specs),
+        scratch_shapes=[
+            vmem((LAYERS, 3, width, width), BF16), vmem((LAYERS, width, width), BF16),
+            vmem((LAYERS, width, feed), BF16), vmem((LAYERS, feed, width), BF16),
+            vmem((LAYERS, wide_rows, width), BF16),
+            vmem(block, BF16), vmem(wide, BF16), vmem(wide, BF16), vmem(far, BF16), vmem(far, BF16),
+            vmem(block, BF16), vmem(block, F32), vmem(block, F32), vmem(block, F32), vmem(block, F32),
+            vmem(block, BF16), vmem((total, feed), BF16), vmem((total, feed), BF16),
+            vmem((total, CHUNK), F32), vmem((wide_rows, PAIR), F32), vmem((4, 40, width), F32),
+            vmem((32, width), F32),
+            tensors, tensors, tensors, tensors, tensors, tensors, tensors, tensors, tensors,
+            dma((LAYERS, 4)), dma((LAYERS, len(SAVED_NAMES))), dma((2,)),
+        ],
+        compiler_params=pltpu.CompilerParams(
+            collective_id=1, has_side_effects=True, vmem_limit_bytes=60 * 1024 * 1024
+        ),
+        name="forward",
+    )(x, qkv_t, out, up, down, small, gains, biases, first, past, keep)
+    size = len(names)
+    stack = [dict(zip(names, outs[2 + size * one : 2 + size * (one + 1)])) for one in range(LAYERS)]
+    return outs[0], outs[1], stack
+
+
 def shards(
     inputs,
     doc_bounds,
@@ -832,68 +1107,41 @@
     bounds = lax.dynamic_slice_in_dim(doc_bounds, place * total, total, 1)
     keep = jnp.pad(tap_mask(bounds[0], bounds[1], base_row).astype(F32), ((0, 0), (0, 3)))
     near_bounds = (bounds - base_row).reshape(2, total // TILE, 1, TILE)
-    masks = (near_bounds[0], near_bounds[1], keep)
     quarter = width // 4
     small = jnp.concatenate(
         [
             qv_bias.reshape(-1, quarter),
             conv_weight.reshape(-1, quarter),
             conv_bias.reshape(-1, quarter),
-            up_bias.reshape(-1, quarter),
         ],
         axis=0,
     )
-    small = gather_small(small)
-    layers = []
-    for index in range(LAYERS):
-        qkv = jnp.concatenate(gather_parts(qkv_weight[index]), axis=2)
-        out = jnp.concatenate(gather_parts(out_weight[index]), axis=0)
-        up = jnp.concatenate(gather_parts(up_weight[index]), axis=1)
-        down = jnp.concatenate(gather_parts(down_weight[index]), axis=0)
-        layers.append((qkv, out, up, down))
-    wide_small = jnp.concatenate(small, axis=1)
-    qv_all = wide_small[:4].reshape(2, 2, width)
-    conv_all = wide_small[4:24].reshape(2, 2, 5, width)
-    conv_bias_all = wide_small[24:28].reshape(2, 2, width)
-    up_bias_all = jnp.stack([part[28:].reshape(2, -1) for part in small], axis=1).reshape(2, -1)
-    hidden = inputs.astype(F32)
-    stack = []
-    for index in range(LAYERS):
-        qkv, out, up, down = layers[index]
-        weights = (
-            qkv,
-            qv_all[index],
-            conv_all[index],
-            conv_bias_all[index],
-            out,
-            up,
-            up_bias_all[index],
-            down,
-            norm_gains[index],
-            shared_biases[index],
-        )
-        hidden, saved = layer_forward(hidden, masks, weights)
-        stack.append(saved)
+    small = jnp.concatenate(
+        [jnp.pad(small, ((0, 32 - small.shape[0]), (0, width - quarter))), jnp.pad(up_bias, ((0, 6), (0, 0)))],
+        axis=0,
+    )
+    hidden, conv_all, stack = forward(
+        inputs, qkv_weight.transpose(0, 1, 3, 2), out_weight, up_weight, down_weight, small, norm_gains,
+        shared_biases, near_bounds[0], near_bounds[1], keep,
+    )
     sums, gradient, _ = backward(
         cotangent, norm_gains, conv_all, near_bounds[0], near_bounds[1], keep, stack
     )
-    sums = sums.astype(F32)
     per_layer = sums[: LAYERS * LAYER_ROWS].reshape(LAYERS, LAYER_ROWS, width)
-    per_layer = jnp.stack([per_layer[1], per_layer[0]])
-    small = sums[LAYERS * LAYER_ROWS :][: 32 * LAYERS].reshape(LAYERS, 32, width)
+    small = sums[LAYERS * LAYER_ROWS :][: 32 * LAYERS].reshape(LAYERS, 32, width).astype(F32)
     units = down_weight.shape[1]
-    grad_down = per_layer[:, :units]
-    grad_up = per_layer[:, units : 2 * units].transpose(0, 2, 1)
+    grad_down = per_layer[:, :units].astype(F32)
+    grad_up = per_layer[:, units : 2 * units].astype(F32)
     rest = per_layer[:, 2 * units :].reshape(LAYERS, 4, quarter, width)
     split = small[:, :14, :quarter]
     return (
         hidden,
         gradient,
-        rest[:, 1:].transpose(0, 1, 3, 2),
+        rest[:, 1:].transpose(0, 1, 3, 2).astype(F32),
         split[:, :2],
         split[:, 2:12].reshape(LAYERS, 2, 5, quarter),
         split[:, 12:14],
-        rest[:, 0],
+        rest[:, 0].astype(F32),
         grad_up,
         small[:, 24],
         grad_down,

time: 602 us -> 479 us (0.80)
  Pallas kernels: 309 us -> 439 us
  matrix products: 61.3 us -> 0 us
  other arithmetic: 64.6 us -> 10.9 us
  starting transfers between devices: 51.3 us -> 0 us
  local copies, waits for them, and re-layouts: 69.2 us -> 18.5 us
  waiting for transfers between devices: 38.7 us -> 0 us
    pallas_call x2 -> x1, Pallas kernels: 32 us -> 158 us  [forward(): pl.pallas_call(forward_kernel, out_shape=tuple(shapes), in_specs=[anywher...]
    dot_general x12 -> x0, matrix products: 61.3 us -> none  [product(): return jnp.dot(left, right, preferred_element_type=F32)]
    ppermute x31 -> x0, starting transfers between devices: 51.3 us -> none  [the longest x27 34.9 us: swap(): return lax.ppermute(values, axis, [(i, i ^ bit) for i in range(count)])]
    ppermute x31 -> x0, waiting for transfers between devices: 38.7 us -> none  [the longest x27 38.6 us: swap(): return lax.ppermute(values, axis, [(i, i ^ bit) for i in range(count)])]
    concatenate x10 -> x1, other arithmetic: 37.6 us -> 1.35 us  [shards(): jnp.concatenate([jnp.pad(small, ((0, 32 - small.shape[0]), (0, width - qu...]
    slice x14 -> x2, local copies, waits for them, and re-layouts: 19.9 us -> 4.36 us  [the longest x1 3.46 us: shards(): per_layer = sums[:LAYERS * LAYER_ROWS].reshape(LAYERS, LAYER_ROWS, width)]
    ppermute x6 -> x0, local copies, waits for them, and re-layouts: 11.2 us -> none  [swap(): return lax.ppermute(values, axis, [(i, i ^ bit) for i in range(count)])]
    squeeze x7 -> x1, local copies, waits for them, and re-layouts: 9.72 us -> 0.59 us  [shards(): near_bounds[1]]
  transfers between devices with their start and end apart: 31 -> 0, of which waited for: 5 -> 0; matrix products, arithmetic and copies ran while one was open for 18% -> 0% of each run, Pallas kernels for 3% -> 0%
where the time goes in v4:
time: 479 us; the launch traced here: 470 us
  Pallas kernels  439 us (92%)
  local copies, waits for them, and re-layouts  18.5 us (4%)
  other arithmetic  10.9 us (2%)
    pallas_call x1, Pallas kernels, backward(): pl.pallas_call(functools.partial(backward_kernel, group, count), out_shap...  281 us
    pallas_call x1, Pallas kernels, forward(): pl.pallas_call(forward_kernel, out_shape=tuple(shapes), in_specs=[anywher...  158 us

profile of v4, /device:TPU:15, one launch (start us, length us, event | category | flops | bytes accessed | tf_op | source)
XLA Modules:
  0.0 469.7 jit_solution(7576653169584966302)
XLA Ops:
  0.7 1.4 constant_dynamic-slice_fusion
  2.0 0.6 broadcast_in_dim.33
  2.7 0.6 broadcast_in_dim.39
  3.3 0.6 broadcast_in_dim.37
  4.0 0.6 broadcast_in_dim.35
  4.7 0.7 dynamic-slice_subtract_fusion
  5.3 0.6 slice_bitcast_fusion.1
  5.9 0.9 dynamic-slice_reduce_fusion.1
  6.8 0.7 reshape.71
  7.5 0.7 reshape.73
  8.2 0.7 copy.37
  8.9 0.1 reshape_squeeze.6
  9.0 0.1 slice_reduce_fusion.1
  9.2 1.4 select_maximum_fusion.refs_5_
  10.5 0.1 reshape_squeeze.7
  10.6 0.1 slice_reduce_fusion
  10.7 0.1 pad_add_fusion
  10.8 0.2 fusion.3
  11.0 0.7 pad_convert_fusion.refs_10_.refs_5_
  11.7 158.1 %forward.1 = (f32[512,768]{1,0:T(8,128)}, f32[2,2,5,768]{3,2,1,0:T(8,128)}, bf16[512,3072]{1,0:T(8,128)(2,1)}, bf16[512,3072]{1,0:T(8,128)(2,1)}, bf16[512,768]{...) custom-call(bf16[512,768]{1,0:T(8,128)(2,1)} %refs_0_.2, ...), custom_call_target="tpu_custom_call" | custom-call | tf_op jit(solution)/shard_map/forward/pallas_call | solution.py:1062
  169.8 280.9 %backward.1 = (bf16[4864,768]{1,0:T(8,128)(2,1)}, f32[512,768]{1,0:T(8,128)}, bf16[4,4864,768]{2,1,0:T(8,128)(2,1)}) custom-call(bf16[512,768]{1,0:T(8,128)(2,1)} %refs_0_.3, f32[2,2,768]{2,1,0:T(2,128)} %refs_1_.1, f32[2,2,5,768]{3,2,1,0:T(8,128)} %get-tuple-element.55.refs_2_, s32[4,1,128]{2,1,0:T(1,128)} %get-tuple-element.144.refs_8_.refs_3_, ...), custom_call_target="tpu_custom_call" | custom-call | tf_op jit(solution)/shard_map/backward/pallas_call | solution.py:668
  450.8 0.9 slice.100
  451.7 3.5 slice.97
  455.1 0.6 copy.45
  455.7 0.6 fusion.4
  456.3 0.6 slice.123
  457.0 0.6 slice.124
  457.6 0.6 copy.41
  458.2 4.7 slice_convert_fusion
  462.9 1.1 fusion
  464.0 0.0 copy-start
  464.0 2.1 convert_bitcast_fusion
  466.1 0.0 copy-done
  466.1 0.0 copy-start.1
  466.1 1.1 copy.48
  467.3 0.8 copy-done.1
  468.1 1.1 copy.49
  (6 shorter events, 0.1 us)
Async XLA Ops:
  464.0 2.1 copy-start
  466.1 2.0 copy-start.1
